TPU v7x, 128 devices: a whole 4x4x4 slice. The times are simulated.
128 devices in a mesh: row: 8 (over x_hi, y), col: 16 (over z, x_lo, core).
Axes of the slice: x: 4 (x_hi: 2, x_lo: 2; x = x_hi * 2 + x_lo), y: 4, z: 4, core: 2. Of those that a mesh axis runs over, the one named last changes fastest.
Arguments:
- scalar: bfloat16 [512, 512, 512], P('row', 'col'), may hold values from -6 to 6
- register_in: float32 [512, 512, 512], P('row', 'col'), may hold values from -6 to 6
- drift_x: bfloat16 [512, 512, 512], P('row', 'col'), may hold values from -6 to 6
- drift_y: bfloat16 [512, 512, 512], P(None, 'col', 'row'), may hold values from -6 to 6
- drift_z: bfloat16 [512, 512, 512], P('row', 'col'), may hold values from -6 to 6
- diffusivity: bfloat16 [512, 512, 512], P('row', 'col'), may hold values from 0.099609375 to 1
- metric_x: float32 [512], replicated, may hold values from 0.5 to 2
- metric_y: float32 [512], replicated, may hold values from 0.5 to 2
- metric_z: float32 [512], replicated, may hold values from 0.5 to 2
- first_x: bfloat16 [512, 512], replicated, may hold values from -0.25 to 0.25
- second_x: bfloat16 [512, 512], replicated, may hold values from -0.25 to 0.25
- first_y: bfloat16 [512, 512], replicated, may hold values from -0.25 to 0.25
- second_y: bfloat16 [512, 512], replicated, may hold values from -0.25 to 0.25
- first_z: bfloat16 [512, 512], replicated, may hold values from -0.25 to 0.25
- second_z: bfloat16 [512, 512], replicated, may hold values from -0.25 to 0.25
Outputs:
- register_out: float32 [512, 512, 512], P('row', 'col')
- scalar_out: bfloat16 [512, 512, 512], P('row', 'col')
All inputs are finite; a program needn't handle non-finite values.
Results may differ from a plain program's by a relative error of at most 0.001.
Values may be sent and summed in bfloat16 or wider, within the bound.
No kernel may reach another device: no remote copies, remote signals or barrier semaphores. Data moves between devices by JAX's collectives and lax.ppermute only.
A program may use at most 128 MiB of HBM per device.

v0:
```python
import jax
import jax.numpy as jnp
from jax import lax
from jax.sharding import PartitionSpec as P


def along_lead(pencil, grad_op, curv_op):
    length = pencil.shape[0]
    flat = pencil.reshape(length, -1)
    grad = jnp.dot(grad_op, flat, preferred_element_type=jnp.float32)
    curv = jnp.dot(curv_op, flat, preferred_element_type=jnp.float32)
    return (grad.reshape(pencil.shape), curv.reshape(pencil.shape))


def along_middle(pencil, grad_op, curv_op):
    grad = jnp.einsum("xyz,ky->xkz", pencil, grad_op, preferred_element_type=jnp.float32)
    curv = jnp.einsum("xyz,ky->xkz", pencil, curv_op, preferred_element_type=jnp.float32)
    return (grad, curv)


def along_last(pencil, grad_op, curv_op):
    grad = jnp.einsum("abz,kz->abk", pencil, grad_op, preferred_element_type=jnp.float32)
    curv = jnp.einsum("abz,kz->abk", pencil, curv_op, preferred_element_type=jnp.float32)
    return (grad, curv)


def combine_terms(drift, coeff, scale, grad, curv):
    return (
        drift.astype(jnp.float32) * scale * grad
        + coeff.astype(jnp.float32) * (scale * scale) * curv
    )


def on_device(
    scalar,
    register_in,
    drift_x,
    drift_y,
    drift_z,
    diffusivity,
    metric_x,
    metric_y,
    metric_z,
    first_x,
    second_x,
    first_y,
    second_y,
    first_z,
    second_z,
):
    scalar_y, coeff_y, wind_z = (
        lax.all_to_all(scalar, "row", split_axis=2, concat_axis=0, tiled=True),
        lax.all_to_all(diffusivity, "row", split_axis=2, concat_axis=0, tiled=True),
        lax.all_to_all(drift_z, "row", split_axis=2, concat_axis=0, tiled=True),
    )
    grad, curv = along_lead(scalar_y, first_y, second_y)
    term_y = combine_terms(drift_y, coeff_y, metric_y[:, None, None], grad, curv)
    grad, curv = along_middle(
        lax.all_to_all(scalar_y, "col", split_axis=0, concat_axis=1, tiled=True), first_z, second_z
    )
    term_z = combine_terms(
        lax.all_to_all(wind_z, "col", split_axis=0, concat_axis=1, tiled=True),
        lax.all_to_all(coeff_y, "col", split_axis=0, concat_axis=1, tiled=True),
        metric_z[None, :, None],
        grad,
        curv,
    )
    back_z = lax.all_to_all(term_z, "col", split_axis=1, concat_axis=0, tiled=True)
    tend_yz = lax.all_to_all(term_y + back_z, "row", split_axis=0, concat_axis=2, tiled=True)
    grad, curv = along_last(scalar, first_x, second_x)
    term_x = combine_terms(drift_x, diffusivity, metric_x[None, None, :], grad, curv)
    tendency = term_x + tend_yz
    register_out = -5.0 / 9.0 * register_in + 0.5 * tendency
    scalar_out = (scalar.astype(jnp.float32) + 15.0 / 16.0 * register_out).astype(jnp.bfloat16)
    return (register_out, scalar_out)


def solution(mesh):
    in_specs = (
        P("row", "col", None),
        P("row", "col", None),
        P("row", "col", None),
        P(None, "col", "row"),
        P("row", "col", None),
        P("row", "col", None),
        P(),
        P(),
        P(),
        P(),
        P(),
        P(),
        P(),
        P(),
        P(),
    )
    out_specs = (P("row", "col", None), P("row", "col", None))
    return jax.shard_map(
        on_device, mesh=mesh, in_specs=in_specs, out_specs=out_specs, check_vma=False
    )
```

profile of v0, /device:TPU:1, one launch (start us, length us, event | category | flops | bytes accessed | tf_op | source)
XLA Modules:
  0.0 520.2 jit_solution(18285560221571784739)
XLA Ops:
  0.6 8.8 %copy.65 = bf16[64,32,512]{0,1,2:T(8,128)(2,1)} copy(bf16[64,32,512]{2,1,0:T(8,128)(2,1)} %param.19) | data formatting | bytes 4194304 | tf_op args[4]
  9.5 7.7 %reshape.50 = bf16[8,2,65536]{2,1,0:T(2,128)(2,1)} reshape(bf16[512,32,64]{2,1,0:T(8,128)(2,1)} %bitcast.107) | data formatting | bytes 4194304
  17.2 7.5 %all-to-all-start.2 = ((bf16[8,2,65536]{2,1,0:T(2,128)(2,1)}), bf16[8,2,65536]{2,1,0:T(2,128)(2,1)}, u32[]{:S(2)}, u32[]{:S(2)}) async-start(bf16[8,2,65536]{2,1,0:T(2,128)(2,1)} %reshape.50), calls=%async_computation.2 | async-start | bytes 4194304 | tf_op jit(solution)/shard_map/all_to_all | solution.py:54
  24.7 7.8 %copy.63 = bf16[64,32,512]{0,1,2:T(8,128)(2,1)} copy(bf16[64,32,512]{2,1,0:T(8,128)(2,1)S(1)} %copy-done.8) | data formatting | bytes 4194304 | tf_op args[5]
  32.5 7.7 %reshape.46 = bf16[8,2,65536]{2,1,0:T(2,128)(2,1)} reshape(bf16[512,32,64]{2,1,0:T(8,128)(2,1)} %bitcast.108) | data formatting | bytes 4194304
  40.2 10.7 %all-to-all-done.2 = bf16[8,2,65536]{2,1,0:T(2,128)(2,1)} async-done(((bf16[8,2,65536]{2,1,0:T(2,128)(2,1)}), bf16[8,2,65536]{2,1,0:T(2,128)(2,1)}, u32[]{:S(2)}, u32[]{:S(2)}) %all-to-all-start.2) | async-done | bytes 2097184 | tf_op jit(solution)/shard_map/all_to_all | solution.py:54
  56.1 7.8 %copy.61 = bf16[64,32,512]{0,1,2:T(8,128)(2,1)} copy(bf16[64,32,512]{2,1,0:T(8,128)(2,1)S(1)} %copy-done.2) | data formatting | bytes 4194304 | tf_op args[0]
  64.0 7.6 %reshape.42 = bf16[8,2,65536]{2,1,0:T(2,128)(2,1)} reshape(bf16[512,32,64]{2,1,0:T(8,128)(2,1)} %bitcast.109) | data formatting | bytes 4194304
  71.5 10.9 %all-to-all-done.1 = bf16[8,2,65536]{2,1,0:T(2,128)(2,1)} async-done(((bf16[8,2,65536]{2,1,0:T(2,128)(2,1)}), bf16[8,2,65536]{2,1,0:T(2,128)(2,1)}, u32[]{:S(2)}, u32[]{:S(2)}) %all-to-all-start.1) | async-done | bytes 2097184 | tf_op jit(solution)/shard_map/all_to_all | solution.py:53
  87.6 7.4 %reshape.51 = bf16[512,32,64]{2,1,0:T(8,128)(2,1)} reshape(bf16[8,2,65536]{2,1,0:T(2,128)(2,1)} %all-to-all-done.2) | data formatting | bytes 4194304
  95.0 9.0 %copy.83 = bf16[8,64,32,64]{3,2,1,0:T(8,128)(2,1)} copy(bf16[8,64,32,64]{1,2,3,0:T(8,128)(2,1)} %bitcast.110) | data formatting | bytes 4194304 | tf_op jit(solution)/shard_map/all_to_all | solution.py:54
  104.0 7.5 %reshape.52 = bf16[16,2,32768]{2,1,0:T(2,128)(2,1)} reshape(bf16[512,32,64]{2,1,0:T(8,128)(2,1)} %bitcast.111) | data formatting | bytes 4194304
  113.8 7.2 %all-to-all-start.3 = ((bf16[16,2,32768]{2,1,0:T(2,128)(2,1)}), bf16[16,2,32768]{2,1,0:T(2,128)(2,1)}, u32[]{:S(2)}, u32[]{:S(2)}) async-start(bf16[16,2,32768]{2,1,0:T(2,128)(2,1)} %reshape.52), calls=%async_computation.3 | async-start | bytes 4194304 | tf_op jit(solution)/shard_map/all_to_all | solution.py:62
  120.9 7.4 %reshape.47 = bf16[512,32,64]{2,1,0:T(8,128)(2,1)} reshape(bf16[8,2,65536]{2,1,0:T(2,128)(2,1)} %all-to-all-done.1) | data formatting | bytes 4194304
  128.3 6.8 %copy.92 = bf16[64,32,8,64]{0,2,3,1:T(8,128)(2,1)} copy(bf16[64,32,8,64]{0,1,3,2:T(8,128)(2,1)} %bitcast.112) | data formatting | bytes 4194304 | tf_op jit(solution)/shard_map/all_to_all | solution.py:53
  135.2 5.4 %all_to_all.98 = bf16[512,32,64]{0,2,1:T(8,128)(2,1)S(1)} reshape(bf16[8,64,32,64]{1,0,3,2:T(8,128)(2,1)} %bitcast.113) | data formatting | bytes 4194304 | tf_op jit(solution)/shard_map/all_to_all | solution.py:53
  140.6 6.6 %copy.73 = bf16[512,32,64]{2,1,0:T(8,128)(2,1)} copy(bf16[512,32,64]{0,2,1:T(8,128)(2,1)S(1)} %all_to_all.98) | data formatting | bytes 4194304 | tf_op jit(solution)/shard_map/all_to_all | solution.py:53
  147.2 7.6 %reshape.48 = bf16[16,2,32768]{2,1,0:T(2,128)(2,1)} reshape(bf16[512,32,64]{2,1,0:T(8,128)(2,1)} %copy.73) | data formatting | bytes 4194304
  154.8 5.9 %all-to-all-start.5 = ((bf16[16,2,32768]{2,1,0:T(2,128)(2,1)}), bf16[16,2,32768]{2,1,0:T(2,128)(2,1)}, u32[]{:S(2)}, u32[]{:S(2)}) async-start(bf16[16,2,32768]{2,1,0:T(2,128)(2,1)} %reshape.48), calls=%async_computation.5 | async-start | bytes 4194304 | tf_op jit(solution)/shard_map/all_to_all | solution.py:63
  165.6 9.0 %copy.84 = bf16[8,64,32,64]{3,2,1,0:T(8,128)(2,1)} copy(bf16[8,64,32,64]{1,2,3,0:T(8,128)(2,1)} %bitcast.92) | data formatting | bytes 4194304 | tf_op jit(solution)/shard_map/all_to_all | solution.py:52
  174.6 7.5 %reshape.44 = bf16[16,2,32768]{2,1,0:T(2,128)(2,1)} reshape(bf16[512,32,64]{2,1,0:T(8,128)(2,1)} %bitcast.117) | data formatting | bytes 4194304
  182.1 5.7 %all-to-all-done.5 = bf16[16,2,32768]{2,1,0:T(2,128)(2,1)} async-done(((bf16[16,2,32768]{2,1,0:T(2,128)(2,1)}), bf16[16,2,32768]{2,1,0:T(2,128)(2,1)}, u32[]{:S(2)}, u32[]{:S(2)}) %all-to-all-start.5) | async-done | bytes 2097184 | tf_op jit(solution)/shard_map/all_to_all | solution.py:63
  192.5 7.4 %reshape.53 = bf16[512,32,64]{2,1,0:T(8,128)(2,1)} reshape(bf16[16,2,32768]{2,1,0:T(2,128)(2,1)} %all-to-all-done.3) | data formatting | bytes 4194304
  207.6 6.8 %copy.69 = f32[32,512,64]{1,2,0:T(8,128)} copy(f32[32,512,64]{2,1,0:T(8,128)} %bitcast.95) | data formatting | bytes 8388608 | tf_op jit(solution)/shard_map/convert_element_type | solution.py:29
  214.4 7.4 %reshape.49 = bf16[512,32,64]{2,1,0:T(8,128)(2,1)} reshape(bf16[16,2,32768]{2,1,0:T(2,128)(2,1)} %all-to-all-done.5) | data formatting | bytes 4194304
  229.5 6.8 %copy.75 = f32[32,512,64]{1,2,0:T(8,128)} copy(f32[32,512,64]{2,1,0:T(8,128)} %bitcast.96) | data formatting | bytes 8388608 | tf_op jit(solution)/shard_map/convert_element_type | solution.py:30
  241.3 5.5 %copy.71 = bf16[32,16,32,64]{3,2,1,0:T(8,128)(2,1)} copy(bf16[32,16,32,64]{3,2,0,1:T(8,128)(2,1)} %bitcast.114) | data formatting | bytes 4194304 | tf_op jit(solution)/shard_map/all_to_all | solution.py:59
  257.0 7.6 %multiply_add_fusion.1 = f32[32,512,64]{1,2,0:T(8,128)} fusion(f32[32,512,64]{1,2,0:T(8,128)} %bitcast.118, f32[32,512,64]{1,2,0:T(8,128)S(1)} %copy-done.5, f32[32,512,64]{1,2,0:T(8,128)} %bitcast.119, f32[32,512,64]{1,2,0:T(8,128)S(1)} %copy-done.4, f32[512]{0:T(512)S(1)} %mul.115, f32[512]{0:T(512)S(1)} %copy-done.15), kind=kLoop, calls=%fused_computation.7 | loop fusion | flops 5242880 | bytes 20975616 | tf_op jit(solution)/shard_map/add | solution.py:29
  264.5 9.2 %copy.77 = f32[32,512,64]{2,0,1:T(8,128)} copy(f32[32,512,64]{1,2,0:T(8,128)} %multiply_add_fusion.1) | data formatting | bytes 8388608 | tf_op jit(solution)/shard_map/add | solution.py:29
  273.7 13.5 %reshape.54 = f32[16,1,65536]{2,1,0:T(1,128)} reshape(f32[512,32,64]{2,1,0:T(8,128)} %bitcast.94) | data formatting | bytes 8388608
  287.2 5.9 %all-to-all-start.6 = ((f32[16,1,65536]{2,1,0:T(1,128)}), f32[16,1,65536]{2,1,0:T(1,128)}, u32[]{:S(2)}, u32[]{:S(2)}) async-start(f32[16,1,65536]{2,1,0:T(1,128)} %reshape.54), calls=%async_computation.6 | async-start | bytes 8388608 | tf_op jit(solution)/shard_map/all_to_all | solution.py:68
  293.1 6.8 %copy.93 = bf16[64,32,8,64]{0,2,3,1:T(8,128)(2,1)} copy(bf16[64,32,8,64]{0,1,3,2:T(8,128)(2,1)} %bitcast.93) | data formatting | bytes 4194304 | tf_op jit(solution)/shard_map/all_to_all | solution.py:52
  300.0 5.4 %reshape.29 = bf16[512,2048]{0,1:T(8,128)(2,1)S(1)} reshape(bf16[8,64,32,64]{1,0,3,2:T(8,128)(2,1)} %bitcast.116) | data formatting | bytes 4194304 | tf_op jit(solution)/shard_map/reshape | solution.py:9
  308.6 34.1 %all-to-all-done.6 = f32[16,1,65536]{2,1,0:T(1,128)} async-done(((f32[16,1,65536]{2,1,0:T(1,128)}), f32[16,1,65536]{2,1,0:T(1,128)}, u32[]{:S(2)}, u32[]{:S(2)}) %all-to-all-start.6) | async-done | bytes 4194336 | tf_op jit(solution)/shard_map/all_to_all | solution.py:68
  343.3 13.8 %reduce = f32[16,65536]{1,0:T(8,128)} reduce(f32[16,1,65536]{2,1,0:T(1,128)} %all-to-all-done.6, f32[]{:T(128)} %broadcast.6), dimensions={1}, to_apply=%all_to_all.110.reduce_sub_computation | reduce | bytes 8388612 | tf_op jit(solution)/shard_map/all_to_all | solution.py:68
  357.1 7.4 %reshape.55 = f32[512,32,64]{2,1,0:T(8,128)} reshape(f32[16,65536]{1,0:T(8,128)} %reduce) | data formatting | bytes 8388608
  364.5 13.1 %copy.79 = f32[16,32,32,64]{3,2,1,0:T(8,128)} copy(f32[16,32,32,64]{3,1,2,0:T(8,128)} %bitcast.97) | data formatting | bytes 8388608 | tf_op jit(solution)/shard_map/all_to_all | solution.py:68
  377.6 6.9 %copy.80 = f32[512,32,64]{0,2,1:T(8,128)} copy(f32[512,32,64]{2,1,0:T(8,128)} %bitcast.98) | data formatting | bytes 8388608 | tf_op jit(solution)/shard_map/all_to_all | solution.py:68
  384.4 8.5 %add_add_fusion = f32[512,32,64]{0,2,1:T(8,128)} fusion(f32[512,32,64]{0,2,1:T(8,128)} %copy.80, bf16[512,32,64]{0,2,1:T(8,128)(2,1)} %copy-done.1, f32[512,32,64]{0,2,1:T(8,128)} %fusion.1, bf16[512,32,64]{0,2,1:T(8,128)(2,1)} %param.18, bf16[32,64,512]{2,1,0:T(8,128)(2,1)S(1)} %bitcast.102, f32[512]{0:T(512)S(1)} %mul.108, f32[512]{0:T(512)S(1)} %copy-done.14, ...), kind=kOutput, calls=%fused_computation.8 | convolution fusion | flops 1082130432 | bytes 19402752 | tf_op jit(solution)/shard_map/dot_general | solution.py:11
  392.9 9.2 %copy.81 = f32[512,32,64]{2,1,0:T(8,128)} copy(f32[512,32,64]{0,2,1:T(8,128)} %add_add_fusion) | data formatting | bytes 8388608 | tf_op jit(solution)/shard_map/add | solution.py:69
  402.1 9.8 %reshape.56 = f32[8,1,131072]{2,1,0:T(1,128)} reshape(f32[512,32,64]{2,1,0:T(8,128)} %copy.81) | data formatting | bytes 8388608
  411.9 5.4 %all-to-all-start.7 = ((f32[8,1,131072]{2,1,0:T(1,128)}), f32[8,1,131072]{2,1,0:T(1,128)}, u32[]{:S(2)}, u32[]{:S(2)}) async-start(f32[8,1,131072]{2,1,0:T(1,128)} %reshape.56), calls=%async_computation.7 | async-start | bytes 8388608 | tf_op jit(solution)/shard_map/all_to_all | solution.py:69
  420.6 45.4 %all-to-all-done.7 = f32[8,1,131072]{2,1,0:T(1,128)} async-done(((f32[8,1,131072]{2,1,0:T(1,128)}), f32[8,1,131072]{2,1,0:T(1,128)}, u32[]{:S(2)}, u32[]{:S(2)}) %all-to-all-start.7) | async-done | bytes 4194336 | tf_op jit(solution)/shard_map/all_to_all | solution.py:69
  466.0 13.9 %reduce.1 = f32[8,131072]{1,0:T(8,128)} reduce(f32[8,1,131072]{2,1,0:T(1,128)} %all-to-all-done.7, f32[]{:T(128)} %broadcast.6), dimensions={1}, to_apply=%all_to_all.114.reduce_sub_computation | reduce | bytes 8388612 | tf_op jit(solution)/shard_map/all_to_all | solution.py:69
  479.9 8.7 %reshape.57 = f32[512,32,64]{2,1,0:T(8,128)} reshape(f32[8,131072]{1,0:T(8,128)} %reduce.1) | data formatting | bytes 8388608
  488.7 14.7 %copy.91 = f32[8,64,32,64]{3,0,2,1:T(8,128)} copy(f32[8,64,32,64]{3,2,1,0:T(8,128)} %bitcast.99) | data formatting | bytes 8388608 | tf_op jit(solution)/shard_map/all_to_all | solution.py:69
  503.4 7.5 %all_to_all.117 = f32[64,32,512]{2,1,0:T(8,128)} reshape(f32[64,32,8,64]{3,2,1,0:T(8,128)} %bitcast.100) | data formatting | bytes 8388608 | tf_op jit(solution)/shard_map/all_to_all | solution.py:69
  510.9 9.1 %add_convert_fusion = (bf16[64,32,512]{2,1,0:T(8,128)(2,1)}, f32[64,32,512]{2,1,0:T(8,128)}) fusion(bf16[64,32,512]{2,1,0:T(8,128)(2,1)S(1)} %copy-done.3, f32[64,32,512]{2,1,0:T(8,128)} %all_to_all.117, bf16[512,512]{1,0:T(8,128)(2,1)S(1)} %copy-done, f32[512]{0:T(512)S(1)} %mul.101, bf16[64,32,512]{2,1,0:T(8,128)(2,1)} %param.20, ...), kind=kOutput, calls=%fused_computation.5 | convolution fusion | flops 1089470464 | bytes 25694208 | tf_op jit(solution)/shard_map/abz,kz->abk/dot_general | solution.py:23
  (55 shorter events, 59.8 us)
Async XLA Ops:
  0.6 510.2 %copy-start = (bf16[512,512]{1,0:T(8,128)(2,1)S(1)}, bf16[512,512]{1,0:T(8,128)(2,1)}, u32[]{:S(2)}) copy-start(bf16[512,512]{1,0:T(8,128)(2,1)} %param.25) | copy-start | bytes 1572868
  9.5 15.2 %copy-start.8 = (bf16[64,32,512]{2,1,0:T(8,128)(2,1)S(1)}, bf16[64,32,512]{2,1,0:T(8,128)(2,1)}, u32[]{:S(2)}) copy-start(bf16[64,32,512]{2,1,0:T(8,128)(2,1)} %param.20) | copy-start | bytes 6291460
  17.2 33.7 %all-to-all-start.2 = ((bf16[8,2,65536]{2,1,0:T(2,128)(2,1)}), bf16[8,2,65536]{2,1,0:T(2,128)(2,1)}, u32[]{:S(2)}, u32[]{:S(2)}) async-start(bf16[8,2,65536]{2,1,0:T(2,128)(2,1)} %reshape.50), calls=%async_computation.2 | async-start | bytes 4194304 | tf_op jit(solution)/shard_map/all_to_all | solution.py:54
  32.5 23.6 %copy-start.2 = (bf16[64,32,512]{2,1,0:T(8,128)(2,1)S(1)}, bf16[64,32,512]{2,1,0:T(8,128)(2,1)}, u32[]{:S(2)}) copy-start(bf16[64,32,512]{2,1,0:T(8,128)(2,1)} %param.15) | copy-start | bytes 6291460
  50.9 31.5 %all-to-all-start.1 = ((bf16[8,2,65536]{2,1,0:T(2,128)(2,1)}), bf16[8,2,65536]{2,1,0:T(2,128)(2,1)}, u32[]{:S(2)}, u32[]{:S(2)}) async-start(bf16[8,2,65536]{2,1,0:T(2,128)(2,1)} %reshape.46), calls=%async_computation.1 | async-start | bytes 4194304 | tf_op jit(solution)/shard_map/all_to_all | solution.py:53
  82.4 31.4 %all-to-all-start = ((bf16[8,2,65536]{2,1,0:T(2,128)(2,1)}), bf16[8,2,65536]{2,1,0:T(2,128)(2,1)S(1)}, u32[]{:S(2)}, u32[]{:S(2)}) async-start(bf16[8,2,65536]{2,1,0:T(2,128)(2,1)} %reshape.42), calls=%async_computation | async-start | bytes 4194304 | tf_op jit(solution)/shard_map/all_to_all | solution.py:52
  113.8 14.6 %copy-start.6 = (bf16[8,2,65536]{2,1,0:T(2,128)(2,1)}, bf16[8,2,65536]{2,1,0:T(2,128)(2,1)S(1)}, u32[]{:S(2)}) copy-start(bf16[8,2,65536]{2,1,0:T(2,128)(2,1)S(1)} %all-to-all-done) | copy-start | bytes 6291460
  113.8 41.0 %all-to-all-start.3 = ((bf16[16,2,32768]{2,1,0:T(2,128)(2,1)}), bf16[16,2,32768]{2,1,0:T(2,128)(2,1)}, u32[]{:S(2)}, u32[]{:S(2)}) async-start(bf16[16,2,32768]{2,1,0:T(2,128)(2,1)} %reshape.52), calls=%async_computation.3 | async-start | bytes 4194304 | tf_op jit(solution)/shard_map/all_to_all | solution.py:62
  140.5 14.2 %copy-start.1 = (bf16[512,32,64]{0,2,1:T(8,128)(2,1)}, bf16[512,32,64]{0,2,1:T(8,128)(2,1)S(1)}, u32[]{:S(2)}) copy-start(bf16[512,32,64]{0,2,1:T(8,128)(2,1)S(1)} %all_to_all.98) | copy-start | bytes 6291460
  154.8 5.9 %copy-start.7 = (bf16[8,2,65536]{2,1,0:T(2,128)(2,1)S(1)}, bf16[8,2,65536]{2,1,0:T(2,128)(2,1)}, u32[]{:S(2)}) copy-start(bf16[8,2,65536]{2,1,0:T(2,128)(2,1)} %copy-done.6) | copy-start | bytes 6291460
  154.8 33.1 %all-to-all-start.5 = ((bf16[16,2,32768]{2,1,0:T(2,128)(2,1)}), bf16[16,2,32768]{2,1,0:T(2,128)(2,1)}, u32[]{:S(2)}, u32[]{:S(2)}) async-start(bf16[16,2,32768]{2,1,0:T(2,128)(2,1)} %reshape.48), calls=%async_computation.5 | async-start | bytes 4194304 | tf_op jit(solution)/shard_map/all_to_all | solution.py:63
  174.6 17.9 %copy-start.15 = (f32[512]{0:T(512)S(1)}, f32[512]{0:T(512)}, u32[]{:S(2)}) copy-start(f32[512]{0:T(512)} %param.23) | copy-start | bytes 6148
  187.9 48.5 %all-to-all-start.4 = ((bf16[16,2,32768]{2,1,0:T(2,128)(2,1)}), bf16[16,2,32768]{2,1,0:T(2,128)(2,1)S(1)}, u32[]{:S(2)}, u32[]{:S(2)}) async-start(bf16[16,2,32768]{2,1,0:T(2,128)(2,1)} %reshape.44), calls=%async_computation.4 | async-start | bytes 4194304 | tf_op jit(solution)/shard_map/all_to_all | solution.py:59
  246.8 3.6 copy-start.10
  250.4 3.3 copy-start.11
  250.4 6.6 %copy-start.5 = (f32[32,512,64]{1,2,0:T(8,128)S(1)}, f32[32,512,64]{1,2,0:T(8,128)}, u32[]{:S(2)}) copy-start(f32[32,512,64]{1,2,0:T(8,128)} %copy.75) | copy-start | bytes 12582916
  253.6 3.3 copy-start.4
  287.2 5.9 %copy-start.14 = (f32[512]{0:T(512)S(1)}, f32[512]{0:T(512)}, u32[]{:S(2)}) copy-start(f32[512]{0:T(512)} %param.22) | copy-start | bytes 6148
  287.2 55.6 %all-to-all-start.6 = ((f32[16,1,65536]{2,1,0:T(1,128)}), f32[16,1,65536]{2,1,0:T(1,128)}, u32[]{:S(2)}, u32[]{:S(2)}) async-start(f32[16,1,65536]{2,1,0:T(1,128)} %reshape.54), calls=%async_computation.6 | async-start | bytes 8388608 | tf_op jit(solution)/shard_map/all_to_all | solution.py:68
  300.0 5.5 %copy-start.12 = (bf16[512,512]{1,0:T(8,128)(2,1)S(1)}, bf16[512,512]{1,0:T(8,128)(2,1)}, u32[]{:S(2)}) copy-start(bf16[512,512]{1,0:T(8,128)(2,1)} %param.26) | copy-start | bytes 1572868
  377.6 6.9 %copy-start.9 = (bf16[512,512]{1,0:T(8,128)(2,1)S(1)}, bf16[512,512]{1,0:T(8,128)(2,1)}, u32[]{:S(2)}) copy-start(bf16[512,512]{1,0:T(8,128)(2,1)} %param.27) | copy-start | bytes 1572868
  411.9 5.4 %copy-start.16 = (f32[512]{0:T(512)S(1)}, f32[512]{0:T(512)}, u32[]{:S(2)}) copy-start(f32[512]{0:T(512)} %param.21) | copy-start | bytes 6148
  411.9 5.4 %copy-start.3 = (bf16[64,32,512]{2,1,0:T(8,128)(2,1)S(1)}, bf16[64,32,512]{2,1,0:T(8,128)(2,1)}, u32[]{:S(2)}) copy-start(bf16[64,32,512]{2,1,0:T(8,128)(2,1)} %param.15) | copy-start | bytes 6291460
  411.9 5.4 %copy-start.13 = (bf16[512,512]{1,0:T(8,128)(2,1)S(1)}, bf16[512,512]{1,0:T(8,128)(2,1)}, u32[]{:S(2)}) copy-start(bf16[512,512]{1,0:T(8,128)(2,1)} %param.24) | copy-start | bytes 1572868
  411.9 54.1 %all-to-all-start.7 = ((f32[8,1,131072]{2,1,0:T(1,128)}), f32[8,1,131072]{2,1,0:T(1,128)}, u32[]{:S(2)}, u32[]{:S(2)}) async-start(f32[8,1,131072]{2,1,0:T(1,128)} %reshape.56), calls=%async_computation.7 | async-start | bytes 8388608 | tf_op jit(solution)/shard_map/all_to_all | solution.py:69
where the time goes:
time: 530 us; the launch traced here: 520 us
  local copies, waits for them, and re-layouts  291 us (55%)
  waiting for transfers between devices  109 us (21%)
  starting transfers between devices  46.8 us (9%)
  other arithmetic  42 us (8%)
  matrix products  30.6 us (6%)
    unnamed x53, local copies, waits for them, and re-layouts  149 us
    all_to_all x1, waiting for transfers between devices, on_device(): lax.all_to_all(term_y + back_z, 'row', split_axis=0, concat_axis=2, tiled...  45.4 us
    all_to_all x1, waiting for transfers between devices, on_device(): lax.all_to_all(term_z, 'col', split_axis=1, concat_axis=0, tiled=True)  34.1 us
    all_to_all x2, local copies, waits for them, and re-layouts, on_device(): lax.all_to_all(term_y + back_z, 'row', split_axis=0, concat_axis=2, tiled...  22.2 us
    all_to_all x3, local copies, waits for them, and re-layouts, on_device(): lax.all_to_all(term_z, 'col', split_axis=1, concat_axis=0, tiled=True)  20.5 us
    all_to_all x3, local copies, waits for them, and re-layouts, on_device(): lax.all_to_all(diffusivity, 'row', split_axis=2, concat_axis=0, tiled=True)  18.8 us
    all_to_all x2, local copies, waits for them, and re-layouts, on_device(): lax.all_to_all(scalar, 'row', split_axis=2, concat_axis=0, tiled=True)  15.8 us
    all_to_all x1, other arithmetic, on_device(): lax.all_to_all(term_y + back_z, 'row', split_axis=0, concat_axis=2, tiled...  13.9 us
  transfers between devices with their start and end apart: 8, of which 6 were waited for; matrix products, arithmetic and copies ran while one was open for 32% of the time, Pallas kernels for 0%

commit v1 on v0

v1 whole, which is shorter than its diff:
```python
import jax
import jax.numpy as jnp
from jax import lax
from jax.experimental import pallas as pl
from jax.experimental.pallas import tpu as pltpu
from jax.sharding import PartitionSpec as P

F32 = jnp.float32
BF16 = jnp.bfloat16
F16 = jnp.float16
VMEM_LIMIT = 60 * 1024 * 1024

NJ, NK, NI = 64, 32, 512
YB = 8
PIECE = YB * 64


def params():
    return pltpu.CompilerParams(vmem_limit_bytes=VMEM_LIMIT)


def pow_of(values):
    top = jnp.max(jnp.abs(values), axis=0, keepdims=True)
    top = jnp.max(top, axis=1, keepdims=True)
    return jnp.floor(jnp.log2(jnp.maximum(top, 1e-30)))


def pack_kernel(at, s_ref, row_ref, z0_ref, z1_ref, z2_ref, z3_ref):
    zc = at[0]
    for s, out in enumerate((z0_ref, z1_ref, z2_ref, z3_ref)):
        off = pl.multiple_of(lax.rem(zc + s, 4) * 128, 128)
        out[...] = s_ref[:, :, pl.ds(off, 128)]
    for c in range(4):
        chunk = s_ref[:, :, 128 * c : 128 * (c + 1)]
        top, bot = chunk[:, :16, :], chunk[:, 16:, :]
        row_ref[2 * c] = jnp.concatenate([top[:, :, :64], bot[:, :, :64]], axis=-1)
        row_ref[2 * c + 1] = jnp.concatenate([top[:, :, 64:], bot[:, :, 64:]], axis=-1)


def pack(at, scalar):
    jb = 16
    piece = jax.ShapeDtypeStruct((NJ, NK, 128), BF16)
    piece_spec = pl.BlockSpec((jb, NK, 128), lambda j, at: (j, 0, 0))
    return pl.pallas_call(
        pack_kernel,
        grid_spec=pltpu.PrefetchScalarGridSpec(
            num_scalar_prefetch=1,
            grid=(NJ // jb,),
            in_specs=[pl.BlockSpec((jb, NK, NI), lambda j, at: (j, 0, 0))],
            out_specs=[pl.BlockSpec((8, jb, 16, 128), lambda j, at: (0, j, 0, 0))] + [piece_spec] * 4,
        ),
        out_shape=[jax.ShapeDtypeStruct((8, NJ, 16, 128), BF16)] + [piece] * 4,
        compiler_params=params(),
        name="pack",
    )(at, scalar)


def operator_kernel(at, first_ref, second_ref, out_ref):
    zc, pair = at[0], at[1]
    rows = []
    for t in range(4):
        start = pl.multiple_of(128 * lax.rem(zc + t, 4) + 32 * pair, 32)
        rows += [first_ref[pl.ds(start, 32), :], second_ref[pl.ds(start, 32), :]]
    rows = jnp.concatenate(rows, axis=0)
    at_k = lax.broadcasted_iota(jnp.int32, (512, 512), 0)
    m = lax.broadcasted_iota(jnp.int32, (512, 512), 1)
    s, flip, low = m // 128, (m // 32) % 4, m % 32
    block = 128 * lax.rem(zc + 4 - s, 4) + 32 * jnp.bitwise_xor(pair, flip)
    pick = jnp.where(at_k == block + low, 1.0, 0.0).astype(BF16)
    out_ref[...] = jnp.dot(rows, pick, preferred_element_type=F32).astype(BF16)


def operator_rows(at, first, second):
    whole = pl.BlockSpec(memory_space=pltpu.VMEM)
    return pl.pallas_call(
        operator_kernel,
        in_specs=[pl.BlockSpec(memory_space=pltpu.SMEM), whole, whole],
        out_specs=whole,
        out_shape=jax.ShapeDtypeStruct((256, 512), BF16),
        compiler_params=params(),
        name="operator",
    )(at, first, second)


def y_kernel(s_ref, drift_ref, first_ref, second_ref, metric_ref, out_ref, s32, g32, c32):
    s32[...] = s_ref[...].astype(F32).reshape(8 * NJ * 16, 128)
    metric = metric_ref[...]
    metric2 = metric * metric
    for z in range(0, 16, 2):
        cols = jnp.concatenate(
            [s32[pl.ds(z + h, 512, stride=16), :].astype(BF16) for h in range(2)], axis=1
        )
        grad = jnp.dot(first_ref[...], cols, preferred_element_type=F32) * metric
        curv = jnp.dot(second_ref[...], cols, preferred_element_type=F32) * metric2
        for h in range(2):
            g32[pl.ds(z + h, 512, stride=16), :] = grad[:, 128 * h : 128 * (h + 1)]
            c32[pl.ds(z + h, 512, stride=16), :] = curv[:, 128 * h : 128 * (h + 1)]
    for d in range(8):
        wind = drift_ref[NJ * d : NJ * (d + 1)]
        wind = jnp.concatenate([wind[:, :16, :], wind[:, 16:, :]], axis=-1)
        p = wind.astype(F32).reshape(1024, 128) * g32[1024 * d : 1024 * (d + 1), :]
        c = c32[1024 * d : 1024 * (d + 1), :]
        pe, ce = pow_of(p), pow_of(c)
        out_ref[d, 0:1024, :] = p * jnp.exp2(13.0 - pe)
        out_ref[d, 1024:2048, :] = c * jnp.exp2(13.0 - ce)
        out_ref[d, 2048:2056, :] = jnp.broadcast_to(pe, (8, 128))
        out_ref[d, 2056:2064, :] = jnp.broadcast_to(ce, (8, 128))


def y_terms(s, drift, first, second, metric):
    whole = pl.BlockSpec(memory_space=pltpu.VMEM)
    scratch = pltpu.VMEM((8 * NJ * 16, 128), F32)
    return pl.pallas_call(
        y_kernel,
        in_specs=[whole] * 5,
        out_specs=whole,
        out_shape=jax.ShapeDtypeStruct((8, 2064, 128), F32),
        scratch_shapes=[scratch, scratch, scratch],
        compiler_params=params(),
        name="yterms",
    )(s, drift, first, second, metric)


def z_kernel(*refs):
    a_ref, pieces, outs = refs[0], refs[1:17], refs[17:21]
    rows = a_ref[...]
    results = []
    for y in range(0, YB, 2):
        cols = [jnp.concatenate([p[y + h] for p in pieces], axis=0) for h in range(2)]
        results.append(jnp.dot(rows, jnp.concatenate(cols, axis=1), preferred_element_type=F32))
    top = jnp.abs(results[0])
    for r in results[1:]:
        top = jnp.maximum(top, jnp.abs(r))
    e = pow_of(top)
    scale = jnp.exp2(13.0 - e)
    for y in range(YB):
        value = results[y // 2][:, 128 * (y % 2) : 128 * (y % 2 + 1)] * scale
        for t in range(4):
            outs[t][0, 64 * y : 64 * (y + 1), :] = value[64 * t : 64 * (t + 1), :]
    for t in range(4):
        outs[t][0, PIECE : PIECE + 16, :] = jnp.broadcast_to(e, (16, 128))


def z_terms(rows, pieces):
    out = jax.ShapeDtypeStruct((NJ // YB, PIECE + 16, 128), F32)
    return pl.pallas_call(
        z_kernel,
        grid=(NJ // YB,),
        in_specs=[pl.BlockSpec((256, 512), lambda j: (0, 0))]
        + [pl.BlockSpec((YB, NK, 128), lambda j: (j, 0, 0))] * 16,
        out_specs=[pl.BlockSpec((1, PIECE + 16, 128), lambda j: (j, 0, 0))] * 4,
        out_shape=[out] * 4,
        compiler_params=params(),
        name="zterms",
    )(rows, *pieces)


def xy_kernel(s_ref, reg_ref, drift_ref, diff_ref, first_ref, second_ref, metric_ref, p_ref, c_ref, e_ref, out_ref):
    jb = s_ref.shape[0]
    flat = s_ref[...].reshape(jb * NK, NI)
    last = (((1,), (1,)), ((), ()))
    grad = lax.dot_general(flat, first_ref[...], last, preferred_element_type=F32)
    curv = lax.dot_general(flat, second_ref[...], last, preferred_element_type=F32)
    metric = metric_ref[...]
    diff = diff_ref[...].astype(F32).reshape(jb * NK, NI)
    total = (drift_ref[...].astype(F32).reshape(jb * NK, NI) * metric) * grad
    total = total + (diff * (metric * metric)) * curv
    total = total.reshape(jb, NK, NI)
    diff = diff.reshape(jb, NK, NI)

    def native(ref, at):
        lows, highs = [], []
        for d in range(8):
            scale = jnp.exp2(e_ref[d, at : at + 1, :] - 13.0)
            v = (ref[d] * scale).reshape(jb, 16, 128)
            lows.append(v[:, :, :64])
            highs.append(v[:, :, 64:])
        return jnp.concatenate(
            [jnp.concatenate(lows, axis=-1), jnp.concatenate(highs, axis=-1)], axis=1
        )

    total = total + (native(p_ref, 0) + diff * native(c_ref, 8))
    out_ref[...] = (-5.0 / 9.0) * reg_ref[...] + 0.5 * total


def xy_terms(scalar, reg, drift, diff, first, second, metric, y_back):
    jb = 8
    field = pl.BlockSpec((jb, NK, NI), lambda j: (j, 0, 0))
    op = pl.BlockSpec((NI, NI), lambda j: (0, 0))
    n = NJ // jb
    return pl.pallas_call(
        xy_kernel,
        grid=(n,),
        in_specs=[
            field, field, field, field, op, op,
            pl.BlockSpec((1, NI), lambda j: (0, 0)),
            pl.BlockSpec((8, jb * 16, 128), lambda j: (0, j, 0)),
            pl.BlockSpec((8, jb * 16, 128), lambda j: (0, n + j, 0)),
            pl.BlockSpec((8, 16, 128), lambda j: (0, 128, 0)),
        ],
        out_specs=field,
        out_shape=jax.ShapeDtypeStruct((NJ, NK, NI), F32),
        compiler_params=params(),
        name="xyterms",
    )(scalar, reg, drift, diff, first, second, metric, y_back, y_back, y_back)


def last_kernel(at, s_ref, part_ref, drift_ref, diff_ref, metric_ref, piece_ref, *refs):
    reg_ref, out_ref = refs[-2:]
    metric = metric_ref[...][None]
    for h in range(LB):
        rows = slice(YB * h, YB * (h + 1))
        scale = jnp.exp2(piece_ref[h, PIECE : PIECE + 1, :] - 13.0)
        value = (piece_ref[h, 0:PIECE, :] * scale).reshape(YB, 2, NK, 128)
        term = (drift_ref[rows].astype(F32) * metric) * value[:, 0]
        term = term + (diff_ref[rows].astype(F32) * (metric * metric)) * value[:, 1]
        reg = part_ref[rows] + 0.5 * term
        reg_ref[rows] = reg
        out_ref[rows] = (s_ref[rows].astype(F32) + (15.0 / 16.0) * reg).astype(BF16)


LB = 2


def last_terms(at, t, scalar, part, drift, diff, metric, piece, done):
    lanes = pl.BlockSpec((LB * YB, NK, 128), lambda j, at: (j, 0, lax.rem(at[0] + 4 - t, 4)))
    return pl.pallas_call(
        last_kernel,
        grid_spec=pltpu.PrefetchScalarGridSpec(
            num_scalar_prefetch=1,
            grid=(NJ // (LB * YB),),
            in_specs=[lanes] * 4
            + [
                pl.BlockSpec((NK, 128), lambda j, at: (0, 0)),
                pl.BlockSpec((LB, PIECE + 16, 128), lambda j, at: (j, 0, 0)),
            ]
            + [pl.BlockSpec(memory_space=pl.ANY)] * len(done),
            out_specs=[lanes, lanes],
        ),
        out_shape=[
            jax.ShapeDtypeStruct((NJ, NK, NI), F32),
            jax.ShapeDtypeStruct((NJ, NK, NI), BF16),
        ],
        input_output_aliases={7 + i: i for i in range(len(done))},
        compiler_params=params(),
        name="last",
    )(at, scalar, part, drift, diff, metric, piece, *done)


def ring(x, shift):
    return lax.ppermute(x, "col", [(c, (c + 4 * shift) % 16) for c in range(16)])


def flip(x, bits):
    return lax.ppermute(x, "col", [(c, c ^ bits) for c in range(16)])


def on_device(
    scalar,
    register_in,
    drift_x,
    drift_y,
    drift_z,
    diffusivity,
    metric_x,
    metric_y,
    metric_z,
    first_x,
    second_x,
    first_y,
    second_y,
    first_z,
    second_z,
):
    col = lax.axis_index("col")
    at = jnp.stack([col // 4, col % 4]).astype(jnp.int32)
    row_send, *mine = pack(at, scalar)
    here = [mine[0]] + [ring(mine[s], s) for s in range(1, 4)]
    across = [flip(part, 2) for part in here]
    scalar_y = lax.all_to_all(row_send, "row", 0, 0, tiled=False)
    rows = operator_rows(at, first_z, second_z)
    scalar_y, rows, *early = lax.optimization_barrier([scalar_y, rows, across[0], *here[1:]])
    y_out = y_terms(scalar_y, drift_y, first_y, second_y, metric_y[:, None]).astype(F16)
    beside = [flip(part, 1) for part in here]
    y_out, *held = lax.optimization_barrier([y_out, *across, *beside])
    pieces = []
    for s in range(4):
        pieces += [here[s], held[4 + s], held[s], flip(held[s], 1)]
    y_back = lax.all_to_all(y_out, "row", 0, 0, tiled=False).astype(F32)
    z_out = z_terms(rows, pieces)
    z_back = [z_out[0]] + [ring(z_out[t].astype(F16), t).astype(F32) for t in range(1, 4)]
    part = xy_terms(
        scalar, register_in, drift_x, diffusivity, first_x, second_x, metric_x[None, :], y_back
    )
    own = lax.dynamic_slice(metric_z, (NK * col,), (NK,))
    own = jnp.broadcast_to(own[:, None], (NK, 128))
    done = ()
    for t in (0, 1, 3, 2):
        done = last_terms(at, t, scalar, part, drift_z, diffusivity, own, z_back[t], done)
    return tuple(done)


def solution(mesh):
    in_specs = (
        P("row", "col", None),
        P("row", "col", None),
        P("row", "col", None),
        P(None, "col", "row"),
        P("row", "col", None),
        P("row", "col", None),
        P(),
        P(),
        P(),
        P(),
        P(),
        P(),
        P(),
        P(),
        P(),
    )
    out_specs = (P("row", "col", None), P("row", "col", None))
    return jax.shard_map(
        on_device, mesh=mesh, in_specs=in_specs, out_specs=out_specs, check_vma=False
    )
```

time: 530 us -> 208 us (0.39); the launches traced: 520 us -> 205 us
  local copies, waits for them, and re-layouts: 291 us -> 13.1 us
  Pallas kernels: 0 us -> 64.2 us
  waiting for transfers between devices: 109 us -> 66 us
  matrix products: 30.6 us -> 0 us
  other arithmetic: 42 us -> 22.9 us
  starting transfers between devices: 46.8 us -> 38.6 us
    unnamed x53 -> x31, local copies, waits for them, and re-layouts: 149 us -> 10.7 us
    all_to_all x8 -> x2, waiting for transfers between devices: 109 us -> 0.01 us  [the longest x1 0.01 us: on_device(): y_back = lax.all_to_all(y_out, 'row', 0, 0, tiled=False).astype(F32)]
    all_to_all x13 -> x0, local copies, waits for them, and re-layouts: 95.4 us -> none  [the longest x2 22.2 us: on_device(): lax.all_to_all(term_y + back_z, 'row', split_axis=0, concat_axis=2, tiled...]
    ppermute x0 -> x18, waiting for transfers between devices: none -> 66 us  [the longest x6 59.4 us: ring(): lax.ppermute(x, 'col', [(c, (c + 4 * shift) % 16) for c in range(16)])]
    pallas_call x0 -> x9, Pallas kernels: none -> 64.2 us  [the longest x4 20.3 us: last_terms(): pl.pallas_call(last_kernel, grid_spec=pltpu.PrefetchScalarGridSpec(num_sc...]
    all_to_all x8 -> x2, starting transfers between devices: 46.8 us -> 14.6 us  [the longest x1 7.62 us: on_device(): scalar_y = lax.all_to_all(row_send, 'row', 0, 0, tiled=False)]
    all_to_all x2 -> x0, other arithmetic: 27.7 us -> none  [the longest x1 13.9 us: on_device(): lax.all_to_all(term_y + back_z, 'row', split_axis=0, concat_axis=2, tiled...]
    dot_general x4 -> x0, matrix products: 24.1 us -> none  [the longest x1 9.12 us: along_last(): jnp.einsum('abz,kz->abk', pencil, curv_op, preferred_element_type=jnp.flo...]
  transfers between devices with their start and end apart: 8 -> 20, of which waited for: 6 -> 9; matrix products, arithmetic and copies ran while one was open for 32% -> 12% of each run, Pallas kernels for 0% -> 13%
where the time goes in v1:
time: 208 us; the launch traced here: 205 us
  waiting for transfers between devices  66 us (32%)
  Pallas kernels  64.2 us (31%)
  starting transfers between devices  38.6 us (19%)
  other arithmetic  22.9 us (11%)
  local copies, waits for them, and re-layouts  13.1 us (6%)
    ppermute x6, waiting for transfers between devices, ring(): lax.ppermute(x, 'col', [(c, (c + 4 * shift) % 16) for c in range(16)])  59.4 us
    pallas_call x4, Pallas kernels, last_terms(): pl.pallas_call(last_kernel, grid_spec=pltpu.PrefetchScalarGridSpec(num_sc...  20.3 us
    ppermute x12, starting transfers between devices, flip(): return lax.ppermute(x, 'col', [(c, c ^ bits) for c in range(16)])  12.9 us
    pallas_call x1, Pallas kernels, y_terms(): pl.pallas_call(y_kernel, in_specs=[whole] * 5, out_specs=whole, out_shape...  12.9 us
    pallas_call x1, Pallas kernels, xy_terms(): pl.pallas_call(xy_kernel, grid=(n,), in_specs=[field, field, field, field...  12.2 us
    pallas_call x1, Pallas kernels, z_terms(): pl.pallas_call(z_kernel, grid=(NJ // YB,), in_specs=[pl.BlockSpec((256, 5...  11.2 us
    ppermute x6, starting transfers between devices, ring(): lax.ppermute(x, 'col', [(c, (c + 4 * shift) % 16) for c in range(16)])  11 us
    unnamed x31, local copies, waits for them, and re-layouts  10.7 us
  transfers between devices with their start and end apart: 20, of which 9 were waited for; matrix products, arithmetic and copies ran while one was open for 12% of the time, Pallas kernels for 13%

profile of v1, /device:TPU:1, one launch (start us, length us, event | category | flops | bytes accessed | tf_op | source)
XLA Modules:
  0.0 205.5 jit_solution(11308355975193569409)
XLA Ops:
  0.6 0.7 pad_add_fusion.at
  1.3 5.3 %pack.1 = (bf16[8,64,16,128]{3,2,1,0:T(8,128)(2,1)}, bf16[64,32,128]{2,1,0:T(8,128)(2,1)}, bf16[64,32,128]{2,1,0:T(8,128)(2,1)}, bf16[64,32,128]{2,1,0:T(8,128)(2,1)}, bf16[64,32,128]{2,1,0:T(8,128)(2,1)}) custom-call(s32[2]{0:T(128)} %pad_add_fusion.at, bf16[64,32,512]{2,1,0:T(8,128)(2,1)} %s_ref.11), custom_call_target="tpu_custom_call" | custom-call | tf_op jit(solution)/shard_map/pack/pallas_call | solution.py:44
  6.6 7.6 %all-to-all-start = ((bf16[8,64,16,128]{3,2,1,0:T(8,128)(2,1)}), bf16[8,64,16,128]{3,2,1,0:T(8,128)(2,1)S(1)}, u32[]{:S(2)}, u32[]{:S(2)}) async-start(bf16[8,64,16,128]{3,2,1,0:T(8,128)(2,1)} %get-tuple-element.28), calls=%async_computation | async-start | bytes 4194304 | tf_op jit(solution)/shard_map/all_to_all | solution.py:280
  14.2 1.6 collective-permute-start.1
  15.8 3.3 %collective-permute-start.2 = (bf16[64,32,128]{2,1,0:T(8,128)(2,1)}, bf16[64,32,128]{2,1,0:T(8,128)(2,1)}, u32[]{:S(2)}, u32[]{:S(2)}) collective-permute-start(bf16[64,32,128]{2,1,0:T(8,128)(2,1)} %get-tuple-element.31), channel_id=1, source_target_pairs={{0,8},{1,9},{2,10},{3,11},{4,12},{5,13},{6,14},{7,15},{8,0},{9,1},... | collective-permute-start | bytes 1572872 | tf_op jit(solution)/shard_map/ppermute | solution.py:251
  19.1 0.7 collective-permute-start.3
  19.9 1.8 collective-permute-start.7
  22.0 7.5 %collective-permute-done.1.refs_5_ = bf16[64,32,128]{2,1,0:T(8,128)(2,1)S(1)} collective-permute-done((bf16[64,32,128]{2,1,0:T(8,128)(2,1)}, bf16[64,32,128]{2,1,0:T(8,128)(2,1)S(1)}, u32[]{:S(2)}, u32[]{:S(2)}) %collective-permute-start.1) | collective-permute-done | bytes 524320 | tf_op jit(solution)/shard_map/ppermute | solution.py:251
  29.5 1.8 collective-permute-start.8
  31.3 10.4 %collective-permute-done.2.refs_9_ = bf16[64,32,128]{2,1,0:T(8,128)(2,1)} collective-permute-done((bf16[64,32,128]{2,1,0:T(8,128)(2,1)}, bf16[64,32,128]{2,1,0:T(8,128)(2,1)}, u32[]{:S(2)}, u32[]{:S(2)}) %collective-permute-start.2) | collective-permute-done | bytes 524320 | tf_op jit(solution)/shard_map/ppermute | solution.py:251
  42.0 2.1 %collective-permute-start.9 = (bf16[64,32,128]{2,1,0:T(8,128)(2,1)}, bf16[64,32,128]{2,1,0:T(8,128)(2,1)}, u32[]{:S(2)}, u32[]{:S(2)}) collective-permute-start(bf16[64,32,128]{2,1,0:T(8,128)(2,1)} %collective-permute-done.2.refs_9_), channel_id=1, source_target_pairs={{0,1},{1,0},{2,3},{3,2},{4,5},{5,4},{6,7},{7,6},{8,9},{9,8},{10,11... | collective-permute-start | bytes 1572872 | tf_op jit(solution)/shard_map/ppermute | solution.py:255
  44.2 1.2 collective-permute-start.5
  45.3 3.2 %collective-permute-done.refs_3_ = bf16[64,32,128]{2,1,0:T(8,128)(2,1)S(1)} collective-permute-done((bf16[64,32,128]{2,1,0:T(8,128)(2,1)S(1)}, bf16[64,32,128]{2,1,0:T(8,128)(2,1)S(1)}, u32[]{:S(2)}, u32[]{:S(2)}) %collective-permute-start) | collective-permute-done | bytes 524320 | tf_op jit(solution)/shard_map/ppermute | solution.py:255
  48.5 2.7 %collective-permute-start.10 = (bf16[64,32,128]{2,1,0:T(8,128)(2,1)}, bf16[64,32,128]{2,1,0:T(8,128)(2,1)S(1)}, u32[]{:S(2)}, u32[]{:S(2)}) collective-permute-start(bf16[64,32,128]{2,1,0:T(8,128)(2,1)} %collective-permute-done.3.refs_13_), channel_id=1, source_target_pairs={{0,1},{1,0},{2,3},{3,2},{4,5},{5,4},{6,7},{7,6},{8,9},{9,8},{10,11... | collective-permute-start | bytes 1572872 | tf_op jit(solution)/shard_map/ppermute | solution.py:255
  51.3 1.4 collective-permute-start.6
  52.7 0.9 copy.25.metric_ref
  53.6 7.4 %copy.24.drift_ref = bf16[512,32,64]{2,1,0:T(8,128)(2,1)} copy(bf16[512,32,64]{0,2,1:T(8,128)(2,1)} %param.18) | data formatting | bytes 4194304 | tf_op args[3]
  61.0 2.2 %operator.1.refs_0_ = bf16[256,512]{1,0:T(8,128)(2,1)} custom-call(s32[2]{0:T(128)} %pad_add_fusion.at, bf16[512,512]{1,0:T(8,128)(2,1)} %first_ref.3, bf16[512,512]{1,0:T(8,128)(2,1)} %second_ref.3), custom_call_target="tpu_custom_call" | custom-call | tf_op jit(solution)/shard_map/operator/pallas_call | solution.py:75
  63.2 1.3 copy-done
  64.5 12.9 %yterms.1 = f32[8,2064,128]{2,1,0:T(8,128)} custom-call(bf16[8,64,16,128]{3,2,1,0:T(8,128)(2,1)} %copy-done, bf16[512,32,64]{2,1,0:T(8,128)(2,1)} %copy.24.drift_ref, bf16[512,512]{1,0:T(8,128)(2,1)} %first_ref.4, bf16[512,512]{1,0:T(8,128)(2,1)} %second_ref.4, f32[512,1]{1,0:T(8,128)} %copy.25.metric_ref), custom_call_target="tpu_custom_call" | custom-call | tf_op jit(solution)/shard_map/yterms/pallas_call | solution.py:113
  77.4 6.0 %convert_element_type.24 = f16[8,2064,128]{2,1,0:T(8,128)(2,1)} convert(f32[8,2064,128]{2,1,0:T(8,128)} %yterms.1) | non-fusion elementwise | flops 2113536 | bytes 12681216 | tf_op jit(solution)/shard_map/convert_element_type | solution.py:283
  83.5 0.8 copy-done.9
  84.3 7.0 %all-to-all-start.1 = ((f16[8,2064,128]{2,1,0:T(8,128)(2,1)}), f16[8,2064,128]{2,1,0:T(8,128)(2,1)}, u32[]{:S(2)}, u32[]{:S(2)}) async-start(f16[8,2064,128]{2,1,0:T(8,128)(2,1)} %convert_element_type.24), calls=%async_computation.1 | async-start | bytes 8454144 | tf_op jit(solution)/shard_map/all_to_all | solution.py:289
  91.3 0.7 collective-permute-start.11
  92.6 0.9 collective-permute-done.11.refs_4_
  93.5 1.0 collective-permute-done.12.refs_8_
  94.5 0.7 collective-permute-done.13.refs_12_
  95.2 0.7 collective-permute-done.14.refs_16_
  96.0 0.8 copy-done.13
  96.8 11.2 %zterms.1 = (f32[8,528,128]{2,1,0:T(8,128)}, f32[8,528,128]{2,1,0:T(8,128)}, f32[8,528,128]{2,1,0:T(8,128)}, f32[8,528,128]{2,1,0:T(8,128)}) custom-call(bf16[256,512]{1,0:T(8,128)(2,1)} %operator.1.refs_0_, bf16[64,32,128]{2,1,0:T(8,128)(2,1)} %get-tuple-element.29.refs_1_, bf16[64,32,128]{2,1,0:T(8,128)(2,1)} %copy-done.5, bf16[64,32,128]{2,1,0:T(8,128)(2,1)} %copy-done.6, ...), custom_call_target="tpu_custom_call" | custom-call | tf_op jit(solution)/shard_map/zterms/pallas_call | solution.py:146
  108.0 1.9 convert_element_type.28
  110.3 1.1 convert_element_type.30
  111.4 1.6 collective-permute-start.17
  113.0 2.1 %collective-permute-start.16 = (f16[8,528,128]{2,1,0:T(8,128)(2,1)S(1)}, f16[8,528,128]{2,1,0:T(8,128)(2,1)S(1)}, u32[]{:S(2)}, u32[]{:S(2)}) collective-permute-start(f16[8,528,128]{2,1,0:T(8,128)(2,1)S(1)} %convert_element_type.28), channel_id=1, source_target_pairs={{0,12},{1,13},{2,14},{3,15},{4,0},{5,1},{6,2},{7,3},{8,4},{9,5},{1... | collective-permute-start | bytes 3244040 | tf_op jit(solution)/shard_map/ppermute | solution.py:251
  115.3 1.6 collective-permute-start.15
  116.9 0.8 dynamic_slice.3
  117.7 21.7 %collective-permute-done.17 = f16[8,528,128]{2,1,0:T(8,128)(2,1)} collective-permute-done((f16[8,528,128]{2,1,0:T(8,128)(2,1)}, f16[8,528,128]{2,1,0:T(8,128)(2,1)}, u32[]{:S(2)}, u32[]{:S(2)}) %collective-permute-start.17) | collective-permute-done | bytes 1081376 | tf_op jit(solution)/shard_map/ppermute | solution.py:251
  139.4 2.8 %convert_element_type.31.piece_ref = f32[8,528,128]{2,1,0:T(8,128)} convert(f16[8,528,128]{2,1,0:T(8,128)(2,1)} %collective-permute-done.17) | non-fusion elementwise | flops 540672 | bytes 3244032 | tf_op jit(solution)/shard_map/convert_element_type | solution.py:291
  142.2 1.5 convert_element_type.29.piece_ref
  143.7 19.7 %collective-permute-done.15 = f16[8,528,128]{2,1,0:T(8,128)(2,1)} collective-permute-done((f16[8,528,128]{2,1,0:T(8,128)(2,1)S(1)}, f16[8,528,128]{2,1,0:T(8,128)(2,1)}, u32[]{:S(2)}, u32[]{:S(2)}) %collective-permute-start.15) | collective-permute-done | bytes 1081376 | tf_op jit(solution)/shard_map/ppermute | solution.py:251
  163.4 2.8 %convert_element_type.27.piece_ref = f32[8,528,128]{2,1,0:T(8,128)} convert(f16[8,528,128]{2,1,0:T(8,128)(2,1)} %collective-permute-done.15) | non-fusion elementwise | flops 540672 | bytes 3244032 | tf_op jit(solution)/shard_map/convert_element_type | solution.py:291
  166.2 6.0 %convert_element_type.25.p_ref.c_ref.e_ref = f32[8,2064,128]{2,1,0:T(8,128)} convert(f16[8,2064,128]{2,1,0:T(8,128)(2,1)} %all-to-all-done.1) | non-fusion elementwise | flops 2113536 | bytes 12681216 | tf_op jit(solution)/shard_map/convert_element_type | solution.py:289
  172.2 12.2 %xyterms.1.part_ref = f32[64,32,512]{2,1,0:T(8,128)} custom-call(bf16[64,32,512]{2,1,0:T(8,128)(2,1)} %s_ref.11, f32[64,32,512]{2,1,0:T(8,128)} %reg_ref.1, bf16[64,32,512]{2,1,0:T(8,128)(2,1)} %drift_ref.6, bf16[64,32,512]{2,1,0:T(8,128)(2,1)} %diff_ref.9, bf16[512,512]{1,0:T(8,128)(2,1)} %first_ref.5, bf16[512,512]{1,0:T(8,128)(2,1)} %second_ref.5, ...), custom_call_target="tpu_custom_call" | custom-call | tf_op jit(solution)/shard_map/xyterms/pallas_call | solution.py:191
  184.5 0.7 broadcast_in_dim.14.metric_ref
  185.1 5.1 %last.4 = (f32[64,32,512]{2,1,0:T(8,128)}, bf16[64,32,512]{2,1,0:T(8,128)(2,1)}) custom-call(s32[2]{0:T(128)} %pad_add_fusion.at, bf16[64,32,512]{2,1,0:T(8,128)(2,1)} %s_ref.11, f32[64,32,512]{2,1,0:T(8,128)} %xyterms.1.part_ref, bf16[64,32,512]{2,1,0:T(8,128)(2,1)} %drift_ref.10, bf16[64,32,512]{2,1,0:T(8,128)(2,1)} %diff_ref.9, ...), custom_call_target="tpu_custom_call" | custom-call | tf_op jit(solution)/shard_map/last/pallas_call | solution.py:227
  190.2 5.1 %last.5 = (f32[64,32,512]{2,1,0:T(8,128)}, bf16[64,32,512]{2,1,0:T(8,128)(2,1)}) custom-call(s32[2]{0:T(128)} %pad_add_fusion.at, bf16[64,32,512]{2,1,0:T(8,128)(2,1)} %s_ref.11, f32[64,32,512]{2,1,0:T(8,128)} %xyterms.1.part_ref, bf16[64,32,512]{2,1,0:T(8,128)(2,1)} %drift_ref.10, ...), custom_call_target="tpu_custom_call", output_to_operand_aliasing={{0}: (7, {}), {1}: (8, {})} | custom-call | tf_op jit(solution)/shard_map/last/pallas_call | solution.py:227
  195.3 5.1 %last.6 = (f32[64,32,512]{2,1,0:T(8,128)}, bf16[64,32,512]{2,1,0:T(8,128)(2,1)}) custom-call(s32[2]{0:T(128)} %pad_add_fusion.at, bf16[64,32,512]{2,1,0:T(8,128)(2,1)} %s_ref.11, f32[64,32,512]{2,1,0:T(8,128)} %xyterms.1.part_ref, bf16[64,32,512]{2,1,0:T(8,128)(2,1)} %drift_ref.10, ...), custom_call_target="tpu_custom_call", output_to_operand_aliasing={{0}: (7, {}), {1}: (8, {})} | custom-call | tf_op jit(solution)/shard_map/last/pallas_call | solution.py:227
  200.4 5.1 %last.7 = (f32[64,32,512]{2,1,0:T(8,128)}, bf16[64,32,512]{2,1,0:T(8,128)(2,1)}) custom-call(s32[2]{0:T(128)} %pad_add_fusion.at, bf16[64,32,512]{2,1,0:T(8,128)(2,1)} %s_ref.11, f32[64,32,512]{2,1,0:T(8,128)} %xyterms.1.part_ref, bf16[64,32,512]{2,1,0:T(8,128)(2,1)} %drift_ref.10, ...), custom_call_target="tpu_custom_call", output_to_operand_aliasing={{0}: (7, {}), {1}: (8, {})} | custom-call | tf_op jit(solution)/shard_map/last/pallas_call | solution.py:227
  (44 shorter events, 1.8 us)
Async XLA Ops:
  6.6 13.3 %copy-start.3 = (bf16[64,32,128]{2,1,0:T(8,128)(2,1)S(1)}, bf16[64,32,128]{2,1,0:T(8,128)(2,1)}, u32[]{:S(2)}) copy-start(bf16[64,32,128]{2,1,0:T(8,128)(2,1)} %get-tuple-element.29.refs_1_) | copy-start | bytes 1572868
  6.6 46.1 %copy-start.14 = (f32[512]{0:T(512)S(1)}, f32[512]{0:T(512)}, u32[]{:S(2)}) copy-start(f32[512]{0:T(512)} %param.22) | copy-start | bytes 6148
  6.6 56.6 %all-to-all-start = ((bf16[8,64,16,128]{3,2,1,0:T(8,128)(2,1)}), bf16[8,64,16,128]{3,2,1,0:T(8,128)(2,1)S(1)}, u32[]{:S(2)}, u32[]{:S(2)}) async-start(bf16[8,64,16,128]{3,2,1,0:T(8,128)(2,1)} %get-tuple-element.28), calls=%async_computation | async-start | bytes 4194304 | tf_op jit(solution)/shard_map/all_to_all | solution.py:280
  14.2 15.3 %collective-permute-start.1 = (bf16[64,32,128]{2,1,0:T(8,128)(2,1)}, bf16[64,32,128]{2,1,0:T(8,128)(2,1)S(1)}, u32[]{:S(2)}, u32[]{:S(2)}) collective-permute-start(bf16[64,32,128]{2,1,0:T(8,128)(2,1)} %get-tuple-element.30), channel_id=1, source_target_pairs={{0,4},{1,5},{2,6},{3,7},{4,8},{5,9},{6,10},{7,11},{8,12},{9,13},{1... | collective-permute-start | bytes 1572872 | tf_op jit(solution)/shard_map/ppermute | solution.py:251
  15.8 25.9 %collective-permute-start.2 = (bf16[64,32,128]{2,1,0:T(8,128)(2,1)}, bf16[64,32,128]{2,1,0:T(8,128)(2,1)}, u32[]{:S(2)}, u32[]{:S(2)}) collective-permute-start(bf16[64,32,128]{2,1,0:T(8,128)(2,1)} %get-tuple-element.31), channel_id=1, source_target_pairs={{0,8},{1,9},{2,10},{3,11},{4,12},{5,13},{6,14},{7,15},{8,0},{9,1},... | collective-permute-start | bytes 1572872 | tf_op jit(solution)/shard_map/ppermute | solution.py:251
  19.1 22.9 %collective-permute-start.3 = (bf16[64,32,128]{2,1,0:T(8,128)(2,1)}, bf16[64,32,128]{2,1,0:T(8,128)(2,1)}, u32[]{:S(2)}, u32[]{:S(2)}) collective-permute-start(bf16[64,32,128]{2,1,0:T(8,128)(2,1)} %get-tuple-element.32), channel_id=1, source_target_pairs={{0,12},{1,13},{2,14},{3,15},{4,0},{5,1},{6,2},{7,3},{8,4},{9,5},{1... | collective-permute-start | bytes 1572872 | tf_op jit(solution)/shard_map/ppermute | solution.py:251
  19.9 24.3 %collective-permute-start.7 = (bf16[64,32,128]{2,1,0:T(8,128)(2,1)S(1)}, bf16[64,32,128]{2,1,0:T(8,128)(2,1)S(1)}, u32[]{:S(2)}, u32[]{:S(2)}) collective-permute-start(bf16[64,32,128]{2,1,0:T(8,128)(2,1)S(1)} %copy-done.3), channel_id=1, source_target_pairs={{0,1},{1,0},{2,3},{3,2},{4,5},{5,4},{6,7},{7,6},{8,9},{9,8},{10,11... | collective-permute-start | bytes 1572872 | tf_op jit(solution)/shard_map/ppermute | solution.py:255
  21.7 26.9 %collective-permute-start = (bf16[64,32,128]{2,1,0:T(8,128)(2,1)S(1)}, bf16[64,32,128]{2,1,0:T(8,128)(2,1)S(1)}, u32[]{:S(2)}, u32[]{:S(2)}) collective-permute-start(bf16[64,32,128]{2,1,0:T(8,128)(2,1)S(1)} %copy-done.3), channel_id=1, source_target_pairs={{0,2},{1,3},{2,0},{3,1},{4,6},{5,7},{6,4},{7,5},{8,10},{9,11},{10,... | collective-permute-start | bytes 1572872 | tf_op jit(solution)/shard_map/ppermute | solution.py:255
  29.5 31.5 %copy-start.4 = (bf16[64,32,128]{2,1,0:T(8,128)(2,1)}, bf16[64,32,128]{2,1,0:T(8,128)(2,1)S(1)}, u32[]{:S(2)}) copy-start(bf16[64,32,128]{2,1,0:T(8,128)(2,1)S(1)} %collective-permute-done.1.refs_5_) | copy-start | bytes 1572868
  29.5 21.7 %collective-permute-start.8 = (bf16[64,32,128]{2,1,0:T(8,128)(2,1)S(1)}, bf16[64,32,128]{2,1,0:T(8,128)(2,1)S(1)}, u32[]{:S(2)}, u32[]{:S(2)}) collective-permute-start(bf16[64,32,128]{2,1,0:T(8,128)(2,1)S(1)} %collective-permute-done.1.refs_5_), channel_id=1, source_target_pairs={{0,1},{1,0},{2,3},{3,2},{4,5},{5,4},{6,7},{7,6},{8,9},{9,8},{10,11... | collective-permute-start | bytes 1572872 | tf_op jit(solution)/shard_map/ppermute | solution.py:255
  41.7 41.7 %collective-permute-start.4 = (bf16[64,32,128]{2,1,0:T(8,128)(2,1)S(1)}, bf16[64,32,128]{2,1,0:T(8,128)(2,1)}, u32[]{:S(2)}, u32[]{:S(2)}) collective-permute-start(bf16[64,32,128]{2,1,0:T(8,128)(2,1)S(1)} %collective-permute-done.1.refs_5_), channel_id=1, source_target_pairs={{0,2},{1,3},{2,0},{3,1},{4,6},{5,7},{6,4},{7,5},{8,10},{9,11},{10,... | collective-permute-start | bytes 1572872 | tf_op jit(solution)/shard_map/ppermute | solution.py:255
  42.0 41.4 %collective-permute-start.9 = (bf16[64,32,128]{2,1,0:T(8,128)(2,1)}, bf16[64,32,128]{2,1,0:T(8,128)(2,1)}, u32[]{:S(2)}, u32[]{:S(2)}) collective-permute-start(bf16[64,32,128]{2,1,0:T(8,128)(2,1)} %collective-permute-done.2.refs_9_), channel_id=1, source_target_pairs={{0,1},{1,0},{2,3},{3,2},{4,5},{5,4},{6,7},{7,6},{8,9},{9,8},{10,11... | collective-permute-start | bytes 1572872 | tf_op jit(solution)/shard_map/ppermute | solution.py:255
  44.2 7.1 %copy-start.5 = (bf16[64,32,128]{2,1,0:T(8,128)(2,1)}, bf16[64,32,128]{2,1,0:T(8,128)(2,1)S(1)}, u32[]{:S(2)}) copy-start(bf16[64,32,128]{2,1,0:T(8,128)(2,1)S(1)} %collective-permute-done.7.refs_2_) | copy-start | bytes 1572868
  44.2 39.3 %collective-permute-start.5 = (bf16[64,32,128]{2,1,0:T(8,128)(2,1)}, bf16[64,32,128]{2,1,0:T(8,128)(2,1)}, u32[]{:S(2)}, u32[]{:S(2)}) collective-permute-start(bf16[64,32,128]{2,1,0:T(8,128)(2,1)} %collective-permute-done.2.refs_9_), channel_id=1, source_target_pairs={{0,2},{1,3},{2,0},{3,1},{4,6},{5,7},{6,4},{7,5},{8,10},{9,11},{10,... | collective-permute-start | bytes 1572872 | tf_op jit(solution)/shard_map/ppermute | solution.py:255
  48.5 4.1 %copy-start.6 = (bf16[64,32,128]{2,1,0:T(8,128)(2,1)}, bf16[64,32,128]{2,1,0:T(8,128)(2,1)S(1)}, u32[]{:S(2)}) copy-start(bf16[64,32,128]{2,1,0:T(8,128)(2,1)S(1)} %collective-permute-done.refs_3_) | copy-start | bytes 1572868
  48.5 34.9 %collective-permute-start.10 = (bf16[64,32,128]{2,1,0:T(8,128)(2,1)}, bf16[64,32,128]{2,1,0:T(8,128)(2,1)S(1)}, u32[]{:S(2)}, u32[]{:S(2)}) collective-permute-start(bf16[64,32,128]{2,1,0:T(8,128)(2,1)} %collective-permute-done.3.refs_13_), channel_id=1, source_target_pairs={{0,1},{1,0},{2,3},{3,2},{4,5},{5,4},{6,7},{7,6},{8,9},{9,8},{10,11... | collective-permute-start | bytes 1572872 | tf_op jit(solution)/shard_map/ppermute | solution.py:255
  51.2 1.4 copy-start.8
  51.3 32.2 %collective-permute-start.6 = (bf16[64,32,128]{2,1,0:T(8,128)(2,1)}, bf16[64,32,128]{2,1,0:T(8,128)(2,1)}, u32[]{:S(2)}, u32[]{:S(2)}) collective-permute-start(bf16[64,32,128]{2,1,0:T(8,128)(2,1)} %collective-permute-done.3.refs_13_), channel_id=1, source_target_pairs={{0,2},{1,3},{2,0},{3,1},{4,6},{5,7},{6,4},{7,5},{8,10},{9,11},{10,... | collective-permute-start | bytes 1572872 | tf_op jit(solution)/shard_map/ppermute | solution.py:255
  63.2 1.3 copy-start
  83.4 7.9 %copy-start.7 = (bf16[64,32,128]{2,1,0:T(8,128)(2,1)S(1)}, bf16[64,32,128]{2,1,0:T(8,128)(2,1)}, u32[]{:S(2)}) copy-start(bf16[64,32,128]{2,1,0:T(8,128)(2,1)} %copy-done.6) | copy-start | bytes 1572868
  83.5 0.8 copy-start.9
  84.3 81.9 %all-to-all-start.1 = ((f16[8,2064,128]{2,1,0:T(8,128)(2,1)}), f16[8,2064,128]{2,1,0:T(8,128)(2,1)}, u32[]{:S(2)}, u32[]{:S(2)}) async-start(f16[8,2064,128]{2,1,0:T(8,128)(2,1)} %convert_element_type.24), calls=%async_computation.1 | async-start | bytes 8454144 | tf_op jit(solution)/shard_map/all_to_all | solution.py:289
  91.3 2.2 %collective-permute-start.11 = (bf16[64,32,128]{2,1,0:T(8,128)(2,1)S(1)}, bf16[64,32,128]{2,1,0:T(8,128)(2,1)S(1)}, u32[]{:S(2)}, u32[]{:S(2)}) collective-permute-start(bf16[64,32,128]{2,1,0:T(8,128)(2,1)S(1)} %copy-done.7), channel_id=1, source_target_pairs={{0,1},{1,0},{2,3},{3,2},{4,5},{5,4},{6,7},{7,6},{8,9},{9,8},{10,11... | collective-permute-start | bytes 1572872 | tf_op jit(solution)/shard_map/ppermute | solution.py:255
  92.0 2.5 %collective-permute-start.12 = (bf16[64,32,128]{2,1,0:T(8,128)(2,1)}, bf16[64,32,128]{2,1,0:T(8,128)(2,1)S(1)}, u32[]{:S(2)}, u32[]{:S(2)}) collective-permute-start(bf16[64,32,128]{2,1,0:T(8,128)(2,1)} %collective-permute-done.4.refs_7_), channel_id=1, source_target_pairs={{0,1},{1,0},{2,3},{3,2},{4,5},{5,4},{6,7},{7,6},{8,9},{9,8},{10,11... | collective-permute-start | bytes 1572872 | tf_op jit(solution)/shard_map/ppermute | solution.py:255
  92.1 3.2 %collective-permute-start.13 = (bf16[64,32,128]{2,1,0:T(8,128)(2,1)}, bf16[64,32,128]{2,1,0:T(8,128)(2,1)S(1)}, u32[]{:S(2)}, u32[]{:S(2)}) collective-permute-start(bf16[64,32,128]{2,1,0:T(8,128)(2,1)} %collective-permute-done.5.refs_11_), channel_id=1, source_target_pairs={{0,1},{1,0},{2,3},{3,2},{4,5},{5,4},{6,7},{7,6},{8,9},{9,8},{10,11... | collective-permute-start | bytes 1572872 | tf_op jit(solution)/shard_map/ppermute | solution.py:255
  92.5 3.5 %collective-permute-start.14 = (bf16[64,32,128]{2,1,0:T(8,128)(2,1)}, bf16[64,32,128]{2,1,0:T(8,128)(2,1)S(1)}, u32[]{:S(2)}, u32[]{:S(2)}) collective-permute-start(bf16[64,32,128]{2,1,0:T(8,128)(2,1)} %collective-permute-done.6.refs_15_), channel_id=1, source_target_pairs={{0,1},{1,0},{2,3},{3,2},{4,5},{5,4},{6,7},{7,6},{8,9},{9,8},{10,11... | collective-permute-start | bytes 1572872 | tf_op jit(solution)/shard_map/ppermute | solution.py:255
  93.5 2.5 %copy-start.10 = (bf16[64,32,128]{2,1,0:T(8,128)(2,1)}, bf16[64,32,128]{2,1,0:T(8,128)(2,1)S(1)}, u32[]{:S(2)}) copy-start(bf16[64,32,128]{2,1,0:T(8,128)(2,1)S(1)} %collective-permute-done.11.refs_4_) | copy-start | bytes 1572868
  94.5 1.5 copy-start.11
  95.2 0.8 copy-start.12
  96.0 0.8 copy-start.13
  108.0 2.3 %copy-start.2 = (f32[8,528,128]{2,1,0:T(8,128)S(1)}, f32[8,528,128]{2,1,0:T(8,128)}, u32[]{:S(2)}) copy-start(f32[8,528,128]{2,1,0:T(8,128)} %get-tuple-element.46) | copy-start | bytes 6488068
  109.9 5.2 %copy-start.1 = (f32[8,528,128]{2,1,0:T(8,128)S(1)}, f32[8,528,128]{2,1,0:T(8,128)}, u32[]{:S(2)}) copy-start(f32[8,528,128]{2,1,0:T(8,128)} %get-tuple-element.44) | copy-start | bytes 6488068
  111.4 28.0 %collective-permute-start.17 = (f16[8,528,128]{2,1,0:T(8,128)(2,1)}, f16[8,528,128]{2,1,0:T(8,128)(2,1)}, u32[]{:S(2)}, u32[]{:S(2)}) collective-permute-start(f16[8,528,128]{2,1,0:T(8,128)(2,1)} %convert_element_type.30), channel_id=1, source_target_pairs={{0,4},{1,5},{2,6},{3,7},{4,8},{5,9},{6,10},{7,11},{8,12},{9,13},{1... | collective-permute-start | bytes 3244040 | tf_op jit(solution)/shard_map/ppermute | solution.py:251
  113.0 29.1 %collective-permute-start.16 = (f16[8,528,128]{2,1,0:T(8,128)(2,1)S(1)}, f16[8,528,128]{2,1,0:T(8,128)(2,1)S(1)}, u32[]{:S(2)}, u32[]{:S(2)}) collective-permute-start(f16[8,528,128]{2,1,0:T(8,128)(2,1)S(1)} %convert_element_type.28), channel_id=1, source_target_pairs={{0,12},{1,13},{2,14},{3,15},{4,0},{5,1},{6,2},{7,3},{8,4},{9,5},{1... | collective-permute-start | bytes 3244040 | tf_op jit(solution)/shard_map/ppermute | solution.py:251
  115.3 48.1 %collective-permute-start.15 = (f16[8,528,128]{2,1,0:T(8,128)(2,1)S(1)}, f16[8,528,128]{2,1,0:T(8,128)(2,1)}, u32[]{:S(2)}, u32[]{:S(2)}) collective-permute-start(f16[8,528,128]{2,1,0:T(8,128)(2,1)S(1)} %convert_element_type.26), channel_id=1, source_target_pairs={{0,8},{1,9},{2,10},{3,11},{4,12},{5,13},{6,14},{7,15},{8,0},{9,1},... | collective-permute-start | bytes 3244040 | tf_op jit(solution)/shard_map/ppermute | solution.py:251

commit v2 on v1

v2 whole, which is shorter than its diff:
```python
import jax
import jax.numpy as jnp
from jax import lax
from jax.experimental import pallas as pl
from jax.experimental.pallas import tpu as pltpu
from jax.sharding import PartitionSpec as P

F32 = jnp.float32
BF16 = jnp.bfloat16
F16 = jnp.float16

NJ, NK, NI = 64, 32, 512
YB = 16
PIECE = YB * 64
HALVES = 2
HJ = NJ // HALVES
CHUNKS = 1
CJ = NJ // CHUNKS


def params(mib):
    return pltpu.CompilerParams(vmem_limit_bytes=mib * 1024 * 1024)


def pow_of(values):
    top = jnp.max(jnp.abs(values), axis=0, keepdims=True)
    top = jnp.max(top, axis=1, keepdims=True)
    return jnp.floor(jnp.log2(jnp.maximum(top, 1e-30)))


def cut_kernel(at, s_ref, *outs):
    for s, out in enumerate(outs):
        off = pl.multiple_of(lax.rem(at[0] + s, 4) * 128, 128)
        out[...] = s_ref[:, :, pl.ds(off, 128)]


def cut(at, scalar):
    jb = 16
    return pl.pallas_call(
        cut_kernel,
        grid_spec=pltpu.PrefetchScalarGridSpec(
            num_scalar_prefetch=1,
            grid=(NJ // jb,),
            in_specs=[pl.BlockSpec((jb, NK, NI), lambda j, at: (j, 0, 0))],
            out_specs=[pl.BlockSpec((jb, NK, 128), lambda j, at: (j, 0, 0))] * 4,
        ),
        out_shape=[jax.ShapeDtypeStruct((NJ, NK, 128), BF16)] * 4,
        compiler_params=params(8),
        name="cut",
    )(at, scalar)


def pack_kernel(s_ref, after_ref, row_ref):
    for c in range(4):
        chunk = s_ref[:, :, 128 * c : 128 * (c + 1)]
        top, bot = chunk[:, :16, :], chunk[:, 16:, :]
        row_ref[2 * c] = jnp.concatenate([top[:, :, :64], bot[:, :, :64]], axis=-1)
        row_ref[2 * c + 1] = jnp.concatenate([bot[:, :, 64:], top[:, :, 64:]], axis=-1)


def merge_kernel(r1, r2, r3, *outs):
    for h, out in enumerate(outs):
        for s, r in enumerate((r1, r2, r3)):
            out[s] = r[CJ * h : CJ * (h + 1)]


def merge(parts):
    whole = pl.BlockSpec(memory_space=pltpu.VMEM)
    return pl.pallas_call(
        merge_kernel,
        in_specs=[whole] * 3,
        out_specs=[whole] * CHUNKS,
        out_shape=[jax.ShapeDtypeStruct((3, CJ, NK, 128), BF16)] * CHUNKS,
        compiler_params=params(8),
        name="merge",
    )(*parts)


def pack(scalar, after):
    jb = 16
    return pl.pallas_call(
        pack_kernel,
        grid=(NJ // jb,),
        in_specs=[
            pl.BlockSpec((jb, NK, NI), lambda j: (j, 0, 0)),
            pl.BlockSpec(memory_space=pl.ANY),
        ],
        out_specs=pl.BlockSpec((8, jb, 16, 128), lambda j: (0, j, 0, 0)),
        out_shape=jax.ShapeDtypeStruct((8, NJ, 16, 128), BF16),
        compiler_params=params(8),
        name="pack",
    )(scalar, after)


def operator_kernel(at, first_ref, second_ref, out_ref):
    zc, pair = at[0], at[1]
    rows = []
    for t in range(4):
        start = pl.multiple_of(128 * lax.rem(zc + t, 4) + 32 * pair, 32)
        rows += [first_ref[pl.ds(start, 32), :], second_ref[pl.ds(start, 32), :]]
    rows = jnp.concatenate(rows, axis=0)
    at_k = lax.broadcasted_iota(jnp.int32, (512, 512), 0)
    m = lax.broadcasted_iota(jnp.int32, (512, 512), 1)
    s, flip, low = m // 128, (m // 32) % 4, m % 32
    block = 128 * lax.rem(zc + 4 - s, 4) + 32 * jnp.bitwise_xor(pair, flip)
    pick = jnp.where(at_k == block + low, 1.0, 0.0).astype(BF16)
    out_ref[...] = jnp.dot(rows, pick, preferred_element_type=F32).astype(BF16)


def operator_rows(at, first, second):
    whole = pl.BlockSpec(memory_space=pltpu.VMEM)
    return pl.pallas_call(
        operator_kernel,
        in_specs=[pl.BlockSpec(memory_space=pltpu.SMEM), whole, whole],
        out_specs=whole,
        out_shape=jax.ShapeDtypeStruct((256, 512), BF16),
        compiler_params=params(8),
        name="operator",
    )(at, first, second)


def y_kernel(odd_ref, s_ref, drift_ref, first_ref, second_ref, metric_ref, out_ref, s32, p32, c32):
    @pl.when(pl.program_id(0) == 0)
    def _():
        s32[...] = s_ref[...].astype(F32).reshape(8 * NJ * 16, 128)
        metric = metric_ref[...]
        metric2 = metric * metric
        ops = jnp.concatenate([first_ref[...], second_ref[...]], axis=0)
        eye = lax.broadcasted_iota(jnp.int32, (512, 512), 0) == lax.broadcasted_iota(jnp.int32, (512, 512), 1)
        eye = jnp.where(eye, 1.0, 0.0).astype(BF16)
        low = 16 * odd_ref[0]
        for z in range(0, 16, 2):
            cols = jnp.concatenate(
                [s32[pl.ds(z + h, 512, stride=16), :].astype(BF16) for h in range(2)], axis=1
            )
            wind = jnp.concatenate(
                [drift_ref[z + h + at] for h in range(2) for at in (low, 16 - low)], axis=0
            )
            both = jnp.dot(ops, cols, preferred_element_type=F32)
            wind = lax.dot_general(eye, wind, (((1,), (1,)), ((), ())), preferred_element_type=F32)
            p, curv = (wind * metric) * both[:512], both[512:] * metric2
            for h in range(2):
                p32[pl.ds(z + h, 512, stride=16), :] = p[:, 128 * h : 128 * (h + 1)]
                c32[pl.ds(z + h, 512, stride=16), :] = curv[:, 128 * h : 128 * (h + 1)]

    rows = pl.ds(pl.multiple_of(pl.program_id(0) * 1024, 1024), 1024)
    p, c = p32[rows, :], c32[rows, :]
    pe, ce = pow_of(p), pow_of(c)
    out_ref[0, 0:1024, :] = p * jnp.exp2(13.0 - pe)
    out_ref[0, 1024:2048, :] = c * jnp.exp2(13.0 - ce)
    out_ref[0, 2048:2056, :] = jnp.broadcast_to(pe, (8, 128))
    out_ref[0, 2056:2064, :] = jnp.broadcast_to(ce, (8, 128))


def y_terms(odd, s, drift, first, second, metric):
    op = pl.BlockSpec((512, 512), lambda d: (0, 0))
    scratch = pltpu.VMEM((8 * NJ * 16, 128), F32)
    return pl.pallas_call(
        y_kernel,
        grid=(8,),
        in_specs=[
            pl.BlockSpec(memory_space=pltpu.SMEM),
            pl.BlockSpec((8, NJ, 16, 128), lambda d: (0, 0, 0, 0)),
            pl.BlockSpec((NK, 64, 512), lambda d: (0, 0, 0)),
            op,
            op,
            pl.BlockSpec((512, 1), lambda d: (0, 0)),
        ],
        out_specs=pl.BlockSpec((1, 2064, 128), lambda d: (d, 0, 0)),
        out_shape=jax.ShapeDtypeStruct((8, 2064, 128), F32),
        scratch_shapes=[scratch, scratch, scratch],
        compiler_params=params(40),
        name="yterms",
    )(odd, s, drift, first, second, metric)


def z_kernel(*refs):
    a_ref, firsts, rests, outs = refs[0], refs[1:5], refs[5:9], refs[9:13]
    rows = a_ref[...]
    results = []
    for y in range(0, YB, 2):
        cols = []
        for h in range(2):
            parts = [f[y + h] for f in firsts] + [m[s, y + h] for s in range(3) for m in rests]
            cols.append(jnp.concatenate(parts, axis=0))
        results.append(jnp.dot(rows, jnp.concatenate(cols, axis=1), preferred_element_type=F32))
    top = jnp.abs(results[0])
    for r in results[1:]:
        top = jnp.maximum(top, jnp.abs(r))
    e = pow_of(top)
    scale = jnp.exp2(13.0 - e)
    for y in range(YB):
        value = results[y // 2][:, 128 * (y % 2) : 128 * (y % 2 + 1)] * scale
        for t in range(4):
            outs[t][0, 64 * y : 64 * (y + 1), :] = value[64 * t : 64 * (t + 1), :]
    for t in range(4):
        outs[t][0, PIECE : PIECE + 16, :] = jnp.broadcast_to(e, (16, 128))


def z_terms(h, rows, firsts, rests):
    out = jax.ShapeDtypeStruct((HJ // YB, PIECE + 16, 128), F32)
    return pl.pallas_call(
        z_kernel,
        grid=(HJ // YB,),
        in_specs=[pl.BlockSpec((256, 512), lambda j: (0, 0))]
        + [pl.BlockSpec((YB, NK, 128), lambda j: (HJ // YB * h + j, 0, 0))] * 4
        + [pl.BlockSpec((3, YB, NK, 128), lambda j: (0, HJ // YB * h + j, 0, 0))] * 4,
        out_specs=[pl.BlockSpec((1, PIECE + 16, 128), lambda j: (j, 0, 0))] * 4,
        out_shape=[out] * 4,
        compiler_params=params(16),
        name="zterms",
    )(rows, *firsts, *rests)


def x_kernel(s_ref, reg_ref, drift_ref, diff_ref, first_ref, second_ref, metric_ref, out_ref):
    jb = s_ref.shape[0]
    flat = s_ref[...].reshape(jb * NK, NI)
    last = (((1,), (1,)), ((), ()))
    grad = lax.dot_general(flat, first_ref[...], last, preferred_element_type=F32)
    curv = lax.dot_general(flat, second_ref[...], last, preferred_element_type=F32)
    metric = metric_ref[...]
    diff = diff_ref[...].astype(F32).reshape(jb * NK, NI)
    total = (drift_ref[...].astype(F32).reshape(jb * NK, NI) * metric) * grad
    total = total + (diff * (metric * metric)) * curv
    out_ref[...] = (-5.0 / 9.0) * reg_ref[...] + 0.5 * total.reshape(jb, NK, NI)


def x_terms(scalar, reg, drift, diff, first, second, metric):
    jb = 8
    field = pl.BlockSpec((jb, NK, NI), lambda j: (j, 0, 0))
    op = pl.BlockSpec((NI, NI), lambda j: (0, 0))
    return pl.pallas_call(
        x_kernel,
        grid=(NJ // jb,),
        in_specs=[field] * 4 + [op, op, pl.BlockSpec((1, NI), lambda j: (0, 0))],
        out_specs=field,
        out_shape=jax.ShapeDtypeStruct((NJ, NK, NI), F32),
        compiler_params=params(20),
        name="xterms",
    )(scalar, reg, drift, diff, first, second, metric)


def last_kernel(at, s_ref, part_ref, drift_ref, diff_ref, metric_ref, p0, p1, p2, p3, *refs):
    reg_ref, out_ref = refs[-2:]
    metric = metric_ref[...][None]
    for t, piece in enumerate((p0, p1, p2, p3)):
        lanes = pl.ds(pl.multiple_of(lax.rem(at[0] + 4 - t, 4) * 128, 128), 128)
        scale = jnp.exp2(piece[0, PIECE : PIECE + 1, :] - 13.0)
        value = (piece[0, 0:PIECE, :] * scale).reshape(YB, 2, NK, 128)
        term = (drift_ref[:, :, lanes].astype(F32) * metric) * value[:, 0]
        term = term + (diff_ref[:, :, lanes].astype(F32) * (metric * metric)) * value[:, 1]
        reg = part_ref[:, :, lanes] + 0.5 * term
        reg_ref[:, :, lanes] = reg
        out_ref[:, :, lanes] = (s_ref[:, :, lanes].astype(F32) + (15.0 / 16.0) * reg).astype(BF16)


def last_terms(at, h, scalar, part, drift, diff, metric, pieces, done):
    n = HJ // YB
    field = pl.BlockSpec((YB, NK, NI), lambda j, at: (n * h + j, 0, 0))
    return pl.pallas_call(
        last_kernel,
        grid_spec=pltpu.PrefetchScalarGridSpec(
            num_scalar_prefetch=1,
            grid=(n,),
            in_specs=[field] * 4
            + [pl.BlockSpec((NK, 128), lambda j, at: (0, 0))]
            + [pl.BlockSpec((1, PIECE + 16, 128), lambda j, at: (j, 0, 0))] * 4
            + [pl.BlockSpec(memory_space=pl.ANY)] * len(done),
            out_specs=[field, field],
        ),
        out_shape=[
            jax.ShapeDtypeStruct((NJ, NK, NI), F32),
            jax.ShapeDtypeStruct((NJ, NK, NI), BF16),
        ],
        input_output_aliases={10 + i: i for i in range(len(done))},
        compiler_params=params(30),
        name="last",
    )(at, scalar, part, drift, diff, metric, *pieces, *done)


def add_y_kernel(part_ref, diff_ref, p_ref, c_ref, e_ref, out_ref):
    jb = part_ref.shape[0]

    low = lax.broadcasted_iota(jnp.int32, (jb, 16, 128), 2) < 64

    def native(ref, at):
        tops, bots = [], []
        for c in range(4):
            even, odd = (
                (ref[d] * jnp.exp2(e_ref[d, at : at + 1, :] - 13.0)).reshape(jb, 16, 128)
                for d in (2 * c, 2 * c + 1)
            )
            tops.append(jnp.where(low, even, odd))
            bots.append(pltpu.roll(jnp.where(low, odd, even), 64, 2))
        return jnp.concatenate(
            [jnp.concatenate(tops, axis=-1), jnp.concatenate(bots, axis=-1)], axis=1
        )

    term = native(p_ref, 0) + diff_ref[...].astype(F32) * native(c_ref, 8)
    out_ref[...] = part_ref[...] + 0.5 * term


def add_y(part, diff, y_back):
    jb = 8
    n = NJ // jb
    field = pl.BlockSpec((jb, NK, NI), lambda j: (j, 0, 0))
    return pl.pallas_call(
        add_y_kernel,
        grid=(n,),
        in_specs=[
            field,
            field,
            pl.BlockSpec((8, jb * 16, 128), lambda j: (0, j, 0)),
            pl.BlockSpec((8, jb * 16, 128), lambda j: (0, n + j, 0)),
            pl.BlockSpec((8, 16, 128), lambda j: (0, 128, 0)),
        ],
        out_specs=field,
        out_shape=jax.ShapeDtypeStruct((NJ, NK, NI), F32),
        compiler_params=params(20),
        name="addy",
    )(part, diff, y_back, y_back, y_back)


def ring(x, shift):
    return lax.ppermute(x, "col", [(c, (c + 4 * shift) % 16) for c in range(16)])


def flip(x, bits):
    return lax.ppermute(x, "col", [(c, c ^ bits) for c in range(16)])


def on_device(
    scalar,
    register_in,
    drift_x,
    drift_y,
    drift_z,
    diffusivity,
    metric_x,
    metric_y,
    metric_z,
    first_x,
    second_x,
    first_y,
    second_y,
    first_z,
    second_z,
):
    col = lax.axis_index("col")
    at = jnp.stack([col // 4, col % 4]).astype(jnp.int32)
    own = lax.dynamic_slice(metric_z, (NK * col,), (NK,))
    own = jnp.broadcast_to(own[:, None], (NK, 128))
    mine = cut(at, scalar)
    beside, across = flip(mine[0], 1), flip(mine[0], 2)
    scalar_y = lax.all_to_all(pack(scalar, beside), "row", 0, 0, tiled=False)
    rows = operator_rows(at, first_z, second_z)
    *rest, across, rows = lax.optimization_barrier(
        [ring(mine[s], s) for s in range(1, 4)] + [across, rows]
    )
    rest = merge(rest)[0]
    far = flip(rest, 2)
    scalar_y, rest = lax.optimization_barrier((scalar_y, rest))
    odd = (lax.axis_index("row") % 2).astype(jnp.int32)[None]
    wind = jnp.transpose(drift_y, (1, 2, 0))
    y_out = y_terms(odd, scalar_y, wind, first_y, second_y, metric_y[:, None]).astype(F16)
    rests = [rest, flip(rest, 1)]
    firsts = [mine[0], beside, across, flip(across, 1)]
    y_out, rests[1], firsts[3] = lax.optimization_barrier((y_out, rests[1], firsts[3]))
    y_back = lax.all_to_all(y_out, "row", 0, 0, tiled=False)
    rests += [far, flip(far, 1)]
    part = x_terms(scalar, register_in, drift_x, diffusivity, first_x, second_x, metric_x[None, :])
    z_back = []
    for h in range(HALVES):
        z_out = z_terms(h, rows, firsts, rests)
        z_back.append([z_out[0]] + [ring(z_out[t].astype(F16), t) for t in range(1, 4)])
    part = add_y(part, diffusivity, y_back.astype(F32))
    done = ()
    for h in range(HALVES):
        part, z_half, done = lax.optimization_barrier((part, z_back[h], done))
        z_half = [z.astype(F32) for z in z_half]
        done = last_terms(at, h, scalar, part, drift_z, diffusivity, own, z_half, done)
    return tuple(done)


def solution(mesh):
    in_specs = (
        P("row", "col", None),
        P("row", "col", None),
        P("row", "col", None),
        P(None, "col", "row"),
        P("row", "col", None),
        P("row", "col", None),
        P(),
        P(),
        P(),
        P(),
        P(),
        P(),
        P(),
        P(),
        P(),
    )
    out_specs = (P("row", "col", None), P("row", "col", None))
    return jax.shard_map(
        on_device, mesh=mesh, in_specs=in_specs, out_specs=out_specs, check_vma=False
    )
```

time: 208 us -> 159 us (0.76)
  Pallas kernels: 64.2 us -> 32.3 us
  waiting for transfers between devices: 66 us -> 53.8 us
  local copies, waits for them, and re-layouts: 13.1 us -> 20.2 us
  other arithmetic: 22.9 us -> 15.9 us
  starting transfers between devices: 38.6 us -> 33.7 us
    ppermute x6 -> x9, waiting for transfers between devices: 59.4 us -> 24.3 us  [ring(): lax.ppermute(x, 'col', [(c, (c + 4 * shift) % 16) for c in range(16)])]
    ppermute x12 -> x6, waiting for transfers between devices: 6.61 us -> 22.6 us  [flip(): return lax.ppermute(x, 'col', [(c, c ^ bits) for c in range(16)])]
    pallas_call x4 -> x8, Pallas kernels: 41.6 us -> 25.7 us  [the longest x1 9.02 us: y_terms(): pl.pallas_call(y_kernel, grid=(8,), in_specs=[pl.BlockSpec(memory_space=p...]
    pallas_call x4 -> x2, Pallas kernels: 20.3 us -> 5.73 us  [last_terms(): pl.pallas_call(last_kernel, grid_spec=pltpu.PrefetchScalarGridSpec(num_sc...]
    unnamed x31 -> x58, local copies, waits for them, and re-layouts: 10.7 us -> 18.6 us
    convert_element_type x5 -> x8, other arithmetic: 19.1 us -> 11.4 us  [the longest x6 5.89 us: on_device(): z_half = [z.astype(F32) for z in z_half]]
    all_to_all x2, waiting for transfers between devices: 0.01 us -> 6.81 us  [the longest x1 6.81 us: on_device(): y_back = lax.all_to_all(y_out, 'row', 0, 0, tiled=False)]
    ppermute x12 -> x6, starting transfers between devices: 12.9 us -> 6.44 us  [flip(): return lax.ppermute(x, 'col', [(c, c ^ bits) for c in range(16)])]
  transfers between devices with their start and end apart: 20 -> 17, of which waited for: 9 -> 10; matrix products, arithmetic and copies ran while one was open for 12% -> 9% of each run, Pallas kernels for 13% -> 17%
where the time goes in v2:
time: 159 us; the launch traced here: 157 us
  waiting for transfers between devices  53.8 us (34%)
  starting transfers between devices  33.7 us (21%)
  Pallas kernels  32.3 us (20%)
  local copies, waits for them, and re-layouts  20.2 us (13%)
  other arithmetic  15.9 us (10%)
    ppermute x9, waiting for transfers between devices, ring(): lax.ppermute(x, 'col', [(c, (c + 4 * shift) % 16) for c in range(16)])  24.3 us
    ppermute x6, waiting for transfers between devices, flip(): return lax.ppermute(x, 'col', [(c, c ^ bits) for c in range(16)])  22.6 us
    unnamed x58, local copies, waits for them, and re-layouts  18.6 us
    ppermute x9, starting transfers between devices, ring(): lax.ppermute(x, 'col', [(c, (c + 4 * shift) % 16) for c in range(16)])  13.7 us
    pallas_call x1, Pallas kernels, y_terms(): pl.pallas_call(y_kernel, grid=(8,), in_specs=[pl.BlockSpec(memory_space=p...  9.02 us
    all_to_all x1, starting transfers between devices, on_device(): scalar_y = lax.all_to_all(pack(scalar, beside), 'row', 0, 0, tiled=False)  6.87 us
    all_to_all x1, waiting for transfers between devices, on_device(): y_back = lax.all_to_all(y_out, 'row', 0, 0, tiled=False)  6.81 us
    all_to_all x1, starting transfers between devices, on_device(): y_back = lax.all_to_all(y_out, 'row', 0, 0, tiled=False)  6.7 us
  transfers between devices with their start and end apart: 17, of which 10 were waited for; matrix products, arithmetic and copies ran while one was open for 9% of the time, Pallas kernels for 17%

profile of v2, /device:TPU:1, one launch (start us, length us, event | category | flops | bytes accessed | tf_op | source)
XLA Modules:
  0.0 156.9 jit_solution(12210159629039739565)
XLA Ops:
  0.7 1.6 %copy-done = bf16[64,32,512]{2,1,0:T(8,128)(2,1)S(1)} copy-done((bf16[64,32,512]{2,1,0:T(8,128)(2,1)S(1)}, bf16[64,32,512]{2,1,0:T(8,128)(2,1)}, u32[]{:S(2)}) %copy-start) | copy-done | bytes 2097176
  2.3 1.0 cut.1
  3.3 1.5 collective-permute-start
  4.8 1.5 collective-permute-done.after_ref.refs_2_
  6.4 2.0 %pack.1 = bf16[8,64,16,128]{3,2,1,0:T(8,128)(2,1)} custom-call(bf16[64,32,512]{2,1,0:T(8,128)(2,1)S(1)} %copy-done, bf16[64,32,128]{2,1,0:T(8,128)(2,1)S(1)} %collective-permute-done.after_ref.refs_2_), custom_call_target="tpu_custom_call" | custom-call | tf_op jit(solution)/shard_map/pack/pallas_call | solution.py:81
  9.2 6.9 %all-to-all-start = ((bf16[8,64,16,128]{3,2,1,0:T(8,128)(2,1)}), bf16[8,64,16,128]{3,2,1,0:T(8,128)(2,1)}, u32[]{:S(2)}, u32[]{:S(2)}) async-start(bf16[8,64,16,128]{3,2,1,0:T(8,128)(2,1)} %pack.1), calls=%async_computation | async-start | bytes 4194304 | tf_op jit(solution)/shard_map/all_to_all | solution.py:355
  16.1 1.6 %collective-permute-start.1 = (bf16[64,32,128]{2,1,0:T(8,128)(2,1)S(1)}, bf16[64,32,128]{2,1,0:T(8,128)(2,1)S(1)}, u32[]{:S(2)}, u32[]{:S(2)}) collective-permute-start(bf16[64,32,128]{2,1,0:T(8,128)(2,1)S(1)} %get-tuple-element.39), channel_id=1, source_target_pairs={{0,4},{1,5},{2,6},{3,7},{4,8},{5,9},{6,10},{7,11},{8,12},{9,13},{1... | collective-permute-start | bytes 1572872 | tf_op jit(solution)/shard_map/ppermute | solution.py:325
  17.7 3.3 %collective-permute-start.2 = (bf16[64,32,128]{2,1,0:T(8,128)(2,1)S(1)}, bf16[64,32,128]{2,1,0:T(8,128)(2,1)S(1)}, u32[]{:S(2)}, u32[]{:S(2)}) collective-permute-start(bf16[64,32,128]{2,1,0:T(8,128)(2,1)S(1)} %get-tuple-element.40), channel_id=1, source_target_pairs={{0,8},{1,9},{2,10},{3,11},{4,12},{5,13},{6,14},{7,15},{8,0},{9,1},... | collective-permute-start | bytes 1572872 | tf_op jit(solution)/shard_map/ppermute | solution.py:325
  23.0 8.7 %collective-permute-done.1.r1 = bf16[64,32,128]{2,1,0:T(8,128)(2,1)S(1)} collective-permute-done((bf16[64,32,128]{2,1,0:T(8,128)(2,1)S(1)}, bf16[64,32,128]{2,1,0:T(8,128)(2,1)S(1)}, u32[]{:S(2)}, u32[]{:S(2)}) %collective-permute-start.1) | collective-permute-done | bytes 524320 | tf_op jit(solution)/shard_map/ppermute | solution.py:325
  31.6 12.1 %collective-permute-done.2.r2 = bf16[64,32,128]{2,1,0:T(8,128)(2,1)S(1)} collective-permute-done((bf16[64,32,128]{2,1,0:T(8,128)(2,1)S(1)}, bf16[64,32,128]{2,1,0:T(8,128)(2,1)S(1)}, u32[]{:S(2)}, u32[]{:S(2)}) %collective-permute-start.2) | collective-permute-done | bytes 524320 | tf_op jit(solution)/shard_map/ppermute | solution.py:325
  43.7 7.2 %collective-permute-done.4.refs_3_ = bf16[64,32,128]{2,1,0:T(8,128)(2,1)} collective-permute-done((bf16[64,32,128]{2,1,0:T(8,128)(2,1)S(1)}, bf16[64,32,128]{2,1,0:T(8,128)(2,1)}, u32[]{:S(2)}, u32[]{:S(2)}) %collective-permute-start.4) | collective-permute-done | bytes 524320 | tf_op jit(solution)/shard_map/ppermute | solution.py:329
  51.0 1.3 collective-permute-start.5
  52.4 1.2 collective-permute-start.7
  54.4 1.6 %copy-done.13 = bf16[512,32,64]{0,2,1:T(8,128)(2,1)S(1)} copy-done((bf16[512,32,64]{0,2,1:T(8,128)(2,1)S(1)}, bf16[512,32,64]{0,2,1:T(8,128)(2,1)}, u32[]{:S(2)}) %copy-start.13) | copy-done | bytes 2097176
  56.0 0.9 copy-done.18
  57.0 1.0 copy-done.21
  58.0 1.0 copy-done.22
  59.0 9.0 %yterms.1 = f32[8,2064,128]{2,1,0:T(8,128)S(1)} custom-call(s32[1]{0:T(128)} %bitcast.3.odd_ref, bf16[8,64,16,128]{3,2,1,0:T(8,128)(2,1)} %all-to-all-done.s_ref, bf16[32,64,512]{2,1,0:T(8,128)(2,1)S(1)} %bitcast.6, bf16[512,512]{1,0:T(8,128)(2,1)S(1)} %copy-done.21, bf16[512,512]{1,0:T(8,128)(2,1)S(1)} %copy-done.22, f32[512,1]{1,0:T(8,128)S(1)} %copy-done.18), custom_call_target="tpu_custom_call" | custom-call | tf_op jit(solution)/shard_map/yterms/pallas_call | solution.py:158
  68.1 2.6 %convert_element_type.42 = f16[8,2064,128]{2,1,0:T(8,128)(2,1)} convert(f32[8,2064,128]{2,1,0:T(8,128)S(1)} %yterms.1) | non-fusion elementwise | flops 2113536 | bytes 12681216 | tf_op jit(solution)/shard_map/convert_element_type | solution.py:365
  70.7 6.7 %all-to-all-start.1 = ((f16[8,2064,128]{2,1,0:T(8,128)(2,1)}), f16[8,2064,128]{2,1,0:T(8,128)(2,1)}, u32[]{:S(2)}, u32[]{:S(2)}) async-start(f16[8,2064,128]{2,1,0:T(8,128)(2,1)} %convert_element_type.42), calls=%async_computation.1 | async-start | bytes 8454144 | tf_op jit(solution)/shard_map/all_to_all | solution.py:369
  77.4 10.7 %collective-permute-done.7.refs_7_ = bf16[3,64,32,128]{3,2,1,0:T(8,128)(2,1)} collective-permute-done((bf16[3,64,32,128]{3,2,1,0:T(8,128)(2,1)S(1)}, bf16[3,64,32,128]{3,2,1,0:T(8,128)(2,1)}, u32[]{:S(2)}, u32[]{:S(2)}) %collective-permute-start.7) | collective-permute-done | bytes 1572896 | tf_op jit(solution)/shard_map/ppermute | solution.py:329
  88.1 2.1 %collective-permute-start.8 = (bf16[3,64,32,128]{3,2,1,0:T(8,128)(2,1)}, bf16[3,64,32,128]{3,2,1,0:T(8,128)(2,1)S(1)}, u32[]{:S(2)}, u32[]{:S(2)}) collective-permute-start(bf16[3,64,32,128]{3,2,1,0:T(8,128)(2,1)} %collective-permute-done.7.refs_7_), channel_id=1, source_target_pairs={{0,1},{1,0},{2,3},{3,2},{4,5},{5,4},{6,7},{7,6},{8,9},{9,8},{10,11... | collective-permute-start | bytes 4718600 | tf_op jit(solution)/shard_map/ppermute | solution.py:329
  90.2 3.2 %collective-permute-done.8.refs_8_ = bf16[3,64,32,128]{3,2,1,0:T(8,128)(2,1)S(1)} collective-permute-done((bf16[3,64,32,128]{3,2,1,0:T(8,128)(2,1)}, bf16[3,64,32,128]{3,2,1,0:T(8,128)(2,1)S(1)}, u32[]{:S(2)}, u32[]{:S(2)}) %collective-permute-start.8) | collective-permute-done | bytes 1572896 | tf_op jit(solution)/shard_map/ppermute | solution.py:329
  93.4 1.0 copy-done.8
  94.5 1.0 copy-done.12
  95.5 3.1 %zterms.2 = (f32[2,1040,128]{2,1,0:T(8,128)S(1)}, f32[2,1040,128]{2,1,0:T(8,128)S(1)}, f32[2,1040,128]{2,1,0:T(8,128)S(1)}, f32[2,1040,128]{2,1,0:T(8,128)S(1)}) custom-call(bf16[256,512]{1,0:T(8,128)(2,1)S(1)} %operator.1.refs_0_, bf16[64,32,128]{2,1,0:T(8,128)(2,1)S(1)} %copy-done.12, bf16[64,32,128]{2,1,0:T(8,128)(2,1)S(1)} %copy-done.8, ...), custom_call_target="tpu_custom_call" | custom-call | tf_op jit(solution)/shard_map/zterms/pallas_call | solution.py:202
  98.7 1.7 %collective-permute-start.9 = (f16[2,1040,128]{2,1,0:T(8,128)(2,1)S(1)}, f16[2,1040,128]{2,1,0:T(8,128)(2,1)S(1)}, u32[]{:S(2)}, u32[]{:S(2)}) collective-permute-start(f16[2,1040,128]{2,1,0:T(8,128)(2,1)S(1)} %convert_element_type.44), channel_id=1, source_target_pairs={{0,4},{1,5},{2,6},{3,7},{4,8},{5,9},{6,10},{7,11},{8,12},{9,13},{1... | collective-permute-start | bytes 1597448 | tf_op jit(solution)/shard_map/ppermute | solution.py:325
  101.3 3.3 %collective-permute-start.10 = (f16[2,1040,128]{2,1,0:T(8,128)(2,1)}, f16[2,1040,128]{2,1,0:T(8,128)(2,1)}, u32[]{:S(2)}, u32[]{:S(2)}) collective-permute-start(f16[2,1040,128]{2,1,0:T(8,128)(2,1)} %convert_element_type.45), channel_id=1, source_target_pairs={{0,8},{1,9},{2,10},{3,11},{4,12},{5,13},{6,14},{7,15},{8,0},{9,1},... | collective-permute-start | bytes 1597448 | tf_op jit(solution)/shard_map/ppermute | solution.py:325
  106.2 3.1 %zterms.3 = (f32[2,1040,128]{2,1,0:T(8,128)S(1)}, f32[2,1040,128]{2,1,0:T(8,128)S(1)}, f32[2,1040,128]{2,1,0:T(8,128)S(1)}, f32[2,1040,128]{2,1,0:T(8,128)S(1)}) custom-call(bf16[256,512]{1,0:T(8,128)(2,1)S(1)} %operator.1.refs_0_, bf16[64,32,128]{2,1,0:T(8,128)(2,1)S(1)} %copy-done.12, bf16[64,32,128]{2,1,0:T(8,128)(2,1)S(1)} %copy-done.8, ...), custom_call_target="tpu_custom_call" | custom-call | tf_op jit(solution)/shard_map/zterms/pallas_call | solution.py:202
  113.3 1.6 %collective-permute-done.9 = f16[2,1040,128]{2,1,0:T(8,128)(2,1)S(1)} collective-permute-done((f16[2,1040,128]{2,1,0:T(8,128)(2,1)S(1)}, f16[2,1040,128]{2,1,0:T(8,128)(2,1)S(1)}, u32[]{:S(2)}, u32[]{:S(2)}) %collective-permute-start.9) | collective-permute-done | bytes 532512 | tf_op jit(solution)/shard_map/ppermute | solution.py:325
  115.6 1.1 collective-permute-start.14
  117.6 1.6 %copy-done.2 = bf16[64,32,512]{2,1,0:T(8,128)(2,1)S(1)} copy-done((bf16[64,32,512]{2,1,0:T(8,128)(2,1)S(1)}, bf16[64,32,512]{2,1,0:T(8,128)(2,1)}, u32[]{:S(2)}) %copy-start.2) | copy-done | bytes 2097176
  119.1 2.2 %copy-done.9 = f32[64,32,512]{2,1,0:T(8,128)S(1)} copy-done((f32[64,32,512]{2,1,0:T(8,128)S(1)}, f32[64,32,512]{2,1,0:T(8,128)}, u32[]{:S(2)}) %copy-start.9) | copy-done | bytes 4194328
  121.3 1.6 %copy-done.10 = bf16[64,32,512]{2,1,0:T(8,128)(2,1)S(1)} copy-done((bf16[64,32,512]{2,1,0:T(8,128)(2,1)S(1)}, bf16[64,32,512]{2,1,0:T(8,128)(2,1)}, u32[]{:S(2)}) %copy-start.10) | copy-done | bytes 2097176
  122.9 4.4 %xterms.1.part_ref = f32[64,32,512]{2,1,0:T(8,128)S(1)} custom-call(bf16[64,32,512]{2,1,0:T(8,128)(2,1)S(1)} %copy-done.1, f32[64,32,512]{2,1,0:T(8,128)S(1)} %copy-done.9, bf16[64,32,512]{2,1,0:T(8,128)(2,1)S(1)} %copy-done.10, bf16[64,32,512]{2,1,0:T(8,128)(2,1)S(1)} %copy-done.2, bf16[512,512]{1,0:T(8,128)(2,1)S(1)} %copy-done.23, ...), custom_call_target="tpu_custom_call" | custom-call | tf_op jit(solution)/shard_map/xterms/pallas_call | solution.py:232
  127.4 2.0 %copy-done.4 = f32[64,32,512]{2,1,0:T(8,128)} copy-done((f32[64,32,512]{2,1,0:T(8,128)}, f32[64,32,512]{2,1,0:T(8,128)S(1)}, u32[]{:S(2)}) %copy-start.4) | copy-done | bytes 4194328
  129.4 6.8 %all-to-all-done.1 = f16[8,2064,128]{2,1,0:T(8,128)(2,1)} async-done(((f16[8,2064,128]{2,1,0:T(8,128)(2,1)}), f16[8,2064,128]{2,1,0:T(8,128)(2,1)}, u32[]{:S(2)}, u32[]{:S(2)}) %all-to-all-start.1) | async-done | bytes 4227104 | tf_op jit(solution)/shard_map/all_to_all | solution.py:369
  136.2 2.9 %convert_element_type.43.p_ref.c_ref.e_ref = f32[8,2064,128]{2,1,0:T(8,128)S(1)} convert(f16[8,2064,128]{2,1,0:T(8,128)(2,1)} %all-to-all-done.1) | non-fusion elementwise | flops 2113536 | bytes 12681216 | tf_op jit(solution)/shard_map/convert_element_type | solution.py:376
  139.1 1.2 copy-done.5
  140.3 2.9 %addy.1.part_ref = f32[64,32,512]{2,1,0:T(8,128)S(1)} custom-call(f32[64,32,512]{2,1,0:T(8,128)S(1)} %copy-done.5, bf16[64,32,512]{2,1,0:T(8,128)(2,1)S(1)} %copy-done.3, f32[8,2064,128]{2,1,0:T(8,128)S(1)} %convert_element_type.43.p_ref.c_ref.e_ref, f32[8,2064,128]{2,1,0:T(8,128)S(1)} %convert_element_type.43.p_ref.c_ref.e_ref, ...), custom_call_target="tpu_custom_call" | custom-call | tf_op jit(solution)/shard_map/addy/pallas_call | solution.py:307
  143.3 1.3 convert_element_type.51.p2
  144.6 1.1 convert_element_type.52.p3
  145.8 2.9 %last.2 = (f32[64,32,512]{2,1,0:T(8,128)}, bf16[64,32,512]{2,1,0:T(8,128)(2,1)}) custom-call(s32[2]{0:T(128)S(1)} %pad_add_fusion.at, bf16[64,32,512]{2,1,0:T(8,128)(2,1)S(1)} %copy-done.1, f32[64,32,512]{2,1,0:T(8,128)S(1)} %addy.1.part_ref, bf16[64,32,512]{2,1,0:T(8,128)(2,1)S(1)} %copy-done.6, bf16[64,32,512]{2,1,0:T(8,128)(2,1)S(1)} %copy-done.3, ...), custom_call_target="tpu_custom_call" | custom-call | tf_op jit(solution)/shard_map/last/pallas_call | solution.py:260
  148.6 1.3 collective-permute-done.13
  150.6 1.2 convert_element_type.53.p1
  151.8 1.1 convert_element_type.54.p2
  152.9 1.1 convert_element_type.55.p3
  154.1 2.9 %last.3 = (f32[64,32,512]{2,1,0:T(8,128)}, bf16[64,32,512]{2,1,0:T(8,128)(2,1)}) custom-call(s32[2]{0:T(128)S(1)} %pad_add_fusion.at, bf16[64,32,512]{2,1,0:T(8,128)(2,1)S(1)} %copy-done.1, f32[64,32,512]{2,1,0:T(8,128)S(1)} %addy.1.part_ref, bf16[64,32,512]{2,1,0:T(8,128)(2,1)S(1)} %copy-done.6, ...), custom_call_target="tpu_custom_call", output_to_operand_aliasing={{0}: (10, {}), {1}: (11, {})} | custom-call | tf_op jit(solution)/shard_map/last/pallas_call | solution.py:260
  (73 shorter events, 12.7 us)
Async XLA Ops:
  0.7 1.6 %copy-start = (bf16[64,32,512]{2,1,0:T(8,128)(2,1)S(1)}, bf16[64,32,512]{2,1,0:T(8,128)(2,1)}, u32[]{:S(2)}) copy-start(bf16[64,32,512]{2,1,0:T(8,128)(2,1)} %s_ref.9) | copy-start | bytes 6291460
  3.3 18.4 %copy-start.11 = (bf16[64,32,128]{2,1,0:T(8,128)(2,1)}, bf16[64,32,128]{2,1,0:T(8,128)(2,1)S(1)}, u32[]{:S(2)}) copy-start(bf16[64,32,128]{2,1,0:T(8,128)(2,1)S(1)} %get-tuple-element.38.refs_1_) | copy-start | bytes 1572868
  3.3 3.0 %collective-permute-start = (bf16[64,32,128]{2,1,0:T(8,128)(2,1)S(1)}, bf16[64,32,128]{2,1,0:T(8,128)(2,1)S(1)}, u32[]{:S(2)}, u32[]{:S(2)}) collective-permute-start(bf16[64,32,128]{2,1,0:T(8,128)(2,1)S(1)} %get-tuple-element.38.refs_1_), channel_id=1, source_target_pairs={{0,1},{1,0},{2,3},{3,2},{4,5},{5,4},{6,7},{7,6},{8,9},{9,8},{10,11... | collective-permute-start | bytes 1572872 | tf_op jit(solution)/shard_map/ppermute | solution.py:329
  8.4 0.8 copy-start.7
  9.2 12.9 %copy-start.19 = (bf16[512,512]{1,0:T(8,128)(2,1)S(1)}, bf16[512,512]{1,0:T(8,128)(2,1)}, u32[]{:S(2)}) copy-start(bf16[512,512]{1,0:T(8,128)(2,1)} %first_ref.4) | copy-start | bytes 1572868
  9.2 12.9 %copy-start.20 = (bf16[512,512]{1,0:T(8,128)(2,1)S(1)}, bf16[512,512]{1,0:T(8,128)(2,1)}, u32[]{:S(2)}) copy-start(bf16[512,512]{1,0:T(8,128)(2,1)} %second_ref.4) | copy-start | bytes 1572868
  9.2 41.8 %all-to-all-start = ((bf16[8,64,16,128]{3,2,1,0:T(8,128)(2,1)}), bf16[8,64,16,128]{3,2,1,0:T(8,128)(2,1)}, u32[]{:S(2)}, u32[]{:S(2)}) async-start(bf16[8,64,16,128]{3,2,1,0:T(8,128)(2,1)} %pack.1), calls=%async_computation | async-start | bytes 4194304 | tf_op jit(solution)/shard_map/all_to_all | solution.py:355
  16.1 15.5 %collective-permute-start.1 = (bf16[64,32,128]{2,1,0:T(8,128)(2,1)S(1)}, bf16[64,32,128]{2,1,0:T(8,128)(2,1)S(1)}, u32[]{:S(2)}, u32[]{:S(2)}) collective-permute-start(bf16[64,32,128]{2,1,0:T(8,128)(2,1)S(1)} %get-tuple-element.39), channel_id=1, source_target_pairs={{0,4},{1,5},{2,6},{3,7},{4,8},{5,9},{6,10},{7,11},{8,12},{9,13},{1... | collective-permute-start | bytes 1572872 | tf_op jit(solution)/shard_map/ppermute | solution.py:325
  17.7 26.0 %collective-permute-start.2 = (bf16[64,32,128]{2,1,0:T(8,128)(2,1)S(1)}, bf16[64,32,128]{2,1,0:T(8,128)(2,1)S(1)}, u32[]{:S(2)}, u32[]{:S(2)}) collective-permute-start(bf16[64,32,128]{2,1,0:T(8,128)(2,1)S(1)} %get-tuple-element.40), channel_id=1, source_target_pairs={{0,8},{1,9},{2,10},{3,11},{4,12},{5,13},{6,14},{7,15},{8,0},{9,1},... | collective-permute-start | bytes 1572872 | tf_op jit(solution)/shard_map/ppermute | solution.py:325
  21.0 32.5 %copy-start.28 = (f32[512]{0:T(512)S(1)}, f32[512]{0:T(512)}, u32[]{:S(2)}) copy-start(f32[512]{0:T(512)} %param.22) | copy-start | bytes 6148
  21.1 22.7 %collective-permute-start.3 = (bf16[64,32,128]{2,1,0:T(8,128)(2,1)S(1)}, bf16[64,32,128]{2,1,0:T(8,128)(2,1)S(1)}, u32[]{:S(2)}, u32[]{:S(2)}) collective-permute-start(bf16[64,32,128]{2,1,0:T(8,128)(2,1)S(1)} %get-tuple-element.41), channel_id=1, source_target_pairs={{0,12},{1,13},{2,14},{3,15},{4,0},{5,1},{6,2},{7,3},{8,4},{9,5},{1... | collective-permute-start | bytes 1572872 | tf_op jit(solution)/shard_map/ppermute | solution.py:325
  21.8 29.1 %collective-permute-start.4 = (bf16[64,32,128]{2,1,0:T(8,128)(2,1)S(1)}, bf16[64,32,128]{2,1,0:T(8,128)(2,1)}, u32[]{:S(2)}, u32[]{:S(2)}) collective-permute-start(bf16[64,32,128]{2,1,0:T(8,128)(2,1)S(1)} %get-tuple-element.38.refs_1_), channel_id=1, source_target_pairs={{0,2},{1,3},{2,0},{3,1},{4,6},{5,7},{6,4},{7,5},{8,10},{9,11},{10,... | collective-permute-start | bytes 1572872 | tf_op jit(solution)/shard_map/ppermute | solution.py:329
  51.0 19.7 %collective-permute-start.5 = (bf16[3,64,32,128]{3,2,1,0:T(8,128)(2,1)S(1)}, bf16[3,64,32,128]{3,2,1,0:T(8,128)(2,1)S(1)}, u32[]{:S(2)}, u32[]{:S(2)}) collective-permute-start(bf16[3,64,32,128]{3,2,1,0:T(8,128)(2,1)S(1)} %merge.1.refs_5_), channel_id=1, source_target_pairs={{0,1},{1,0},{2,3},{3,2},{4,5},{5,4},{6,7},{7,6},{8,9},{9,8},{10,11... | collective-permute-start | bytes 4718600 | tf_op jit(solution)/shard_map/ppermute | solution.py:329
  52.3 18.4 %collective-permute-start.6 = (bf16[64,32,128]{2,1,0:T(8,128)(2,1)}, bf16[64,32,128]{2,1,0:T(8,128)(2,1)}, u32[]{:S(2)}, u32[]{:S(2)}) collective-permute-start(bf16[64,32,128]{2,1,0:T(8,128)(2,1)} %collective-permute-done.4.refs_3_), channel_id=1, source_target_pairs={{0,1},{1,0},{2,3},{3,2},{4,5},{5,4},{6,7},{7,6},{8,9},{9,8},{10,11... | collective-permute-start | bytes 1572872 | tf_op jit(solution)/shard_map/ppermute | solution.py:329
  52.4 35.7 %collective-permute-start.7 = (bf16[3,64,32,128]{3,2,1,0:T(8,128)(2,1)S(1)}, bf16[3,64,32,128]{3,2,1,0:T(8,128)(2,1)}, u32[]{:S(2)}, u32[]{:S(2)}) collective-permute-start(bf16[3,64,32,128]{3,2,1,0:T(8,128)(2,1)S(1)} %merge.1.refs_5_), channel_id=1, source_target_pairs={{0,2},{1,3},{2,0},{3,1},{4,6},{5,7},{6,4},{7,5},{8,10},{9,11},{10,... | collective-permute-start | bytes 4718600 | tf_op jit(solution)/shard_map/ppermute | solution.py:329
  54.4 1.6 %copy-start.13 = (bf16[512,32,64]{0,2,1:T(8,128)(2,1)S(1)}, bf16[512,32,64]{0,2,1:T(8,128)(2,1)}, u32[]{:S(2)}) copy-start(bf16[512,32,64]{0,2,1:T(8,128)(2,1)} %param.18) | copy-start | bytes 6291460
  56.0 0.9 copy-start.18
  57.0 1.0 copy-start.21
  58.0 1.0 copy-start.22
  70.7 65.5 %all-to-all-start.1 = ((f16[8,2064,128]{2,1,0:T(8,128)(2,1)}), f16[8,2064,128]{2,1,0:T(8,128)(2,1)}, u32[]{:S(2)}, u32[]{:S(2)}) async-start(f16[8,2064,128]{2,1,0:T(8,128)(2,1)} %convert_element_type.42), calls=%async_computation.1 | async-start | bytes 8454144 | tf_op jit(solution)/shard_map/all_to_all | solution.py:369
  88.1 5.3 %collective-permute-start.8 = (bf16[3,64,32,128]{3,2,1,0:T(8,128)(2,1)}, bf16[3,64,32,128]{3,2,1,0:T(8,128)(2,1)S(1)}, u32[]{:S(2)}, u32[]{:S(2)}) collective-permute-start(bf16[3,64,32,128]{3,2,1,0:T(8,128)(2,1)} %collective-permute-done.7.refs_7_), channel_id=1, source_target_pairs={{0,1},{1,0},{2,3},{3,2},{4,5},{5,4},{6,7},{7,6},{8,9},{9,8},{10,11... | collective-permute-start | bytes 4718600 | tf_op jit(solution)/shard_map/ppermute | solution.py:329
  93.4 1.0 copy-start.8
  94.5 1.0 copy-start.12
  98.6 6.9 %copy-start.14 = (f32[2,1040,128]{2,1,0:T(8,128)}, f32[2,1040,128]{2,1,0:T(8,128)S(1)}, u32[]{:S(2)}) copy-start(f32[2,1040,128]{2,1,0:T(8,128)S(1)} %get-tuple-element.61.p0) | copy-start | bytes 3194884
  98.7 16.1 %collective-permute-start.9 = (f16[2,1040,128]{2,1,0:T(8,128)(2,1)S(1)}, f16[2,1040,128]{2,1,0:T(8,128)(2,1)S(1)}, u32[]{:S(2)}, u32[]{:S(2)}) collective-permute-start(f16[2,1040,128]{2,1,0:T(8,128)(2,1)S(1)} %convert_element_type.44), channel_id=1, source_target_pairs={{0,4},{1,5},{2,6},{3,7},{4,8},{5,9},{6,10},{7,11},{8,12},{9,13},{1... | collective-permute-start | bytes 1597448 | tf_op jit(solution)/shard_map/ppermute | solution.py:325
  101.3 41.9 %collective-permute-start.10 = (f16[2,1040,128]{2,1,0:T(8,128)(2,1)}, f16[2,1040,128]{2,1,0:T(8,128)(2,1)}, u32[]{:S(2)}, u32[]{:S(2)}) collective-permute-start(f16[2,1040,128]{2,1,0:T(8,128)(2,1)} %convert_element_type.45), channel_id=1, source_target_pairs={{0,8},{1,9},{2,10},{3,11},{4,12},{5,13},{6,14},{7,15},{8,0},{9,1},... | collective-permute-start | bytes 1597448 | tf_op jit(solution)/shard_map/ppermute | solution.py:325
  105.5 37.7 %collective-permute-start.11 = (f16[2,1040,128]{2,1,0:T(8,128)(2,1)}, f16[2,1040,128]{2,1,0:T(8,128)(2,1)}, u32[]{:S(2)}, u32[]{:S(2)}) collective-permute-start(f16[2,1040,128]{2,1,0:T(8,128)(2,1)} %convert_element_type.46), channel_id=1, source_target_pairs={{0,12},{1,13},{2,14},{3,15},{4,0},{5,1},{6,2},{7,3},{8,4},{9,5},{1... | collective-permute-start | bytes 1597448 | tf_op jit(solution)/shard_map/ppermute | solution.py:325
  109.4 3.9 %copy-start.16 = (f32[2,1040,128]{2,1,0:T(8,128)}, f32[2,1040,128]{2,1,0:T(8,128)S(1)}, u32[]{:S(2)}) copy-start(f32[2,1040,128]{2,1,0:T(8,128)S(1)} %get-tuple-element.68.p0) | copy-start | bytes 3194884
  109.4 8.1 %copy-start.1 = (bf16[64,32,512]{2,1,0:T(8,128)(2,1)S(1)}, bf16[64,32,512]{2,1,0:T(8,128)(2,1)}, u32[]{:S(2)}) copy-start(bf16[64,32,512]{2,1,0:T(8,128)(2,1)} %s_ref.9) | copy-start | bytes 6291460
  109.4 8.1 %copy-start.23 = (bf16[512,512]{1,0:T(8,128)(2,1)S(1)}, bf16[512,512]{1,0:T(8,128)(2,1)}, u32[]{:S(2)}) copy-start(bf16[512,512]{1,0:T(8,128)(2,1)} %first_ref.3) | copy-start | bytes 1572868
  109.4 8.1 %copy-start.24 = (bf16[512,512]{1,0:T(8,128)(2,1)S(1)}, bf16[512,512]{1,0:T(8,128)(2,1)}, u32[]{:S(2)}) copy-start(bf16[512,512]{1,0:T(8,128)(2,1)} %second_ref.3) | copy-start | bytes 1572868
  109.4 8.1 %copy-start.25 = (f32[512]{0:T(512)S(1)}, f32[512]{0:T(512)}, u32[]{:S(2)}) copy-start(f32[512]{0:T(512)} %param.21) | copy-start | bytes 6148
  110.3 38.3 %collective-permute-start.12 = (f16[2,1040,128]{2,1,0:T(8,128)(2,1)}, f16[2,1040,128]{2,1,0:T(8,128)(2,1)}, u32[]{:S(2)}, u32[]{:S(2)}) collective-permute-start(f16[2,1040,128]{2,1,0:T(8,128)(2,1)} %convert_element_type.47), channel_id=1, source_target_pairs={{0,4},{1,5},{2,6},{3,7},{4,8},{5,9},{6,10},{7,11},{8,12},{9,13},{1... | collective-permute-start | bytes 1597448 | tf_op jit(solution)/shard_map/ppermute | solution.py:325
  111.9 38.1 %collective-permute-start.13 = (f16[2,1040,128]{2,1,0:T(8,128)(2,1)}, f16[2,1040,128]{2,1,0:T(8,128)(2,1)}, u32[]{:S(2)}, u32[]{:S(2)}) collective-permute-start(f16[2,1040,128]{2,1,0:T(8,128)(2,1)} %convert_element_type.48), channel_id=1, source_target_pairs={{0,8},{1,9},{2,10},{3,11},{4,12},{5,13},{6,14},{7,15},{8,0},{9,1},... | collective-permute-start | bytes 1597448 | tf_op jit(solution)/shard_map/ppermute | solution.py:325
  114.8 0.8 copy-start.26
  115.6 35.0 %collective-permute-start.14 = (f16[2,1040,128]{2,1,0:T(8,128)(2,1)}, f16[2,1040,128]{2,1,0:T(8,128)(2,1)}, u32[]{:S(2)}, u32[]{:S(2)}) collective-permute-start(f16[2,1040,128]{2,1,0:T(8,128)(2,1)} %convert_element_type.49), channel_id=1, source_target_pairs={{0,12},{1,13},{2,14},{3,15},{4,0},{5,1},{6,2},{7,3},{8,4},{9,5},{1... | collective-permute-start | bytes 1597448 | tf_op jit(solution)/shard_map/ppermute | solution.py:325
  117.5 1.6 %copy-start.2 = (bf16[64,32,512]{2,1,0:T(8,128)(2,1)S(1)}, bf16[64,32,512]{2,1,0:T(8,128)(2,1)}, u32[]{:S(2)}) copy-start(bf16[64,32,512]{2,1,0:T(8,128)(2,1)} %diff_ref.7) | copy-start | bytes 6291460
  119.1 2.2 %copy-start.9 = (f32[64,32,512]{2,1,0:T(8,128)S(1)}, f32[64,32,512]{2,1,0:T(8,128)}, u32[]{:S(2)}) copy-start(f32[64,32,512]{2,1,0:T(8,128)} %reg_ref.1) | copy-start | bytes 12582916
  121.3 1.6 %copy-start.10 = (bf16[64,32,512]{2,1,0:T(8,128)(2,1)S(1)}, bf16[64,32,512]{2,1,0:T(8,128)(2,1)}, u32[]{:S(2)}) copy-start(bf16[64,32,512]{2,1,0:T(8,128)(2,1)} %drift_ref.3) | copy-start | bytes 6291460
  127.4 2.0 %copy-start.4 = (f32[64,32,512]{2,1,0:T(8,128)}, f32[64,32,512]{2,1,0:T(8,128)S(1)}, u32[]{:S(2)}) copy-start(f32[64,32,512]{2,1,0:T(8,128)S(1)} %xterms.1.part_ref) | copy-start | bytes 12582916
  136.2 2.9 %copy-start.3 = (bf16[64,32,512]{2,1,0:T(8,128)(2,1)S(1)}, bf16[64,32,512]{2,1,0:T(8,128)(2,1)}, u32[]{:S(2)}) copy-start(bf16[64,32,512]{2,1,0:T(8,128)(2,1)} %diff_ref.7) | copy-start | bytes 6291460
  136.2 4.1 %copy-start.5 = (f32[64,32,512]{2,1,0:T(8,128)S(1)}, f32[64,32,512]{2,1,0:T(8,128)}, u32[]{:S(2)}) copy-start(f32[64,32,512]{2,1,0:T(8,128)} %copy-done.4) | copy-start | bytes 12582916
  140.3 2.9 %copy-start.27 = (f16[2,1040,128]{2,1,0:T(8,128)(2,1)S(1)}, f16[2,1040,128]{2,1,0:T(8,128)(2,1)}, u32[]{:S(2)}) copy-start(f16[2,1040,128]{2,1,0:T(8,128)(2,1)} %copy-done.26) | copy-start | bytes 1597444
  143.2 2.6 %copy-start.6 = (bf16[64,32,512]{2,1,0:T(8,128)(2,1)S(1)}, bf16[64,32,512]{2,1,0:T(8,128)(2,1)}, u32[]{:S(2)}) copy-start(bf16[64,32,512]{2,1,0:T(8,128)(2,1)} %drift_ref.5) | copy-start | bytes 6291460
  143.2 2.6 %copy-start.15 = (f32[2,1040,128]{2,1,0:T(8,128)S(1)}, f32[2,1040,128]{2,1,0:T(8,128)}, u32[]{:S(2)}) copy-start(f32[2,1040,128]{2,1,0:T(8,128)} %copy-done.14) | copy-start | bytes 3194884
  150.6 3.4 %copy-start.17 = (f32[2,1040,128]{2,1,0:T(8,128)S(1)}, f32[2,1040,128]{2,1,0:T(8,128)}, u32[]{:S(2)}) copy-start(f32[2,1040,128]{2,1,0:T(8,128)} %copy-done.16) | copy-start | bytes 3194884

commit v3 on v2

--- a/solution.py
+++ b/solution.py
@@ -11,10 +11,11 @@
 
 NJ, NK, NI = 64, 32, 512
 YB = 16
+ZB = 20000000000
 PIECE = YB * 64
 HALVES = 2
 HJ = NJ // HALVES
-CHUNKS = 1
+CHUNKS = 2
 CJ = NJ // CHUNKS
 
 
@@ -72,6 +73,7 @@
         out_specs=[whole] * CHUNKS,
         out_shape=[jax.ShapeDtypeStruct((3, CJ, NK, 128), BF16)] * CHUNKS,
         compiler_params=params(8),
+        cost_estimate=pl.CostEstimate(flops=20 * 10**9, transcendentals=0, bytes_accessed=3 << 20),
         name="merge",
     )(*parts)
 
@@ -92,7 +94,7 @@
     )(scalar, after)
 
 
-def operator_kernel(at, first_ref, second_ref, out_ref):
+def operator_kernel(at, first_ref, second_ref, first_y, second_y, drift_ref, out_ref, ops_ref, wind_ref):
     zc, pair = at[0], at[1]
     rows = []
     for t in range(4):
@@ -105,27 +107,34 @@
     block = 128 * lax.rem(zc + 4 - s, 4) + 32 * jnp.bitwise_xor(pair, flip)
     pick = jnp.where(at_k == block + low, 1.0, 0.0).astype(BF16)
     out_ref[...] = jnp.dot(rows, pick, preferred_element_type=F32).astype(BF16)
-
-
-def operator_rows(at, first, second):
+    ops_ref[0:512] = first_y[...]
+    ops_ref[512:1024] = second_y[...]
+    wind_ref[...] = drift_ref[...]
+
+
+def operator_rows(at, first, second, first_y, second_y, drift):
     whole = pl.BlockSpec(memory_space=pltpu.VMEM)
     return pl.pallas_call(
         operator_kernel,
-        in_specs=[pl.BlockSpec(memory_space=pltpu.SMEM), whole, whole],
-        out_specs=whole,
-        out_shape=jax.ShapeDtypeStruct((256, 512), BF16),
-        compiler_params=params(8),
+        in_specs=[pl.BlockSpec(memory_space=pltpu.SMEM)] + [whole] * 5,
+        out_specs=[whole] * 3,
+        out_shape=[
+            jax.ShapeDtypeStruct((256, 512), BF16),
+            jax.ShapeDtypeStruct((1024, 512), BF16),
+            jax.ShapeDtypeStruct((NK, 64, 512), BF16),
+        ],
+        compiler_params=params(16),
         name="operator",
-    )(at, first, second)
-
-
-def y_kernel(odd_ref, s_ref, drift_ref, first_ref, second_ref, metric_ref, out_ref, s32, p32, c32):
+    )(at, first, second, first_y, second_y, drift)
+
+
+def y_kernel(odd_ref, s_ref, drift_ref, ops_ref, metric_ref, out_ref, s32, p32, c32):
     @pl.when(pl.program_id(0) == 0)
     def _():
         s32[...] = s_ref[...].astype(F32).reshape(8 * NJ * 16, 128)
         metric = metric_ref[...]
         metric2 = metric * metric
-        ops = jnp.concatenate([first_ref[...], second_ref[...]], axis=0)
+        ops = ops_ref[...]
         eye = lax.broadcasted_iota(jnp.int32, (512, 512), 0) == lax.broadcasted_iota(jnp.int32, (512, 512), 1)
         eye = jnp.where(eye, 1.0, 0.0).astype(BF16)
         low = 16 * odd_ref[0]
@@ -152,8 +161,7 @@
     out_ref[0, 2056:2064, :] = jnp.broadcast_to(ce, (8, 128))
 
 
-def y_terms(odd, s, drift, first, second, metric):
-    op = pl.BlockSpec((512, 512), lambda d: (0, 0))
+def y_terms(odd, s, drift, ops, metric):
     scratch = pltpu.VMEM((8 * NJ * 16, 128), F32)
     return pl.pallas_call(
         y_kernel,
@@ -162,16 +170,16 @@
             pl.BlockSpec(memory_space=pltpu.SMEM),
             pl.BlockSpec((8, NJ, 16, 128), lambda d: (0, 0, 0, 0)),
             pl.BlockSpec((NK, 64, 512), lambda d: (0, 0, 0)),
-            op,
-            op,
+            pl.BlockSpec((1024, 512), lambda d: (0, 0)),
             pl.BlockSpec((512, 1), lambda d: (0, 0)),
         ],
         out_specs=pl.BlockSpec((1, 2064, 128), lambda d: (d, 0, 0)),
         out_shape=jax.ShapeDtypeStruct((8, 2064, 128), F32),
         scratch_shapes=[scratch, scratch, scratch],
         compiler_params=params(40),
+        cost_estimate=pl.CostEstimate(flops=1000, transcendentals=0, bytes_accessed=8 << 10),
         name="yterms",
-    )(odd, s, drift, first, second, metric)
+    )(odd, s, drift, ops, metric)
 
 
 def z_kernel(*refs):
@@ -204,10 +212,11 @@
         grid=(HJ // YB,),
         in_specs=[pl.BlockSpec((256, 512), lambda j: (0, 0))]
         + [pl.BlockSpec((YB, NK, 128), lambda j: (HJ // YB * h + j, 0, 0))] * 4
-        + [pl.BlockSpec((3, YB, NK, 128), lambda j: (0, HJ // YB * h + j, 0, 0))] * 4,
+        + [pl.BlockSpec((3, YB, NK, 128), lambda j: (0, j, 0, 0))] * 4,
         out_specs=[pl.BlockSpec((1, PIECE + 16, 128), lambda j: (j, 0, 0))] * 4,
         out_shape=[out] * 4,
         compiler_params=params(16),
+        cost_estimate=pl.CostEstimate(flops=(1000, ZB)[h], transcendentals=0, bytes_accessed=8 << 10),
         name="zterms",
     )(rows, *firsts, *rests)
 
@@ -236,6 +245,7 @@
         out_specs=field,
         out_shape=jax.ShapeDtypeStruct((NJ, NK, NI), F32),
         compiler_params=params(20),
+        cost_estimate=pl.CostEstimate(flops=1000, transcendentals=0, bytes_accessed=8 << 10),
         name="xterms",
     )(scalar, reg, drift, diff, first, second, metric)
 
@@ -352,33 +362,43 @@
     own = jnp.broadcast_to(own[:, None], (NK, 128))
     mine = cut(at, scalar)
     beside, across = flip(mine[0], 1), flip(mine[0], 2)
-    scalar_y = lax.all_to_all(pack(scalar, beside), "row", 0, 0, tiled=False)
-    rows = operator_rows(at, first_z, second_z)
-    *rest, across, rows = lax.optimization_barrier(
-        [ring(mine[s], s) for s in range(1, 4)] + [across, rows]
+    scalar_y = lax.all_to_all(pack(scalar, mine[0]), "row", 0, 0, tiled=False)
+    wind = jnp.transpose(drift_y, (1, 2, 0))
+    rows, ops, wind = operator_rows(at, first_z, second_z, first_y, second_y, wind)
+    part = x_terms(scalar, register_in, drift_x, diffusivity, first_x, second_x, metric_x[None, :])
+    *rest, across, rows, ops, wind, part = lax.optimization_barrier(
+        [ring(mine[s], s) for s in range(1, 4)] + [across, rows, ops, wind, part]
     )
-    rest = merge(rest)[0]
-    far = flip(rest, 2)
-    scalar_y, rest = lax.optimization_barrier((scalar_y, rest))
+    rest = list(merge(rest))
+    far = [flip(rest[0], 2)]
+    near = [flip(part, 1) for part in rest]
+    scalar_y, *rest = lax.optimization_barrier((scalar_y, *rest))
     odd = (lax.axis_index("row") % 2).astype(jnp.int32)[None]
-    wind = jnp.transpose(drift_y, (1, 2, 0))
-    y_out = y_terms(odd, scalar_y, wind, first_y, second_y, metric_y[:, None]).astype(F16)
-    rests = [rest, flip(rest, 1)]
+    y_out = y_terms(odd, scalar_y, wind, ops, metric_y[:, None]).astype(F16)
+    far[0], rest[1] = lax.optimization_barrier((far[0], rest[1]))
+    far.append(flip(rest[1], 2))
+    near[0], across, far[0], y_out = lax.optimization_barrier((near[0], across, far[0], y_out))
     firsts = [mine[0], beside, across, flip(across, 1)]
-    y_out, rests[1], firsts[3] = lax.optimization_barrier((y_out, rests[1], firsts[3]))
+
+    def z_half(h):
+        z_out = z_terms(h, rows, firsts, [rest[h], near[h], far[h], flip(far[h], 1)])
+        return [z_out[0]] + [z_out[t].astype(F16) for t in range(1, 4)]
+
+    def send_back(z_out):
+        return [z_out[0]] + [ring(z_out[t], t) for t in range(1, 4)]
+
+    z_send = z_half(0)
+    y_out, z_send = lax.optimization_barrier((y_out, z_send))
+    z_back = [send_back(z_send)]
     y_back = lax.all_to_all(y_out, "row", 0, 0, tiled=False)
-    rests += [far, flip(far, 1)]
-    part = x_terms(scalar, register_in, drift_x, diffusivity, first_x, second_x, metric_x[None, :])
-    z_back = []
-    for h in range(HALVES):
-        z_out = z_terms(h, rows, firsts, rests)
-        z_back.append([z_out[0]] + [ring(z_out[t].astype(F16), t) for t in range(1, 4)])
+    z_back.append(send_back(z_half(1)))
     part = add_y(part, diffusivity, y_back.astype(F32))
+    z_back[0] = [z.astype(F32) for z in z_back[0]]
+    part, z_back[1] = lax.optimization_barrier((part, z_back[1]))
+    z_back[1] = [z.astype(F32) for z in z_back[1]]
     done = ()
     for h in range(HALVES):
-        part, z_half, done = lax.optimization_barrier((part, z_back[h], done))
-        z_half = [z.astype(F32) for z in z_half]
-        done = last_terms(at, h, scalar, part, drift_z, diffusivity, own, z_half, done)
+        done = last_terms(at, h, scalar, part, drift_z, diffusivity, own, z_back[h], done)
     return tuple(done)
 
 

time: 159 us -> 150 us (0.943)
  waiting for transfers between devices: 53.8 us -> 40.8 us
  Pallas kernels: 32.3 us -> 36.5 us
  other arithmetic: 15.9 us -> 19.9 us
  local copies, waits for them, and re-layouts: 20.2 us -> 17.2 us
    ppermute x6 -> x9, waiting for transfers between devices: 22.6 us -> 7.06 us  [flip(): return lax.ppermute(x, 'col', [(c, c ^ bits) for c in range(16)])]
    ppermute x9, waiting for transfers between devices: 24.3 us -> 14.5 us  [ring(): lax.ppermute(x, 'col', [(c, (c + 4 * shift) % 16) for c in range(16)])]
    all_to_all x1, waiting for transfers between devices: 0.01 us -> 7.94 us  [on_device(): scalar_y = lax.all_to_all(pack(scalar, mine[0]), 'row', 0, 0, tiled=False)]
    all_to_all x1, waiting for transfers between devices: 6.81 us -> 11.2 us  [on_device(): y_back = lax.all_to_all(y_out, 'row', 0, 0, tiled=False)]
    convert_element_type x13, other arithmetic: 13 us -> 16.9 us  [the longest x6 5.43 us: z_half(): return [z_out[0]] + [z_out[t].astype(F16) for t in range(1, 4)]]
    ppermute x6 -> x9, starting transfers between devices: 6.44 us -> 10.1 us  [flip(): return lax.ppermute(x, 'col', [(c, c ^ bits) for c in range(16)])]
    pallas_call x1, Pallas kernels: 0.1 us -> 3.67 us  [merge(): pl.pallas_call(merge_kernel, in_specs=[whole] * 3, out_specs=[whole] * CH...]
    unnamed x58 -> x64, local copies, waits for them, and re-layouts: 18.6 us -> 16.2 us
  transfers between devices with their start and end apart: 17 -> 20, of which waited for: 10 -> 6; matrix products, arithmetic and copies ran while one was open for 9% -> 11% of each run, Pallas kernels for 17% -> 19%
where the time goes in v3:
time: 150 us; the launch traced here: 149 us
  waiting for transfers between devices  40.8 us (27%)
  Pallas kernels  36.5 us (24%)
  starting transfers between devices  33.7 us (22%)
  other arithmetic  19.9 us (13%)
  local copies, waits for them, and re-layouts  17.2 us (11%)
    unnamed x64, local copies, waits for them, and re-layouts  16.2 us
    ppermute x9, waiting for transfers between devices, ring(): lax.ppermute(x, 'col', [(c, (c + 4 * shift) % 16) for c in range(16)])  14.5 us
    ppermute x9, starting transfers between devices, ring(): lax.ppermute(x, 'col', [(c, (c + 4 * shift) % 16) for c in range(16)])  11.7 us
    all_to_all x1, waiting for transfers between devices, on_device(): y_back = lax.all_to_all(y_out, 'row', 0, 0, tiled=False)  11.2 us
    ppermute x9, starting transfers between devices, flip(): return lax.ppermute(x, 'col', [(c, c ^ bits) for c in range(16)])  10.1 us
    pallas_call x1, Pallas kernels, y_terms(): pl.pallas_call(y_kernel, grid=(8,), in_specs=[pl.BlockSpec(memory_space=p...  9.01 us
    all_to_all x1, waiting for transfers between devices, on_device(): scalar_y = lax.all_to_all(pack(scalar, mine[0]), 'row', 0, 0, tiled=False)  7.94 us
    ppermute x9, waiting for transfers between devices, flip(): return lax.ppermute(x, 'col', [(c, c ^ bits) for c in range(16)])  7.06 us
  transfers between devices with their start and end apart: 20, of which 6 were waited for; matrix products, arithmetic and copies ran while one was open for 11% of the time, Pallas kernels for 19%

profile of v3, /device:TPU:1, one launch (start us, length us, event | category | flops | bytes accessed | tf_op | source)
XLA Modules:
  0.0 149.0 jit_solution(15012488645239998012)
XLA Ops:
  0.7 1.6 %copy-done = bf16[64,32,512]{2,1,0:T(8,128)(2,1)S(1)} copy-done((bf16[64,32,512]{2,1,0:T(8,128)(2,1)S(1)}, bf16[64,32,512]{2,1,0:T(8,128)(2,1)}, u32[]{:S(2)}) %copy-start) | copy-done | bytes 2097176
  2.3 2.4 %cut.1 = (bf16[64,32,128]{2,1,0:T(8,128)(2,1)S(1)}, bf16[64,32,128]{2,1,0:T(8,128)(2,1)}, bf16[64,32,128]{2,1,0:T(8,128)(2,1)}, bf16[64,32,128]{2,1,0:T(8,128)(2,1)}) custom-call(s32[2]{0:T(128)S(1)} %pad_add_fusion.at, bf16[64,32,512]{2,1,0:T(8,128)(2,1)S(1)} %copy-done), custom_call_target="tpu_custom_call" | custom-call | tf_op jit(solution)/shard_map/cut/pallas_call | solution.py:40
  4.7 2.5 %collective-permute-start = (bf16[64,32,128]{2,1,0:T(8,128)(2,1)}, bf16[64,32,128]{2,1,0:T(8,128)(2,1)}, u32[]{:S(2)}, u32[]{:S(2)}) collective-permute-start(bf16[64,32,128]{2,1,0:T(8,128)(2,1)} %get-tuple-element.48), channel_id=1, source_target_pairs={{0,4},{1,5},{2,6},{3,7},{4,8},{5,9},{6,10},{7,11},{8,12},{9,13},{1... | collective-permute-start | bytes 1572872 | tf_op jit(solution)/shard_map/ppermute | solution.py:335
  7.2 3.3 %collective-permute-start.1 = (bf16[64,32,128]{2,1,0:T(8,128)(2,1)}, bf16[64,32,128]{2,1,0:T(8,128)(2,1)}, u32[]{:S(2)}, u32[]{:S(2)}) collective-permute-start(bf16[64,32,128]{2,1,0:T(8,128)(2,1)} %get-tuple-element.49), channel_id=1, source_target_pairs={{0,8},{1,9},{2,10},{3,11},{4,12},{5,13},{6,14},{7,15},{8,0},{9,1},... | collective-permute-start | bytes 1572872 | tf_op jit(solution)/shard_map/ppermute | solution.py:335
  11.2 1.2 collective-permute-start.3
  13.2 1.3 copy-done.6
  14.5 6.6 %all-to-all-start = ((bf16[8,64,16,128]{3,2,1,0:T(8,128)(2,1)}), bf16[8,64,16,128]{3,2,1,0:T(8,128)(2,1)}, u32[]{:S(2)}, u32[]{:S(2)}) async-start(bf16[8,64,16,128]{3,2,1,0:T(8,128)(2,1)} %copy-done.6), calls=%async_computation | async-start | bytes 4194304 | tf_op jit(solution)/shard_map/all_to_all | solution.py:365
  21.1 1.6 %copy-done.2 = bf16[64,32,512]{2,1,0:T(8,128)(2,1)S(1)} copy-done((bf16[64,32,512]{2,1,0:T(8,128)(2,1)S(1)}, bf16[64,32,512]{2,1,0:T(8,128)(2,1)}, u32[]{:S(2)}) %copy-start.2) | copy-done | bytes 2097176
  22.7 2.2 %copy-done.10 = f32[64,32,512]{2,1,0:T(8,128)S(1)} copy-done((f32[64,32,512]{2,1,0:T(8,128)S(1)}, f32[64,32,512]{2,1,0:T(8,128)}, u32[]{:S(2)}) %copy-start.10) | copy-done | bytes 4194328
  24.9 1.6 %copy-done.11 = bf16[64,32,512]{2,1,0:T(8,128)(2,1)S(1)} copy-done((bf16[64,32,512]{2,1,0:T(8,128)(2,1)S(1)}, bf16[64,32,512]{2,1,0:T(8,128)(2,1)}, u32[]{:S(2)}) %copy-start.11) | copy-done | bytes 2097176
  26.5 1.0 copy-done.22
  27.6 4.4 %xterms.1.part_ref = f32[64,32,512]{2,1,0:T(8,128)S(1)} custom-call(bf16[64,32,512]{2,1,0:T(8,128)(2,1)S(1)} %copy-done.1, f32[64,32,512]{2,1,0:T(8,128)S(1)} %copy-done.10, bf16[64,32,512]{2,1,0:T(8,128)(2,1)S(1)} %copy-done.11, bf16[64,32,512]{2,1,0:T(8,128)(2,1)S(1)} %copy-done.2, bf16[512,512]{1,0:T(8,128)(2,1)S(1)} %copy-done.21, ...), custom_call_target="tpu_custom_call" | custom-call | flops 1000 | bytes 8192 | tf_op jit(solution)/shard_map/xterms/pallas_call | solution.py:241
  32.1 1.0 operator.1
  33.1 1.0 copy-done.4
  34.1 3.7 %merge.1 = (bf16[3,32,32,128]{3,2,1,0:T(8,128)(2,1)}, bf16[3,32,32,128]{3,2,1,0:T(8,128)(2,1)}) custom-call(bf16[64,32,128]{2,1,0:T(8,128)(2,1)} %collective-permute-done.r1, bf16[64,32,128]{2,1,0:T(8,128)(2,1)} %collective-permute-done.1.r2, bf16[64,32,128]{2,1,0:T(8,128)(2,1)} %collective-permute-done.2.r3), custom_call_target="tpu_custom_call" | custom-call | flops 20000000000 | bytes 3145728 | tf_op jit(solution)/shard_map/merge/pallas_call | solution.py:70
  37.8 2.3 %collective-permute-start.4 = (bf16[3,32,32,128]{3,2,1,0:T(8,128)(2,1)}, bf16[3,32,32,128]{3,2,1,0:T(8,128)(2,1)}, u32[]{:S(2)}, u32[]{:S(2)}) collective-permute-start(bf16[3,32,32,128]{3,2,1,0:T(8,128)(2,1)} %get-tuple-element.70.refs_5_), channel_id=1, source_target_pairs={{0,1},{1,0},{2,3},{3,2},{4,5},{5,4},{6,7},{7,6},{8,9},{9,8},{10,11... | collective-permute-start | bytes 2359304 | tf_op jit(solution)/shard_map/ppermute | solution.py:339
  40.2 7.9 %all-to-all-done.s_ref = bf16[8,64,16,128]{3,2,1,0:T(8,128)(2,1)} async-done(((bf16[8,64,16,128]{3,2,1,0:T(8,128)(2,1)}), bf16[8,64,16,128]{3,2,1,0:T(8,128)(2,1)}, u32[]{:S(2)}, u32[]{:S(2)}) %all-to-all-start) | async-done | bytes 2097184 | tf_op jit(solution)/shard_map/all_to_all | solution.py:365
  48.2 1.6 %copy-done.14 = bf16[32,64,512]{2,1,0:T(8,128)(2,1)S(1)} copy-done((bf16[32,64,512]{2,1,0:T(8,128)(2,1)S(1)}, bf16[32,64,512]{2,1,0:T(8,128)(2,1)}, u32[]{:S(2)}) %copy-start.14) | copy-done | bytes 2097176
  49.8 1.2 copy-done.20
  51.0 9.0 %yterms.1 = f32[8,2064,128]{2,1,0:T(8,128)S(1)} custom-call(s32[1]{0:T(128)} %bitcast.4.odd_ref, bf16[8,64,16,128]{3,2,1,0:T(8,128)(2,1)} %all-to-all-done.s_ref, bf16[32,64,512]{2,1,0:T(8,128)(2,1)S(1)} %copy-done.14, bf16[1024,512]{1,0:T(8,128)(2,1)S(1)} %copy-done.20, f32[512,1]{1,0:T(8,128)S(1)} %copy.19.metric_ref), custom_call_target="tpu_custom_call" | custom-call | flops 1000 | bytes 8192 | tf_op jit(solution)/shard_map/yterms/pallas_call | solution.py:166
  60.0 2.5 %convert_element_type.42 = f16[8,2064,128]{2,1,0:T(8,128)(2,1)} convert(f32[8,2064,128]{2,1,0:T(8,128)S(1)} %yterms.1) | non-fusion elementwise | flops 2113536 | bytes 12681216 | tf_op jit(solution)/shard_map/convert_element_type | solution.py:377
  62.5 3.9 %collective-permute-start.8 = (bf16[3,32,32,128]{3,2,1,0:T(8,128)(2,1)}, bf16[3,32,32,128]{3,2,1,0:T(8,128)(2,1)S(1)}, u32[]{:S(2)}, u32[]{:S(2)}) collective-permute-start(bf16[3,32,32,128]{3,2,1,0:T(8,128)(2,1)} %collective-permute-done.5.refs_7_), channel_id=1, source_target_pairs={{0,1},{1,0},{2,3},{3,2},{4,5},{5,4},{6,7},{7,6},{8,9},{9,8},{10,11... | collective-permute-start | bytes 2359304 | tf_op jit(solution)/shard_map/ppermute | solution.py:339
  67.2 2.6 %collective-permute-done.6.refs_2_ = bf16[64,32,128]{2,1,0:T(8,128)(2,1)S(1)} collective-permute-done((bf16[64,32,128]{2,1,0:T(8,128)(2,1)S(1)}, bf16[64,32,128]{2,1,0:T(8,128)(2,1)S(1)}, u32[]{:S(2)}, u32[]{:S(2)}) %collective-permute-start.6) | collective-permute-done | bytes 524320 | tf_op jit(solution)/shard_map/ppermute | solution.py:339
  70.1 3.5 %zterms.2 = (f32[2,1040,128]{2,1,0:T(8,128)S(1)}, f32[2,1040,128]{2,1,0:T(8,128)S(1)}, f32[2,1040,128]{2,1,0:T(8,128)S(1)}, f32[2,1040,128]{2,1,0:T(8,128)S(1)}) custom-call(bf16[256,512]{1,0:T(8,128)(2,1)S(1)} %get-tuple-element.68.refs_0_, bf16[64,32,128]{2,1,0:T(8,128)(2,1)S(1)} %get-tuple-element.51.after_ref.refs_1_, ...), custom_call_target="tpu_custom_call" | custom-call | flops 1000 | bytes 8192 | tf_op jit(solution)/shard_map/zterms/pallas_call | solution.py:210
  73.6 1.0 convert_element_type.43
  74.6 0.9 convert_element_type.44
  76.3 5.3 %all-to-all-start.1 = ((f16[8,2064,128]{2,1,0:T(8,128)(2,1)}), f16[8,2064,128]{2,1,0:T(8,128)(2,1)}, u32[]{:S(2)}, u32[]{:S(2)}) async-start(f16[8,2064,128]{2,1,0:T(8,128)(2,1)} %convert_element_type.42), calls=%async_computation.1 | async-start | bytes 8454144 | tf_op jit(solution)/shard_map/all_to_all | solution.py:393
  82.3 4.1 %collective-permute-done.10.refs_7_ = bf16[3,32,32,128]{3,2,1,0:T(8,128)(2,1)} collective-permute-done((bf16[3,32,32,128]{3,2,1,0:T(8,128)(2,1)}, bf16[3,32,32,128]{3,2,1,0:T(8,128)(2,1)}, u32[]{:S(2)}, u32[]{:S(2)}) %collective-permute-start.10) | collective-permute-done | bytes 786464 | tf_op jit(solution)/shard_map/ppermute | solution.py:339
  86.4 1.3 collective-permute-start.11
  88.9 2.0 %collective-permute-start.17 = (f16[2,1040,128]{2,1,0:T(8,128)(2,1)}, f16[2,1040,128]{2,1,0:T(8,128)(2,1)}, u32[]{:S(2)}, u32[]{:S(2)}) collective-permute-start(f16[2,1040,128]{2,1,0:T(8,128)(2,1)} %convert_element_type.45), channel_id=1, source_target_pairs={{0,12},{1,13},{2,14},{3,15},{4,0},{5,1},{6,2},{7,3},{8,4},{9,5},{1... | collective-permute-start | bytes 1597448 | tf_op jit(solution)/shard_map/ppermute | solution.py:335
  90.9 1.0 copy-done.28
  91.9 3.2 %zterms.3 = (f32[2,1040,128]{2,1,0:T(8,128)S(1)}, f32[2,1040,128]{2,1,0:T(8,128)S(1)}, f32[2,1040,128]{2,1,0:T(8,128)S(1)}, f32[2,1040,128]{2,1,0:T(8,128)S(1)}) custom-call(bf16[256,512]{1,0:T(8,128)(2,1)S(1)} %get-tuple-element.68.refs_0_, bf16[64,32,128]{2,1,0:T(8,128)(2,1)S(1)} %get-tuple-element.51.after_ref.refs_1_, ...), custom_call_target="tpu_custom_call" | custom-call | flops 20000000000 | bytes 8192 | tf_op jit(solution)/shard_map/zterms/pallas_call | solution.py:210
  95.1 1.0 convert_element_type.47
  97.1 1.9 %collective-permute-start.13 = (f16[2,1040,128]{2,1,0:T(8,128)(2,1)}, f16[2,1040,128]{2,1,0:T(8,128)(2,1)}, u32[]{:S(2)}, u32[]{:S(2)}) collective-permute-start(f16[2,1040,128]{2,1,0:T(8,128)(2,1)} %convert_element_type.48), channel_id=1, source_target_pairs={{0,8},{1,9},{2,10},{3,11},{4,12},{5,13},{6,14},{7,15},{8,0},{9,1},... | collective-permute-start | bytes 1597448 | tf_op jit(solution)/shard_map/ppermute | solution.py:335
  99.0 0.9 convert_element_type.49
  99.9 14.5 %collective-permute-done.15 = f16[2,1040,128]{2,1,0:T(8,128)(2,1)S(1)} collective-permute-done((f16[2,1040,128]{2,1,0:T(8,128)(2,1)}, f16[2,1040,128]{2,1,0:T(8,128)(2,1)S(1)}, u32[]{:S(2)}, u32[]{:S(2)}) %collective-permute-start.15) | collective-permute-done | bytes 532512 | tf_op jit(solution)/shard_map/ppermute | solution.py:335
  116.0 1.1 convert_element_type.53.p1
  117.1 2.1 %convert_element_type.54.p2 = f32[2,1040,128]{2,1,0:T(8,128)} convert(f16[2,1040,128]{2,1,0:T(8,128)(2,1)} %collective-permute-done.16) | non-fusion elementwise | flops 266240 | bytes 1597440 | tf_op jit(solution)/shard_map/convert_element_type | solution.py:396
  119.2 2.1 %convert_element_type.55.p3 = f32[2,1040,128]{2,1,0:T(8,128)} convert(f16[2,1040,128]{2,1,0:T(8,128)(2,1)} %collective-permute-done.17) | non-fusion elementwise | flops 266240 | bytes 1597440 | tf_op jit(solution)/shard_map/convert_element_type | solution.py:396
  121.3 11.2 %all-to-all-done.1 = f16[8,2064,128]{2,1,0:T(8,128)(2,1)} async-done(((f16[8,2064,128]{2,1,0:T(8,128)(2,1)}), f16[8,2064,128]{2,1,0:T(8,128)(2,1)}, u32[]{:S(2)}, u32[]{:S(2)}) %all-to-all-start.1) | async-done | bytes 4227104 | tf_op jit(solution)/shard_map/all_to_all | solution.py:393
  132.5 2.9 %convert_element_type.46.p_ref.c_ref.e_ref = f32[8,2064,128]{2,1,0:T(8,128)S(1)} convert(f16[8,2064,128]{2,1,0:T(8,128)(2,1)} %all-to-all-done.1) | non-fusion elementwise | flops 2113536 | bytes 12681216 | tf_op jit(solution)/shard_map/convert_element_type | solution.py:395
  135.4 1.2 copy-done.5
  136.6 2.9 %addy.1.part_ref = f32[64,32,512]{2,1,0:T(8,128)S(1)} custom-call(f32[64,32,512]{2,1,0:T(8,128)S(1)} %copy-done.5, bf16[64,32,512]{2,1,0:T(8,128)(2,1)S(1)} %copy-done.3, f32[8,2064,128]{2,1,0:T(8,128)S(1)} %convert_element_type.46.p_ref.c_ref.e_ref, f32[8,2064,128]{2,1,0:T(8,128)S(1)} %convert_element_type.46.p_ref.c_ref.e_ref, ...), custom_call_target="tpu_custom_call" | custom-call | tf_op jit(solution)/shard_map/addy/pallas_call | solution.py:317
  139.5 1.3 convert_element_type.50.p1
  140.8 1.2 convert_element_type.51.p2
  142.1 1.1 convert_element_type.52.p3
  143.3 2.9 %last.2 = (f32[64,32,512]{2,1,0:T(8,128)}, bf16[64,32,512]{2,1,0:T(8,128)(2,1)}) custom-call(s32[2]{0:T(128)S(1)} %pad_add_fusion.at, bf16[64,32,512]{2,1,0:T(8,128)(2,1)S(1)} %copy-done.1, f32[64,32,512]{2,1,0:T(8,128)S(1)} %addy.1.part_ref, bf16[64,32,512]{2,1,0:T(8,128)(2,1)S(1)} %copy-done.7, bf16[64,32,512]{2,1,0:T(8,128)(2,1)S(1)} %copy-done.3, ...), custom_call_target="tpu_custom_call" | custom-call | tf_op jit(solution)/shard_map/last/pallas_call | solution.py:270
  146.2 2.9 %last.3 = (f32[64,32,512]{2,1,0:T(8,128)}, bf16[64,32,512]{2,1,0:T(8,128)(2,1)}) custom-call(s32[2]{0:T(128)S(1)} %pad_add_fusion.at, bf16[64,32,512]{2,1,0:T(8,128)(2,1)S(1)} %copy-done.1, f32[64,32,512]{2,1,0:T(8,128)S(1)} %addy.1.part_ref, bf16[64,32,512]{2,1,0:T(8,128)(2,1)S(1)} %copy-done.7, ...), custom_call_target="tpu_custom_call", output_to_operand_aliasing={{0}: (10, {}), {1}: (11, {})} | custom-call | tf_op jit(solution)/shard_map/last/pallas_call | solution.py:270
  (85 shorter events, 8.2 us)
Async XLA Ops:
  0.7 1.6 %copy-start = (bf16[64,32,512]{2,1,0:T(8,128)(2,1)S(1)}, bf16[64,32,512]{2,1,0:T(8,128)(2,1)}, u32[]{:S(2)}) copy-start(bf16[64,32,512]{2,1,0:T(8,128)(2,1)} %s_ref.9) | copy-start | bytes 6291460
  4.7 29.3 %collective-permute-start = (bf16[64,32,128]{2,1,0:T(8,128)(2,1)}, bf16[64,32,128]{2,1,0:T(8,128)(2,1)}, u32[]{:S(2)}, u32[]{:S(2)}) collective-permute-start(bf16[64,32,128]{2,1,0:T(8,128)(2,1)} %get-tuple-element.48), channel_id=1, source_target_pairs={{0,4},{1,5},{2,6},{3,7},{4,8},{5,9},{6,10},{7,11},{8,12},{9,13},{1... | collective-permute-start | bytes 1572872 | tf_op jit(solution)/shard_map/ppermute | solution.py:335
  7.2 26.9 %collective-permute-start.1 = (bf16[64,32,128]{2,1,0:T(8,128)(2,1)}, bf16[64,32,128]{2,1,0:T(8,128)(2,1)}, u32[]{:S(2)}, u32[]{:S(2)}) collective-permute-start(bf16[64,32,128]{2,1,0:T(8,128)(2,1)} %get-tuple-element.49), channel_id=1, source_target_pairs={{0,8},{1,9},{2,10},{3,11},{4,12},{5,13},{6,14},{7,15},{8,0},{9,1},... | collective-permute-start | bytes 1572872 | tf_op jit(solution)/shard_map/ppermute | solution.py:335
  10.5 23.6 %collective-permute-start.2 = (bf16[64,32,128]{2,1,0:T(8,128)(2,1)}, bf16[64,32,128]{2,1,0:T(8,128)(2,1)}, u32[]{:S(2)}, u32[]{:S(2)}) collective-permute-start(bf16[64,32,128]{2,1,0:T(8,128)(2,1)} %get-tuple-element.50), channel_id=1, source_target_pairs={{0,12},{1,13},{2,14},{3,15},{4,0},{5,1},{6,2},{7,3},{8,4},{9,5},{1... | collective-permute-start | bytes 1572872 | tf_op jit(solution)/shard_map/ppermute | solution.py:335
  11.2 22.9 %collective-permute-start.3 = (bf16[64,32,128]{2,1,0:T(8,128)(2,1)S(1)}, bf16[64,32,128]{2,1,0:T(8,128)(2,1)}, u32[]{:S(2)}, u32[]{:S(2)}) collective-permute-start(bf16[64,32,128]{2,1,0:T(8,128)(2,1)S(1)} %get-tuple-element.51.after_ref.refs_1_), channel_id=1, source_target_pairs={{0,2},{1,3},{2,0},{3,1},{4,6},{5,7},{6,4},{7,5},{8,10},{9,11},{10,... | collective-permute-start | bytes 1572872 | tf_op jit(solution)/shard_map/ppermute | solution.py:339
  13.2 1.3 copy-start.6
  14.5 6.6 %copy-start.1 = (bf16[64,32,512]{2,1,0:T(8,128)(2,1)S(1)}, bf16[64,32,512]{2,1,0:T(8,128)(2,1)}, u32[]{:S(2)}) copy-start(bf16[64,32,512]{2,1,0:T(8,128)(2,1)} %s_ref.9) | copy-start | bytes 6291460
  14.5 6.6 %copy-start.21 = (bf16[512,512]{1,0:T(8,128)(2,1)S(1)}, bf16[512,512]{1,0:T(8,128)(2,1)}, u32[]{:S(2)}) copy-start(bf16[512,512]{1,0:T(8,128)(2,1)} %first_ref.3) | copy-start | bytes 1572868
  14.5 6.6 %copy-start.29 = (f32[512]{0:T(512)S(1)}, f32[512]{0:T(512)}, u32[]{:S(2)}) copy-start(f32[512]{0:T(512)} %param.21) | copy-start | bytes 6148
  14.5 33.7 %all-to-all-start = ((bf16[8,64,16,128]{3,2,1,0:T(8,128)(2,1)}), bf16[8,64,16,128]{3,2,1,0:T(8,128)(2,1)}, u32[]{:S(2)}, u32[]{:S(2)}) async-start(bf16[8,64,16,128]{3,2,1,0:T(8,128)(2,1)} %copy-done.6), calls=%async_computation | async-start | bytes 4194304 | tf_op jit(solution)/shard_map/all_to_all | solution.py:365
  21.1 1.6 %copy-start.2 = (bf16[64,32,512]{2,1,0:T(8,128)(2,1)S(1)}, bf16[64,32,512]{2,1,0:T(8,128)(2,1)}, u32[]{:S(2)}) copy-start(bf16[64,32,512]{2,1,0:T(8,128)(2,1)} %diff_ref.7) | copy-start | bytes 6291460
  22.7 2.2 %copy-start.10 = (f32[64,32,512]{2,1,0:T(8,128)S(1)}, f32[64,32,512]{2,1,0:T(8,128)}, u32[]{:S(2)}) copy-start(f32[64,32,512]{2,1,0:T(8,128)} %reg_ref.1) | copy-start | bytes 12582916
  24.9 1.6 %copy-start.11 = (bf16[64,32,512]{2,1,0:T(8,128)(2,1)S(1)}, bf16[64,32,512]{2,1,0:T(8,128)(2,1)}, u32[]{:S(2)}) copy-start(bf16[64,32,512]{2,1,0:T(8,128)(2,1)} %drift_ref.3) | copy-start | bytes 6291460
  27.5 4.5 %copy-start.12 = (bf16[512,32,64]{0,2,1:T(8,128)(2,1)S(1)}, bf16[512,32,64]{0,2,1:T(8,128)(2,1)}, u32[]{:S(2)}) copy-start(bf16[512,32,64]{0,2,1:T(8,128)(2,1)} %param.18) | copy-start | bytes 6291460
  27.5 4.5 %copy-start.23 = (bf16[512,512]{1,0:T(8,128)(2,1)S(1)}, bf16[512,512]{1,0:T(8,128)(2,1)}, u32[]{:S(2)}) copy-start(bf16[512,512]{1,0:T(8,128)(2,1)} %first_ref.2) | copy-start | bytes 1572868
  27.5 4.5 %copy-start.24 = (bf16[512,512]{1,0:T(8,128)(2,1)S(1)}, bf16[512,512]{1,0:T(8,128)(2,1)}, u32[]{:S(2)}) copy-start(bf16[512,512]{1,0:T(8,128)(2,1)} %second_ref.2) | copy-start | bytes 1572868
  27.5 4.5 %copy-start.25 = (bf16[512,512]{1,0:T(8,128)(2,1)S(1)}, bf16[512,512]{1,0:T(8,128)(2,1)}, u32[]{:S(2)}) copy-start(bf16[512,512]{1,0:T(8,128)(2,1)} %first_y.1) | copy-start | bytes 1572868
  27.6 4.5 %copy-start.26 = (bf16[512,512]{1,0:T(8,128)(2,1)S(1)}, bf16[512,512]{1,0:T(8,128)(2,1)}, u32[]{:S(2)}) copy-start(bf16[512,512]{1,0:T(8,128)(2,1)} %second_y.1) | copy-start | bytes 1572868
  32.0 2.0 %copy-start.4 = (f32[64,32,512]{2,1,0:T(8,128)}, f32[64,32,512]{2,1,0:T(8,128)S(1)}, u32[]{:S(2)}) copy-start(f32[64,32,512]{2,1,0:T(8,128)S(1)} %xterms.1.part_ref) | copy-start | bytes 12582916
  34.0 3.7 %copy-start.13 = (bf16[32,64,512]{2,1,0:T(8,128)(2,1)}, bf16[32,64,512]{2,1,0:T(8,128)(2,1)S(1)}, u32[]{:S(2)}) copy-start(bf16[32,64,512]{2,1,0:T(8,128)(2,1)S(1)} %get-tuple-element.65.drift_ref) | copy-start | bytes 6291460
  34.0 3.7 %copy-start.19 = (bf16[1024,512]{1,0:T(8,128)(2,1)}, bf16[1024,512]{1,0:T(8,128)(2,1)S(1)}, u32[]{:S(2)}) copy-start(bf16[1024,512]{1,0:T(8,128)(2,1)S(1)} %get-tuple-element.66.ops_ref) | copy-start | bytes 3145732
  34.1 6.0 %copy-start.31 = (f32[512]{0:T(512)S(1)}, f32[512]{0:T(512)}, u32[]{:S(2)}) copy-start(f32[512]{0:T(512)} %param.22) | copy-start | bytes 6148
  37.8 24.8 %collective-permute-start.5 = (bf16[3,32,32,128]{3,2,1,0:T(8,128)(2,1)}, bf16[3,32,32,128]{3,2,1,0:T(8,128)(2,1)}, u32[]{:S(2)}, u32[]{:S(2)}) collective-permute-start(bf16[3,32,32,128]{3,2,1,0:T(8,128)(2,1)} %get-tuple-element.70.refs_5_), channel_id=1, source_target_pairs={{0,2},{1,3},{2,0},{3,1},{4,6},{5,7},{6,4},{7,5},{8,10},{9,11},{10,... | collective-permute-start | bytes 2359304 | tf_op jit(solution)/shard_map/ppermute | solution.py:339
  37.8 24.8 %collective-permute-start.4 = (bf16[3,32,32,128]{3,2,1,0:T(8,128)(2,1)}, bf16[3,32,32,128]{3,2,1,0:T(8,128)(2,1)}, u32[]{:S(2)}, u32[]{:S(2)}) collective-permute-start(bf16[3,32,32,128]{3,2,1,0:T(8,128)(2,1)} %get-tuple-element.70.refs_5_), channel_id=1, source_target_pairs={{0,1},{1,0},{2,3},{3,2},{4,5},{5,4},{6,7},{7,6},{8,9},{9,8},{10,11... | collective-permute-start | bytes 2359304 | tf_op jit(solution)/shard_map/ppermute | solution.py:339
  48.2 1.6 %copy-start.14 = (bf16[32,64,512]{2,1,0:T(8,128)(2,1)S(1)}, bf16[32,64,512]{2,1,0:T(8,128)(2,1)}, u32[]{:S(2)}) copy-start(bf16[32,64,512]{2,1,0:T(8,128)(2,1)} %copy-done.13) | copy-start | bytes 6291460
  62.5 7.6 %collective-permute-start.8 = (bf16[3,32,32,128]{3,2,1,0:T(8,128)(2,1)}, bf16[3,32,32,128]{3,2,1,0:T(8,128)(2,1)S(1)}, u32[]{:S(2)}, u32[]{:S(2)}) collective-permute-start(bf16[3,32,32,128]{3,2,1,0:T(8,128)(2,1)} %collective-permute-done.5.refs_7_), channel_id=1, source_target_pairs={{0,1},{1,0},{2,3},{3,2},{4,5},{5,4},{6,7},{7,6},{8,9},{9,8},{10,11... | collective-permute-start | bytes 2359304 | tf_op jit(solution)/shard_map/ppermute | solution.py:339
  66.5 3.3 %collective-permute-start.6 = (bf16[64,32,128]{2,1,0:T(8,128)(2,1)S(1)}, bf16[64,32,128]{2,1,0:T(8,128)(2,1)S(1)}, u32[]{:S(2)}, u32[]{:S(2)}) collective-permute-start(bf16[64,32,128]{2,1,0:T(8,128)(2,1)S(1)} %get-tuple-element.51.after_ref.refs_1_), channel_id=1, source_target_pairs={{0,1},{1,0},{2,3},{3,2},{4,5},{5,4},{6,7},{7,6},{8,9},{9,8},{10,11... | collective-permute-start | bytes 1572872 | tf_op jit(solution)/shard_map/ppermute | solution.py:339
  66.6 3.5 %collective-permute-start.7 = (bf16[64,32,128]{2,1,0:T(8,128)(2,1)}, bf16[64,32,128]{2,1,0:T(8,128)(2,1)S(1)}, u32[]{:S(2)}, u32[]{:S(2)}) collective-permute-start(bf16[64,32,128]{2,1,0:T(8,128)(2,1)} %collective-permute-done.3.refs_3_), channel_id=1, source_target_pairs={{0,1},{1,0},{2,3},{3,2},{4,5},{5,4},{6,7},{7,6},{8,9},{9,8},{10,11... | collective-permute-start | bytes 1572872 | tf_op jit(solution)/shard_map/ppermute | solution.py:339
  67.0 19.4 %collective-permute-start.10 = (bf16[3,32,32,128]{3,2,1,0:T(8,128)(2,1)}, bf16[3,32,32,128]{3,2,1,0:T(8,128)(2,1)}, u32[]{:S(2)}, u32[]{:S(2)}) collective-permute-start(bf16[3,32,32,128]{3,2,1,0:T(8,128)(2,1)} %get-tuple-element.78.refs_5_), channel_id=1, source_target_pairs={{0,2},{1,3},{2,0},{3,1},{4,6},{5,7},{6,4},{7,5},{8,10},{9,11},{10,... | collective-permute-start | bytes 2359304 | tf_op jit(solution)/shard_map/ppermute | solution.py:339
  70.1 3.5 %copy-start.27 = (bf16[64,32,128]{2,1,0:T(8,128)(2,1)}, bf16[64,32,128]{2,1,0:T(8,128)(2,1)S(1)}, u32[]{:S(2)}) copy-start(bf16[64,32,128]{2,1,0:T(8,128)(2,1)S(1)} %collective-permute-done.7.refs_4_) | copy-start | bytes 1572868
  73.6 2.7 %copy-start.15 = (f32[2,1040,128]{2,1,0:T(8,128)}, f32[2,1040,128]{2,1,0:T(8,128)S(1)}, u32[]{:S(2)}) copy-start(f32[2,1040,128]{2,1,0:T(8,128)S(1)} %get-tuple-element.88.p0) | copy-start | bytes 3194884
  76.3 56.2 %all-to-all-start.1 = ((f16[8,2064,128]{2,1,0:T(8,128)(2,1)}), f16[8,2064,128]{2,1,0:T(8,128)(2,1)}, u32[]{:S(2)}, u32[]{:S(2)}) async-start(f16[8,2064,128]{2,1,0:T(8,128)(2,1)} %convert_element_type.42), calls=%async_computation.1 | async-start | bytes 8454144 | tf_op jit(solution)/shard_map/all_to_all | solution.py:393
  81.6 9.2 %collective-permute-start.9 = (bf16[3,32,32,128]{3,2,1,0:T(8,128)(2,1)}, bf16[3,32,32,128]{3,2,1,0:T(8,128)(2,1)S(1)}, u32[]{:S(2)}, u32[]{:S(2)}) collective-permute-start(bf16[3,32,32,128]{3,2,1,0:T(8,128)(2,1)} %get-tuple-element.78.refs_5_), channel_id=1, source_target_pairs={{0,1},{1,0},{2,3},{3,2},{4,5},{5,4},{6,7},{7,6},{8,9},{9,8},{10,11... | collective-permute-start | bytes 2359304 | tf_op jit(solution)/shard_map/ppermute | solution.py:339
  86.4 4.5 %collective-permute-start.11 = (bf16[3,32,32,128]{3,2,1,0:T(8,128)(2,1)}, bf16[3,32,32,128]{3,2,1,0:T(8,128)(2,1)S(1)}, u32[]{:S(2)}, u32[]{:S(2)}) collective-permute-start(bf16[3,32,32,128]{3,2,1,0:T(8,128)(2,1)} %collective-permute-done.10.refs_7_), channel_id=1, source_target_pairs={{0,1},{1,0},{2,3},{3,2},{4,5},{5,4},{6,7},{7,6},{8,9},{9,8},{10,11... | collective-permute-start | bytes 2359304 | tf_op jit(solution)/shard_map/ppermute | solution.py:339
  87.7 26.7 %collective-permute-start.15 = (f16[2,1040,128]{2,1,0:T(8,128)(2,1)}, f16[2,1040,128]{2,1,0:T(8,128)(2,1)S(1)}, u32[]{:S(2)}, u32[]{:S(2)}) collective-permute-start(f16[2,1040,128]{2,1,0:T(8,128)(2,1)} %convert_element_type.43), channel_id=1, source_target_pairs={{0,4},{1,5},{2,6},{3,7},{4,8},{5,9},{6,10},{7,11},{8,12},{9,13},{1... | collective-permute-start | bytes 1597448 | tf_op jit(solution)/shard_map/ppermute | solution.py:335
  88.5 28.6 %collective-permute-start.16 = (f16[2,1040,128]{2,1,0:T(8,128)(2,1)}, f16[2,1040,128]{2,1,0:T(8,128)(2,1)}, u32[]{:S(2)}, u32[]{:S(2)}) collective-permute-start(f16[2,1040,128]{2,1,0:T(8,128)(2,1)} %convert_element_type.44), channel_id=1, source_target_pairs={{0,8},{1,9},{2,10},{3,11},{4,12},{5,13},{6,14},{7,15},{8,0},{9,1},... | collective-permute-start | bytes 1597448 | tf_op jit(solution)/shard_map/ppermute | solution.py:335
  88.9 30.3 %collective-permute-start.17 = (f16[2,1040,128]{2,1,0:T(8,128)(2,1)}, f16[2,1040,128]{2,1,0:T(8,128)(2,1)}, u32[]{:S(2)}, u32[]{:S(2)}) collective-permute-start(f16[2,1040,128]{2,1,0:T(8,128)(2,1)} %convert_element_type.45), channel_id=1, source_target_pairs={{0,12},{1,13},{2,14},{3,15},{4,0},{5,1},{6,2},{7,3},{8,4},{9,5},{1... | collective-permute-start | bytes 1597448 | tf_op jit(solution)/shard_map/ppermute | solution.py:335
  95.1 4.8 %copy-start.17 = (f32[2,1040,128]{2,1,0:T(8,128)}, f32[2,1040,128]{2,1,0:T(8,128)S(1)}, u32[]{:S(2)}) copy-start(f32[2,1040,128]{2,1,0:T(8,128)S(1)} %get-tuple-element.84.p0) | copy-start | bytes 3194884
  96.1 43.4 %collective-permute-start.12 = (f16[2,1040,128]{2,1,0:T(8,128)(2,1)}, f16[2,1040,128]{2,1,0:T(8,128)(2,1)}, u32[]{:S(2)}, u32[]{:S(2)}) collective-permute-start(f16[2,1040,128]{2,1,0:T(8,128)(2,1)} %convert_element_type.47), channel_id=1, source_target_pairs={{0,4},{1,5},{2,6},{3,7},{4,8},{5,9},{6,10},{7,11},{8,12},{9,13},{1... | collective-permute-start | bytes 1597448 | tf_op jit(solution)/shard_map/ppermute | solution.py:335
  97.1 42.4 %collective-permute-start.13 = (f16[2,1040,128]{2,1,0:T(8,128)(2,1)}, f16[2,1040,128]{2,1,0:T(8,128)(2,1)}, u32[]{:S(2)}, u32[]{:S(2)}) collective-permute-start(f16[2,1040,128]{2,1,0:T(8,128)(2,1)} %convert_element_type.48), channel_id=1, source_target_pairs={{0,8},{1,9},{2,10},{3,11},{4,12},{5,13},{6,14},{7,15},{8,0},{9,1},... | collective-permute-start | bytes 1597448 | tf_op jit(solution)/shard_map/ppermute | solution.py:335
  115.2 24.3 %collective-permute-start.14 = (f16[2,1040,128]{2,1,0:T(8,128)(2,1)}, f16[2,1040,128]{2,1,0:T(8,128)(2,1)}, u32[]{:S(2)}, u32[]{:S(2)}) collective-permute-start(f16[2,1040,128]{2,1,0:T(8,128)(2,1)} %convert_element_type.49), channel_id=1, source_target_pairs={{0,12},{1,13},{2,14},{3,15},{4,0},{5,1},{6,2},{7,3},{8,4},{9,5},{1... | collective-permute-start | bytes 1597448 | tf_op jit(solution)/shard_map/ppermute | solution.py:335
  132.5 2.9 %copy-start.3 = (bf16[64,32,512]{2,1,0:T(8,128)(2,1)S(1)}, bf16[64,32,512]{2,1,0:T(8,128)(2,1)}, u32[]{:S(2)}) copy-start(bf16[64,32,512]{2,1,0:T(8,128)(2,1)} %diff_ref.7) | copy-start | bytes 6291460
  132.5 4.1 %copy-start.5 = (f32[64,32,512]{2,1,0:T(8,128)S(1)}, f32[64,32,512]{2,1,0:T(8,128)}, u32[]{:S(2)}) copy-start(f32[64,32,512]{2,1,0:T(8,128)} %copy-done.4) | copy-start | bytes 12582916
  136.6 6.7 %copy-start.16 = (f32[2,1040,128]{2,1,0:T(8,128)S(1)}, f32[2,1040,128]{2,1,0:T(8,128)}, u32[]{:S(2)}) copy-start(f32[2,1040,128]{2,1,0:T(8,128)} %copy-done.15) | copy-start | bytes 3194884
  139.5 3.7 %copy-start.7 = (bf16[64,32,512]{2,1,0:T(8,128)(2,1)S(1)}, bf16[64,32,512]{2,1,0:T(8,128)(2,1)}, u32[]{:S(2)}) copy-start(bf16[64,32,512]{2,1,0:T(8,128)(2,1)} %drift_ref.5) | copy-start | bytes 6291460
  139.5 3.7 %copy-start.8 = (f32[2,1040,128]{2,1,0:T(8,128)S(1)}, f32[2,1040,128]{2,1,0:T(8,128)}, u32[]{:S(2)}) copy-start(f32[2,1040,128]{2,1,0:T(8,128)} %convert_element_type.54.p2) | copy-start | bytes 3194884
  139.5 3.7 %copy-start.9 = (f32[2,1040,128]{2,1,0:T(8,128)S(1)}, f32[2,1040,128]{2,1,0:T(8,128)}, u32[]{:S(2)}) copy-start(f32[2,1040,128]{2,1,0:T(8,128)} %convert_element_type.55.p3) | copy-start | bytes 3194884
  143.3 2.9 %copy-start.18 = (f32[2,1040,128]{2,1,0:T(8,128)S(1)}, f32[2,1040,128]{2,1,0:T(8,128)}, u32[]{:S(2)}) copy-start(f32[2,1040,128]{2,1,0:T(8,128)} %copy-done.17) | copy-start | bytes 3194884
  (4 other events, 4.1 us)

commit v4 on v3

--- a/solution.py
+++ b/solution.py
@@ -250,42 +250,51 @@
     )(scalar, reg, drift, diff, first, second, metric)
 
 
-def last_kernel(at, s_ref, part_ref, drift_ref, diff_ref, metric_ref, p0, p1, p2, p3, *refs):
-    reg_ref, out_ref = refs[-2:]
+def last_kernel(at, s_ref, part_ref, drift_ref, diff_ref, metric_ref, *refs):
+    pieces, (reg_ref, out_ref) = refs[:-2], refs[-2:]
     metric = metric_ref[...][None]
-    for t, piece in enumerate((p0, p1, p2, p3)):
-        lanes = pl.ds(pl.multiple_of(lax.rem(at[0] + 4 - t, 4) * 128, 128), 128)
-        scale = jnp.exp2(piece[0, PIECE : PIECE + 1, :] - 13.0)
-        value = (piece[0, 0:PIECE, :] * scale).reshape(YB, 2, NK, 128)
-        term = (drift_ref[:, :, lanes].astype(F32) * metric) * value[:, 0]
-        term = term + (diff_ref[:, :, lanes].astype(F32) * (metric * metric)) * value[:, 1]
-        reg = part_ref[:, :, lanes] + 0.5 * term
-        reg_ref[:, :, lanes] = reg
-        out_ref[:, :, lanes] = (s_ref[:, :, lanes].astype(F32) + (15.0 / 16.0) * reg).astype(BF16)
-
-
-def last_terms(at, h, scalar, part, drift, diff, metric, pieces, done):
-    n = HJ // YB
-    field = pl.BlockSpec((YB, NK, NI), lambda j, at: (n * h + j, 0, 0))
+
+    def finish(pieces):
+        for t, piece in enumerate(pieces):
+            lanes = pl.ds(pl.multiple_of(lax.rem(at[0] + 4 - t, 4) * 128, 128), 128)
+            scale = jnp.exp2(piece[0, PIECE : PIECE + 1, :] - 13.0)
+            value = (piece[0, 0:PIECE, :] * scale).reshape(YB, 2, NK, 128)
+            term = (drift_ref[:, :, lanes].astype(F32) * metric) * value[:, 0]
+            term = term + (diff_ref[:, :, lanes].astype(F32) * (metric * metric)) * value[:, 1]
+            reg = part_ref[:, :, lanes] + 0.5 * term
+            reg_ref[:, :, lanes] = reg
+            out_ref[:, :, lanes] = (s_ref[:, :, lanes].astype(F32) + (15.0 / 16.0) * reg).astype(BF16)
+
+    for h in range(HALVES):
+
+        @pl.when(pl.program_id(0) // (HJ // YB) == h)
+        def _():
+            finish(pieces[4 * h : 4 * (h + 1)])
+
+
+def last_terms(at, scalar, part, drift, diff, metric, pieces):
+    m = HJ // YB
+    field = pl.BlockSpec((YB, NK, NI), lambda j, at: (j, 0, 0))
+    specs = []
+    for h in range(HALVES):
+        specs += [
+            pl.BlockSpec((1, PIECE + 16, 128), lambda j, at, h=h: (jnp.clip(j - m * h, 0, m - 1), 0, 0))
+        ] * 4
     return pl.pallas_call(
         last_kernel,
         grid_spec=pltpu.PrefetchScalarGridSpec(
             num_scalar_prefetch=1,
-            grid=(n,),
-            in_specs=[field] * 4
-            + [pl.BlockSpec((NK, 128), lambda j, at: (0, 0))]
-            + [pl.BlockSpec((1, PIECE + 16, 128), lambda j, at: (j, 0, 0))] * 4
-            + [pl.BlockSpec(memory_space=pl.ANY)] * len(done),
+            grid=(NJ // YB,),
+            in_specs=[field] * 4 + [pl.BlockSpec((NK, 128), lambda j, at: (0, 0))] + specs,
             out_specs=[field, field],
         ),
         out_shape=[
             jax.ShapeDtypeStruct((NJ, NK, NI), F32),
             jax.ShapeDtypeStruct((NJ, NK, NI), BF16),
         ],
-        input_output_aliases={10 + i: i for i in range(len(done))},
         compiler_params=params(30),
         name="last",
-    )(at, scalar, part, drift, diff, metric, *pieces, *done)
+    )(at, scalar, part, drift, diff, metric, *pieces)
 
 
 def add_y_kernel(part_ref, diff_ref, p_ref, c_ref, e_ref, out_ref):
@@ -396,10 +405,9 @@
     z_back[0] = [z.astype(F32) for z in z_back[0]]
     part, z_back[1] = lax.optimization_barrier((part, z_back[1]))
     z_back[1] = [z.astype(F32) for z in z_back[1]]
-    done = ()
-    for h in range(HALVES):
-        done = last_terms(at, h, scalar, part, drift_z, diffusivity, own, z_back[h], done)
-    return tuple(done)
+    return tuple(
+        last_terms(at, scalar, part, drift_z, diffusivity, own, z_back[0] + z_back[1])
+    )
 
 
 def solution(mesh):

time: 150 us -> 149 us (level)
    pallas_call x2 -> x1, Pallas kernels: 5.73 us -> 4.63 us  [last_terms(): pl.pallas_call(last_kernel, grid_spec=pltpu.PrefetchScalarGridSpec(num_sc...]
  transfers between devices with their start and end apart: 20 -> 20, of which waited for: 6 -> 6; matrix products, arithmetic and copies ran while one was open for 11% -> 12% of each run, Pallas kernels for 19% -> 19%
where the time goes in v4:
time: 149 us; the launch traced here: 148 us
  waiting for transfers between devices  40.7 us (27%)
  Pallas kernels  35.4 us (24%)
  starting transfers between devices  33.7 us (23%)
  other arithmetic  19.9 us (13%)
  local copies, waits for them, and re-layouts  17.2 us (12%)
    unnamed x64, local copies, waits for them, and re-layouts  16.2 us
    ppermute x9, waiting for transfers between devices, ring(): lax.ppermute(x, 'col', [(c, (c + 4 * shift) % 16) for c in range(16)])  14.5 us
    ppermute x9, starting transfers between devices, ring(): lax.ppermute(x, 'col', [(c, (c + 4 * shift) % 16) for c in range(16)])  11.7 us
    all_to_all x1, waiting for transfers between devices, on_device(): y_back = lax.all_to_all(y_out, 'row', 0, 0, tiled=False)  11.2 us
    ppermute x9, starting transfers between devices, flip(): return lax.ppermute(x, 'col', [(c, c ^ bits) for c in range(16)])  10.1 us
    pallas_call x1, Pallas kernels, y_terms(): pl.pallas_call(y_kernel, grid=(8,), in_specs=[pl.BlockSpec(memory_space=p...  9.01 us
    all_to_all x1, waiting for transfers between devices, on_device(): scalar_y = lax.all_to_all(pack(scalar, mine[0]), 'row', 0, 0, tiled=False)  7.95 us
    ppermute x9, waiting for transfers between devices, flip(): return lax.ppermute(x, 'col', [(c, c ^ bits) for c in range(16)])  7.05 us
  transfers between devices with their start and end apart: 20, of which 6 were waited for; matrix products, arithmetic and copies ran while one was open for 12% of the time, Pallas kernels for 19%

profile of v4, /device:TPU:1, one launch (start us, length us, event | category | flops | bytes accessed | tf_op | source)
XLA Modules:
  0.0 147.9 jit_solution(627194441190025807)
XLA Ops:
  0.7 1.6 %copy-done = bf16[64,32,512]{2,1,0:T(8,128)(2,1)S(1)} copy-done((bf16[64,32,512]{2,1,0:T(8,128)(2,1)S(1)}, bf16[64,32,512]{2,1,0:T(8,128)(2,1)}, u32[]{:S(2)}) %copy-start) | copy-done | bytes 2097176
  2.3 2.4 %cut.1 = (bf16[64,32,128]{2,1,0:T(8,128)(2,1)S(1)}, bf16[64,32,128]{2,1,0:T(8,128)(2,1)}, bf16[64,32,128]{2,1,0:T(8,128)(2,1)}, bf16[64,32,128]{2,1,0:T(8,128)(2,1)}) custom-call(s32[2]{0:T(128)S(1)} %pad_add_fusion.at, bf16[64,32,512]{2,1,0:T(8,128)(2,1)S(1)} %copy-done), custom_call_target="tpu_custom_call" | custom-call | tf_op jit(solution)/shard_map/cut/pallas_call | solution.py:40
  4.7 2.5 %collective-permute-start = (bf16[64,32,128]{2,1,0:T(8,128)(2,1)}, bf16[64,32,128]{2,1,0:T(8,128)(2,1)}, u32[]{:S(2)}, u32[]{:S(2)}) collective-permute-start(bf16[64,32,128]{2,1,0:T(8,128)(2,1)} %get-tuple-element.46), channel_id=1, source_target_pairs={{0,4},{1,5},{2,6},{3,7},{4,8},{5,9},{6,10},{7,11},{8,12},{9,13},{1... | collective-permute-start | bytes 1572872 | tf_op jit(solution)/shard_map/ppermute | solution.py:344
  7.2 3.3 %collective-permute-start.1 = (bf16[64,32,128]{2,1,0:T(8,128)(2,1)}, bf16[64,32,128]{2,1,0:T(8,128)(2,1)}, u32[]{:S(2)}, u32[]{:S(2)}) collective-permute-start(bf16[64,32,128]{2,1,0:T(8,128)(2,1)} %get-tuple-element.47), channel_id=1, source_target_pairs={{0,8},{1,9},{2,10},{3,11},{4,12},{5,13},{6,14},{7,15},{8,0},{9,1},... | collective-permute-start | bytes 1572872 | tf_op jit(solution)/shard_map/ppermute | solution.py:344
  11.2 1.2 collective-permute-start.3
  13.2 1.3 copy-done.6
  14.5 6.6 %all-to-all-start = ((bf16[8,64,16,128]{3,2,1,0:T(8,128)(2,1)}), bf16[8,64,16,128]{3,2,1,0:T(8,128)(2,1)}, u32[]{:S(2)}, u32[]{:S(2)}) async-start(bf16[8,64,16,128]{3,2,1,0:T(8,128)(2,1)} %copy-done.6), calls=%async_computation | async-start | bytes 4194304 | tf_op jit(solution)/shard_map/all_to_all | solution.py:374
  21.2 1.6 %copy-done.2 = bf16[64,32,512]{2,1,0:T(8,128)(2,1)S(1)} copy-done((bf16[64,32,512]{2,1,0:T(8,128)(2,1)S(1)}, bf16[64,32,512]{2,1,0:T(8,128)(2,1)}, u32[]{:S(2)}) %copy-start.2) | copy-done | bytes 2097176
  22.7 2.2 %copy-done.9 = f32[64,32,512]{2,1,0:T(8,128)S(1)} copy-done((f32[64,32,512]{2,1,0:T(8,128)S(1)}, f32[64,32,512]{2,1,0:T(8,128)}, u32[]{:S(2)}) %copy-start.9) | copy-done | bytes 4194328
  24.9 1.6 %copy-done.10 = bf16[64,32,512]{2,1,0:T(8,128)(2,1)S(1)} copy-done((bf16[64,32,512]{2,1,0:T(8,128)(2,1)S(1)}, bf16[64,32,512]{2,1,0:T(8,128)(2,1)}, u32[]{:S(2)}) %copy-start.10) | copy-done | bytes 2097176
  26.5 1.0 copy-done.22
  27.6 4.4 %xterms.1.part_ref = f32[64,32,512]{2,1,0:T(8,128)S(1)} custom-call(bf16[64,32,512]{2,1,0:T(8,128)(2,1)S(1)} %copy-done.1, f32[64,32,512]{2,1,0:T(8,128)S(1)} %copy-done.9, bf16[64,32,512]{2,1,0:T(8,128)(2,1)S(1)} %copy-done.10, bf16[64,32,512]{2,1,0:T(8,128)(2,1)S(1)} %copy-done.2, bf16[512,512]{1,0:T(8,128)(2,1)S(1)} %copy-done.21, ...), custom_call_target="tpu_custom_call" | custom-call | flops 1000 | bytes 8192 | tf_op jit(solution)/shard_map/xterms/pallas_call | solution.py:241
  32.1 1.0 operator.1
  33.1 1.0 copy-done.4
  34.1 3.7 %merge.1 = (bf16[3,32,32,128]{3,2,1,0:T(8,128)(2,1)}, bf16[3,32,32,128]{3,2,1,0:T(8,128)(2,1)}) custom-call(bf16[64,32,128]{2,1,0:T(8,128)(2,1)} %collective-permute-done.r1, bf16[64,32,128]{2,1,0:T(8,128)(2,1)} %collective-permute-done.1.r2, bf16[64,32,128]{2,1,0:T(8,128)(2,1)} %collective-permute-done.2.r3), custom_call_target="tpu_custom_call" | custom-call | flops 20000000000 | bytes 3145728 | tf_op jit(solution)/shard_map/merge/pallas_call | solution.py:70
  37.8 2.3 %collective-permute-start.4 = (bf16[3,32,32,128]{3,2,1,0:T(8,128)(2,1)}, bf16[3,32,32,128]{3,2,1,0:T(8,128)(2,1)}, u32[]{:S(2)}, u32[]{:S(2)}) collective-permute-start(bf16[3,32,32,128]{3,2,1,0:T(8,128)(2,1)} %get-tuple-element.68.refs_5_), channel_id=1, source_target_pairs={{0,1},{1,0},{2,3},{3,2},{4,5},{5,4},{6,7},{7,6},{8,9},{9,8},{10,11... | collective-permute-start | bytes 2359304 | tf_op jit(solution)/shard_map/ppermute | solution.py:348
  40.2 7.9 %all-to-all-done.s_ref = bf16[8,64,16,128]{3,2,1,0:T(8,128)(2,1)} async-done(((bf16[8,64,16,128]{3,2,1,0:T(8,128)(2,1)}), bf16[8,64,16,128]{3,2,1,0:T(8,128)(2,1)}, u32[]{:S(2)}, u32[]{:S(2)}) %all-to-all-start) | async-done | bytes 2097184 | tf_op jit(solution)/shard_map/all_to_all | solution.py:374
  48.2 1.6 %copy-done.14 = bf16[32,64,512]{2,1,0:T(8,128)(2,1)S(1)} copy-done((bf16[32,64,512]{2,1,0:T(8,128)(2,1)S(1)}, bf16[32,64,512]{2,1,0:T(8,128)(2,1)}, u32[]{:S(2)}) %copy-start.14) | copy-done | bytes 2097176
  49.8 1.2 copy-done.20
  51.0 9.0 %yterms.1 = f32[8,2064,128]{2,1,0:T(8,128)S(1)} custom-call(s32[1]{0:T(128)} %bitcast.4.odd_ref, bf16[8,64,16,128]{3,2,1,0:T(8,128)(2,1)} %all-to-all-done.s_ref, bf16[32,64,512]{2,1,0:T(8,128)(2,1)S(1)} %copy-done.14, bf16[1024,512]{1,0:T(8,128)(2,1)S(1)} %copy-done.20, f32[512,1]{1,0:T(8,128)S(1)} %copy.17.metric_ref), custom_call_target="tpu_custom_call" | custom-call | flops 1000 | bytes 8192 | tf_op jit(solution)/shard_map/yterms/pallas_call | solution.py:166
  60.0 2.6 %convert_element_type.42 = f16[8,2064,128]{2,1,0:T(8,128)(2,1)} convert(f32[8,2064,128]{2,1,0:T(8,128)S(1)} %yterms.1) | non-fusion elementwise | flops 2113536 | bytes 12681216 | tf_op jit(solution)/shard_map/convert_element_type | solution.py:386
  62.6 3.9 %collective-permute-start.8 = (bf16[3,32,32,128]{3,2,1,0:T(8,128)(2,1)}, bf16[3,32,32,128]{3,2,1,0:T(8,128)(2,1)S(1)}, u32[]{:S(2)}, u32[]{:S(2)}) collective-permute-start(bf16[3,32,32,128]{3,2,1,0:T(8,128)(2,1)} %collective-permute-done.5.refs_7_), channel_id=1, source_target_pairs={{0,1},{1,0},{2,3},{3,2},{4,5},{5,4},{6,7},{7,6},{8,9},{9,8},{10,11... | collective-permute-start | bytes 2359304 | tf_op jit(solution)/shard_map/ppermute | solution.py:348
  67.2 2.6 %collective-permute-done.6.refs_2_ = bf16[64,32,128]{2,1,0:T(8,128)(2,1)S(1)} collective-permute-done((bf16[64,32,128]{2,1,0:T(8,128)(2,1)S(1)}, bf16[64,32,128]{2,1,0:T(8,128)(2,1)S(1)}, u32[]{:S(2)}, u32[]{:S(2)}) %collective-permute-start.6) | collective-permute-done | bytes 524320 | tf_op jit(solution)/shard_map/ppermute | solution.py:348
  70.1 3.5 %zterms.2 = (f32[2,1040,128]{2,1,0:T(8,128)S(1)}, f32[2,1040,128]{2,1,0:T(8,128)S(1)}, f32[2,1040,128]{2,1,0:T(8,128)S(1)}, f32[2,1040,128]{2,1,0:T(8,128)S(1)}) custom-call(bf16[256,512]{1,0:T(8,128)(2,1)S(1)} %get-tuple-element.66.refs_0_, bf16[64,32,128]{2,1,0:T(8,128)(2,1)S(1)} %get-tuple-element.49.after_ref.refs_1_, ...), custom_call_target="tpu_custom_call" | custom-call | flops 1000 | bytes 8192 | tf_op jit(solution)/shard_map/zterms/pallas_call | solution.py:210
  73.6 1.0 convert_element_type.43
  74.6 0.9 convert_element_type.44
  76.4 5.3 %all-to-all-start.1 = ((f16[8,2064,128]{2,1,0:T(8,128)(2,1)}), f16[8,2064,128]{2,1,0:T(8,128)(2,1)}, u32[]{:S(2)}, u32[]{:S(2)}) async-start(f16[8,2064,128]{2,1,0:T(8,128)(2,1)} %convert_element_type.42), calls=%async_computation.1 | async-start | bytes 8454144 | tf_op jit(solution)/shard_map/all_to_all | solution.py:402
  82.3 4.1 %collective-permute-done.10.refs_7_ = bf16[3,32,32,128]{3,2,1,0:T(8,128)(2,1)} collective-permute-done((bf16[3,32,32,128]{3,2,1,0:T(8,128)(2,1)}, bf16[3,32,32,128]{3,2,1,0:T(8,128)(2,1)}, u32[]{:S(2)}, u32[]{:S(2)}) %collective-permute-start.10) | collective-permute-done | bytes 786464 | tf_op jit(solution)/shard_map/ppermute | solution.py:348
  86.4 1.3 collective-permute-start.11
  88.9 1.9 %collective-permute-start.17 = (f16[2,1040,128]{2,1,0:T(8,128)(2,1)}, f16[2,1040,128]{2,1,0:T(8,128)(2,1)}, u32[]{:S(2)}, u32[]{:S(2)}) collective-permute-start(f16[2,1040,128]{2,1,0:T(8,128)(2,1)} %convert_element_type.45), channel_id=1, source_target_pairs={{0,12},{1,13},{2,14},{3,15},{4,0},{5,1},{6,2},{7,3},{8,4},{9,5},{1... | collective-permute-start | bytes 1597448 | tf_op jit(solution)/shard_map/ppermute | solution.py:344
  90.9 1.0 copy-done.28
  91.9 3.2 %zterms.3 = (f32[2,1040,128]{2,1,0:T(8,128)S(1)}, f32[2,1040,128]{2,1,0:T(8,128)S(1)}, f32[2,1040,128]{2,1,0:T(8,128)S(1)}, f32[2,1040,128]{2,1,0:T(8,128)S(1)}) custom-call(bf16[256,512]{1,0:T(8,128)(2,1)S(1)} %get-tuple-element.66.refs_0_, bf16[64,32,128]{2,1,0:T(8,128)(2,1)S(1)} %get-tuple-element.49.after_ref.refs_1_, ...), custom_call_target="tpu_custom_call" | custom-call | flops 20000000000 | bytes 8192 | tf_op jit(solution)/shard_map/zterms/pallas_call | solution.py:210
  95.1 1.0 convert_element_type.47
  96.2 0.9 convert_element_type.48
  97.1 1.9 %collective-permute-start.13 = (f16[2,1040,128]{2,1,0:T(8,128)(2,1)}, f16[2,1040,128]{2,1,0:T(8,128)(2,1)}, u32[]{:S(2)}, u32[]{:S(2)}) collective-permute-start(f16[2,1040,128]{2,1,0:T(8,128)(2,1)} %convert_element_type.48), channel_id=1, source_target_pairs={{0,8},{1,9},{2,10},{3,11},{4,12},{5,13},{6,14},{7,15},{8,0},{9,1},... | collective-permute-start | bytes 1597448 | tf_op jit(solution)/shard_map/ppermute | solution.py:344
  99.0 0.9 convert_element_type.49
  99.9 14.5 %collective-permute-done.15 = f16[2,1040,128]{2,1,0:T(8,128)(2,1)S(1)} collective-permute-done((f16[2,1040,128]{2,1,0:T(8,128)(2,1)}, f16[2,1040,128]{2,1,0:T(8,128)(2,1)S(1)}, u32[]{:S(2)}, u32[]{:S(2)}) %collective-permute-start.15) | collective-permute-done | bytes 532512 | tf_op jit(solution)/shard_map/ppermute | solution.py:344
  116.0 1.1 convert_element_type.50.refs_1_
  117.1 2.1 %convert_element_type.51.refs_2_ = f32[2,1040,128]{2,1,0:T(8,128)} convert(f16[2,1040,128]{2,1,0:T(8,128)(2,1)} %collective-permute-done.16) | non-fusion elementwise | flops 266240 | bytes 1597440 | tf_op jit(solution)/shard_map/convert_element_type | solution.py:405
  119.2 2.1 %convert_element_type.52.refs_3_ = f32[2,1040,128]{2,1,0:T(8,128)} convert(f16[2,1040,128]{2,1,0:T(8,128)(2,1)} %collective-permute-done.17) | non-fusion elementwise | flops 266240 | bytes 1597440 | tf_op jit(solution)/shard_map/convert_element_type | solution.py:405
  121.3 11.2 %all-to-all-done.1 = f16[8,2064,128]{2,1,0:T(8,128)(2,1)} async-done(((f16[8,2064,128]{2,1,0:T(8,128)(2,1)}), f16[8,2064,128]{2,1,0:T(8,128)(2,1)}, u32[]{:S(2)}, u32[]{:S(2)}) %all-to-all-start.1) | async-done | bytes 4227104 | tf_op jit(solution)/shard_map/all_to_all | solution.py:402
  132.5 2.9 %convert_element_type.46.p_ref.c_ref.e_ref = f32[8,2064,128]{2,1,0:T(8,128)S(1)} convert(f16[8,2064,128]{2,1,0:T(8,128)(2,1)} %all-to-all-done.1) | non-fusion elementwise | flops 2113536 | bytes 12681216 | tf_op jit(solution)/shard_map/convert_element_type | solution.py:404
  135.4 1.2 copy-done.5
  136.6 2.9 %addy.1.part_ref = f32[64,32,512]{2,1,0:T(8,128)S(1)} custom-call(f32[64,32,512]{2,1,0:T(8,128)S(1)} %copy-done.5, bf16[64,32,512]{2,1,0:T(8,128)(2,1)S(1)} %copy-done.3, f32[8,2064,128]{2,1,0:T(8,128)S(1)} %convert_element_type.46.p_ref.c_ref.e_ref, f32[8,2064,128]{2,1,0:T(8,128)S(1)} %convert_element_type.46.p_ref.c_ref.e_ref, ...), custom_call_target="tpu_custom_call" | custom-call | tf_op jit(solution)/shard_map/addy/pallas_call | solution.py:326
  139.6 1.3 convert_element_type.53.refs_5_
  140.8 1.2 convert_element_type.54.refs_6_
  142.1 1.1 convert_element_type.55.refs_7_
  143.3 4.6 %last.1 = (f32[64,32,512]{2,1,0:T(8,128)}, bf16[64,32,512]{2,1,0:T(8,128)(2,1)}) custom-call(s32[2]{0:T(128)S(1)} %pad_add_fusion.at, bf16[64,32,512]{2,1,0:T(8,128)(2,1)S(1)} %copy-done.1, f32[64,32,512]{2,1,0:T(8,128)S(1)} %addy.1.part_ref, bf16[64,32,512]{2,1,0:T(8,128)(2,1)S(1)} %copy-done.11, bf16[64,32,512]{2,1,0:T(8,128)(2,1)S(1)} %copy-done.3, ...), custom_call_target="tpu_custom_call" | custom-call | tf_op jit(solution)/shard_map/last/pallas_call | solution.py:283
  (84 shorter events, 7.3 us)
Async XLA Ops:
  0.7 1.6 %copy-start = (bf16[64,32,512]{2,1,0:T(8,128)(2,1)S(1)}, bf16[64,32,512]{2,1,0:T(8,128)(2,1)}, u32[]{:S(2)}) copy-start(bf16[64,32,512]{2,1,0:T(8,128)(2,1)} %s_ref.7) | copy-start | bytes 6291460
  4.7 29.3 %collective-permute-start = (bf16[64,32,128]{2,1,0:T(8,128)(2,1)}, bf16[64,32,128]{2,1,0:T(8,128)(2,1)}, u32[]{:S(2)}, u32[]{:S(2)}) collective-permute-start(bf16[64,32,128]{2,1,0:T(8,128)(2,1)} %get-tuple-element.46), channel_id=1, source_target_pairs={{0,4},{1,5},{2,6},{3,7},{4,8},{5,9},{6,10},{7,11},{8,12},{9,13},{1... | collective-permute-start | bytes 1572872 | tf_op jit(solution)/shard_map/ppermute | solution.py:344
  7.2 26.9 %collective-permute-start.1 = (bf16[64,32,128]{2,1,0:T(8,128)(2,1)}, bf16[64,32,128]{2,1,0:T(8,128)(2,1)}, u32[]{:S(2)}, u32[]{:S(2)}) collective-permute-start(bf16[64,32,128]{2,1,0:T(8,128)(2,1)} %get-tuple-element.47), channel_id=1, source_target_pairs={{0,8},{1,9},{2,10},{3,11},{4,12},{5,13},{6,14},{7,15},{8,0},{9,1},... | collective-permute-start | bytes 1572872 | tf_op jit(solution)/shard_map/ppermute | solution.py:344
  10.5 23.6 %collective-permute-start.2 = (bf16[64,32,128]{2,1,0:T(8,128)(2,1)}, bf16[64,32,128]{2,1,0:T(8,128)(2,1)}, u32[]{:S(2)}, u32[]{:S(2)}) collective-permute-start(bf16[64,32,128]{2,1,0:T(8,128)(2,1)} %get-tuple-element.48), channel_id=1, source_target_pairs={{0,12},{1,13},{2,14},{3,15},{4,0},{5,1},{6,2},{7,3},{8,4},{9,5},{1... | collective-permute-start | bytes 1572872 | tf_op jit(solution)/shard_map/ppermute | solution.py:344
  11.2 22.9 %collective-permute-start.3 = (bf16[64,32,128]{2,1,0:T(8,128)(2,1)S(1)}, bf16[64,32,128]{2,1,0:T(8,128)(2,1)}, u32[]{:S(2)}, u32[]{:S(2)}) collective-permute-start(bf16[64,32,128]{2,1,0:T(8,128)(2,1)S(1)} %get-tuple-element.49.after_ref.refs_1_), channel_id=1, source_target_pairs={{0,2},{1,3},{2,0},{3,1},{4,6},{5,7},{6,4},{7,5},{8,10},{9,11},{10,... | collective-permute-start | bytes 1572872 | tf_op jit(solution)/shard_map/ppermute | solution.py:348
  13.2 1.3 copy-start.6
  14.5 6.6 %copy-start.1 = (bf16[64,32,512]{2,1,0:T(8,128)(2,1)S(1)}, bf16[64,32,512]{2,1,0:T(8,128)(2,1)}, u32[]{:S(2)}) copy-start(bf16[64,32,512]{2,1,0:T(8,128)(2,1)} %s_ref.7) | copy-start | bytes 6291460
  14.5 6.6 %copy-start.21 = (bf16[512,512]{1,0:T(8,128)(2,1)S(1)}, bf16[512,512]{1,0:T(8,128)(2,1)}, u32[]{:S(2)}) copy-start(bf16[512,512]{1,0:T(8,128)(2,1)} %first_ref.3) | copy-start | bytes 1572868
  14.5 6.6 %copy-start.29 = (f32[512]{0:T(512)S(1)}, f32[512]{0:T(512)}, u32[]{:S(2)}) copy-start(f32[512]{0:T(512)} %param.21) | copy-start | bytes 6148
  14.5 33.7 %all-to-all-start = ((bf16[8,64,16,128]{3,2,1,0:T(8,128)(2,1)}), bf16[8,64,16,128]{3,2,1,0:T(8,128)(2,1)}, u32[]{:S(2)}, u32[]{:S(2)}) async-start(bf16[8,64,16,128]{3,2,1,0:T(8,128)(2,1)} %copy-done.6), calls=%async_computation | async-start | bytes 4194304 | tf_op jit(solution)/shard_map/all_to_all | solution.py:374
  21.1 1.6 %copy-start.2 = (bf16[64,32,512]{2,1,0:T(8,128)(2,1)S(1)}, bf16[64,32,512]{2,1,0:T(8,128)(2,1)}, u32[]{:S(2)}) copy-start(bf16[64,32,512]{2,1,0:T(8,128)(2,1)} %diff_ref.5) | copy-start | bytes 6291460
  22.7 2.2 %copy-start.9 = (f32[64,32,512]{2,1,0:T(8,128)S(1)}, f32[64,32,512]{2,1,0:T(8,128)}, u32[]{:S(2)}) copy-start(f32[64,32,512]{2,1,0:T(8,128)} %reg_ref.1) | copy-start | bytes 12582916
  24.9 1.6 %copy-start.10 = (bf16[64,32,512]{2,1,0:T(8,128)(2,1)S(1)}, bf16[64,32,512]{2,1,0:T(8,128)(2,1)}, u32[]{:S(2)}) copy-start(bf16[64,32,512]{2,1,0:T(8,128)(2,1)} %drift_ref.2) | copy-start | bytes 6291460
  27.6 4.5 %copy-start.12 = (bf16[512,32,64]{0,2,1:T(8,128)(2,1)S(1)}, bf16[512,32,64]{0,2,1:T(8,128)(2,1)}, u32[]{:S(2)}) copy-start(bf16[512,32,64]{0,2,1:T(8,128)(2,1)} %param.18) | copy-start | bytes 6291460
  27.6 4.5 %copy-start.23 = (bf16[512,512]{1,0:T(8,128)(2,1)S(1)}, bf16[512,512]{1,0:T(8,128)(2,1)}, u32[]{:S(2)}) copy-start(bf16[512,512]{1,0:T(8,128)(2,1)} %first_ref.2) | copy-start | bytes 1572868
  27.6 4.5 %copy-start.24 = (bf16[512,512]{1,0:T(8,128)(2,1)S(1)}, bf16[512,512]{1,0:T(8,128)(2,1)}, u32[]{:S(2)}) copy-start(bf16[512,512]{1,0:T(8,128)(2,1)} %second_ref.2) | copy-start | bytes 1572868
  27.6 4.5 %copy-start.25 = (bf16[512,512]{1,0:T(8,128)(2,1)S(1)}, bf16[512,512]{1,0:T(8,128)(2,1)}, u32[]{:S(2)}) copy-start(bf16[512,512]{1,0:T(8,128)(2,1)} %first_y.1) | copy-start | bytes 1572868
  27.6 4.5 %copy-start.26 = (bf16[512,512]{1,0:T(8,128)(2,1)S(1)}, bf16[512,512]{1,0:T(8,128)(2,1)}, u32[]{:S(2)}) copy-start(bf16[512,512]{1,0:T(8,128)(2,1)} %second_y.1) | copy-start | bytes 1572868
  32.0 2.0 %copy-start.4 = (f32[64,32,512]{2,1,0:T(8,128)}, f32[64,32,512]{2,1,0:T(8,128)S(1)}, u32[]{:S(2)}) copy-start(f32[64,32,512]{2,1,0:T(8,128)S(1)} %xterms.1.part_ref) | copy-start | bytes 12582916
  34.1 3.7 %copy-start.13 = (bf16[32,64,512]{2,1,0:T(8,128)(2,1)}, bf16[32,64,512]{2,1,0:T(8,128)(2,1)S(1)}, u32[]{:S(2)}) copy-start(bf16[32,64,512]{2,1,0:T(8,128)(2,1)S(1)} %get-tuple-element.63.drift_ref) | copy-start | bytes 6291460
  34.1 3.7 %copy-start.19 = (bf16[1024,512]{1,0:T(8,128)(2,1)}, bf16[1024,512]{1,0:T(8,128)(2,1)S(1)}, u32[]{:S(2)}) copy-start(bf16[1024,512]{1,0:T(8,128)(2,1)S(1)} %get-tuple-element.64.ops_ref) | copy-start | bytes 3145732
  34.1 6.0 %copy-start.31 = (f32[512]{0:T(512)S(1)}, f32[512]{0:T(512)}, u32[]{:S(2)}) copy-start(f32[512]{0:T(512)} %param.22) | copy-start | bytes 6148
  37.8 24.8 %collective-permute-start.5 = (bf16[3,32,32,128]{3,2,1,0:T(8,128)(2,1)}, bf16[3,32,32,128]{3,2,1,0:T(8,128)(2,1)}, u32[]{:S(2)}, u32[]{:S(2)}) collective-permute-start(bf16[3,32,32,128]{3,2,1,0:T(8,128)(2,1)} %get-tuple-element.68.refs_5_), channel_id=1, source_target_pairs={{0,2},{1,3},{2,0},{3,1},{4,6},{5,7},{6,4},{7,5},{8,10},{9,11},{10,... | collective-permute-start | bytes 2359304 | tf_op jit(solution)/shard_map/ppermute | solution.py:348
  37.8 24.8 %collective-permute-start.4 = (bf16[3,32,32,128]{3,2,1,0:T(8,128)(2,1)}, bf16[3,32,32,128]{3,2,1,0:T(8,128)(2,1)}, u32[]{:S(2)}, u32[]{:S(2)}) collective-permute-start(bf16[3,32,32,128]{3,2,1,0:T(8,128)(2,1)} %get-tuple-element.68.refs_5_), channel_id=1, source_target_pairs={{0,1},{1,0},{2,3},{3,2},{4,5},{5,4},{6,7},{7,6},{8,9},{9,8},{10,11... | collective-permute-start | bytes 2359304 | tf_op jit(solution)/shard_map/ppermute | solution.py:348
  48.2 1.6 %copy-start.14 = (bf16[32,64,512]{2,1,0:T(8,128)(2,1)S(1)}, bf16[32,64,512]{2,1,0:T(8,128)(2,1)}, u32[]{:S(2)}) copy-start(bf16[32,64,512]{2,1,0:T(8,128)(2,1)} %copy-done.13) | copy-start | bytes 6291460
  62.6 7.6 %collective-permute-start.8 = (bf16[3,32,32,128]{3,2,1,0:T(8,128)(2,1)}, bf16[3,32,32,128]{3,2,1,0:T(8,128)(2,1)S(1)}, u32[]{:S(2)}, u32[]{:S(2)}) collective-permute-start(bf16[3,32,32,128]{3,2,1,0:T(8,128)(2,1)} %collective-permute-done.5.refs_7_), channel_id=1, source_target_pairs={{0,1},{1,0},{2,3},{3,2},{4,5},{5,4},{6,7},{7,6},{8,9},{9,8},{10,11... | collective-permute-start | bytes 2359304 | tf_op jit(solution)/shard_map/ppermute | solution.py:348
  66.5 3.3 %collective-permute-start.6 = (bf16[64,32,128]{2,1,0:T(8,128)(2,1)S(1)}, bf16[64,32,128]{2,1,0:T(8,128)(2,1)S(1)}, u32[]{:S(2)}, u32[]{:S(2)}) collective-permute-start(bf16[64,32,128]{2,1,0:T(8,128)(2,1)S(1)} %get-tuple-element.49.after_ref.refs_1_), channel_id=1, source_target_pairs={{0,1},{1,0},{2,3},{3,2},{4,5},{5,4},{6,7},{7,6},{8,9},{9,8},{10,11... | collective-permute-start | bytes 1572872 | tf_op jit(solution)/shard_map/ppermute | solution.py:348
  66.6 3.5 %collective-permute-start.7 = (bf16[64,32,128]{2,1,0:T(8,128)(2,1)}, bf16[64,32,128]{2,1,0:T(8,128)(2,1)S(1)}, u32[]{:S(2)}, u32[]{:S(2)}) collective-permute-start(bf16[64,32,128]{2,1,0:T(8,128)(2,1)} %collective-permute-done.3.refs_3_), channel_id=1, source_target_pairs={{0,1},{1,0},{2,3},{3,2},{4,5},{5,4},{6,7},{7,6},{8,9},{9,8},{10,11... | collective-permute-start | bytes 1572872 | tf_op jit(solution)/shard_map/ppermute | solution.py:348
  67.0 19.4 %collective-permute-start.10 = (bf16[3,32,32,128]{3,2,1,0:T(8,128)(2,1)}, bf16[3,32,32,128]{3,2,1,0:T(8,128)(2,1)}, u32[]{:S(2)}, u32[]{:S(2)}) collective-permute-start(bf16[3,32,32,128]{3,2,1,0:T(8,128)(2,1)} %get-tuple-element.76.refs_5_), channel_id=1, source_target_pairs={{0,2},{1,3},{2,0},{3,1},{4,6},{5,7},{6,4},{7,5},{8,10},{9,11},{10,... | collective-permute-start | bytes 2359304 | tf_op jit(solution)/shard_map/ppermute | solution.py:348
  70.1 3.5 %copy-start.27 = (bf16[64,32,128]{2,1,0:T(8,128)(2,1)}, bf16[64,32,128]{2,1,0:T(8,128)(2,1)S(1)}, u32[]{:S(2)}) copy-start(bf16[64,32,128]{2,1,0:T(8,128)(2,1)S(1)} %collective-permute-done.7.refs_4_) | copy-start | bytes 1572868
  73.6 2.7 %copy-start.15 = (f32[2,1040,128]{2,1,0:T(8,128)}, f32[2,1040,128]{2,1,0:T(8,128)S(1)}, u32[]{:S(2)}) copy-start(f32[2,1040,128]{2,1,0:T(8,128)S(1)} %get-tuple-element.82.refs_0_) | copy-start | bytes 3194884
  76.4 56.1 %all-to-all-start.1 = ((f16[8,2064,128]{2,1,0:T(8,128)(2,1)}), f16[8,2064,128]{2,1,0:T(8,128)(2,1)}, u32[]{:S(2)}, u32[]{:S(2)}) async-start(f16[8,2064,128]{2,1,0:T(8,128)(2,1)} %convert_element_type.42), calls=%async_computation.1 | async-start | bytes 8454144 | tf_op jit(solution)/shard_map/all_to_all | solution.py:402
  81.7 9.2 %collective-permute-start.9 = (bf16[3,32,32,128]{3,2,1,0:T(8,128)(2,1)}, bf16[3,32,32,128]{3,2,1,0:T(8,128)(2,1)S(1)}, u32[]{:S(2)}, u32[]{:S(2)}) collective-permute-start(bf16[3,32,32,128]{3,2,1,0:T(8,128)(2,1)} %get-tuple-element.76.refs_5_), channel_id=1, source_target_pairs={{0,1},{1,0},{2,3},{3,2},{4,5},{5,4},{6,7},{7,6},{8,9},{9,8},{10,11... | collective-permute-start | bytes 2359304 | tf_op jit(solution)/shard_map/ppermute | solution.py:348
  86.4 4.5 %collective-permute-start.11 = (bf16[3,32,32,128]{3,2,1,0:T(8,128)(2,1)}, bf16[3,32,32,128]{3,2,1,0:T(8,128)(2,1)S(1)}, u32[]{:S(2)}, u32[]{:S(2)}) collective-permute-start(bf16[3,32,32,128]{3,2,1,0:T(8,128)(2,1)} %collective-permute-done.10.refs_7_), channel_id=1, source_target_pairs={{0,1},{1,0},{2,3},{3,2},{4,5},{5,4},{6,7},{7,6},{8,9},{9,8},{10,11... | collective-permute-start | bytes 2359304 | tf_op jit(solution)/shard_map/ppermute | solution.py:348
  87.8 26.7 %collective-permute-start.15 = (f16[2,1040,128]{2,1,0:T(8,128)(2,1)}, f16[2,1040,128]{2,1,0:T(8,128)(2,1)S(1)}, u32[]{:S(2)}, u32[]{:S(2)}) collective-permute-start(f16[2,1040,128]{2,1,0:T(8,128)(2,1)} %convert_element_type.43), channel_id=1, source_target_pairs={{0,4},{1,5},{2,6},{3,7},{4,8},{5,9},{6,10},{7,11},{8,12},{9,13},{1... | collective-permute-start | bytes 1597448 | tf_op jit(solution)/shard_map/ppermute | solution.py:344
  88.5 28.6 %collective-permute-start.16 = (f16[2,1040,128]{2,1,0:T(8,128)(2,1)}, f16[2,1040,128]{2,1,0:T(8,128)(2,1)}, u32[]{:S(2)}, u32[]{:S(2)}) collective-permute-start(f16[2,1040,128]{2,1,0:T(8,128)(2,1)} %convert_element_type.44), channel_id=1, source_target_pairs={{0,8},{1,9},{2,10},{3,11},{4,12},{5,13},{6,14},{7,15},{8,0},{9,1},... | collective-permute-start | bytes 1597448 | tf_op jit(solution)/shard_map/ppermute | solution.py:344
  88.9 30.3 %collective-permute-start.17 = (f16[2,1040,128]{2,1,0:T(8,128)(2,1)}, f16[2,1040,128]{2,1,0:T(8,128)(2,1)}, u32[]{:S(2)}, u32[]{:S(2)}) collective-permute-start(f16[2,1040,128]{2,1,0:T(8,128)(2,1)} %convert_element_type.45), channel_id=1, source_target_pairs={{0,12},{1,13},{2,14},{3,15},{4,0},{5,1},{6,2},{7,3},{8,4},{9,5},{1... | collective-permute-start | bytes 1597448 | tf_op jit(solution)/shard_map/ppermute | solution.py:344
  95.1 4.8 %copy-start.17 = (f32[2,1040,128]{2,1,0:T(8,128)}, f32[2,1040,128]{2,1,0:T(8,128)S(1)}, u32[]{:S(2)}) copy-start(f32[2,1040,128]{2,1,0:T(8,128)S(1)} %get-tuple-element.86.refs_4_) | copy-start | bytes 3194884
  96.1 43.4 %collective-permute-start.12 = (f16[2,1040,128]{2,1,0:T(8,128)(2,1)}, f16[2,1040,128]{2,1,0:T(8,128)(2,1)}, u32[]{:S(2)}, u32[]{:S(2)}) collective-permute-start(f16[2,1040,128]{2,1,0:T(8,128)(2,1)} %convert_element_type.47), channel_id=1, source_target_pairs={{0,4},{1,5},{2,6},{3,7},{4,8},{5,9},{6,10},{7,11},{8,12},{9,13},{1... | collective-permute-start | bytes 1597448 | tf_op jit(solution)/shard_map/ppermute | solution.py:344
  97.1 42.4 %collective-permute-start.13 = (f16[2,1040,128]{2,1,0:T(8,128)(2,1)}, f16[2,1040,128]{2,1,0:T(8,128)(2,1)}, u32[]{:S(2)}, u32[]{:S(2)}) collective-permute-start(f16[2,1040,128]{2,1,0:T(8,128)(2,1)} %convert_element_type.48), channel_id=1, source_target_pairs={{0,8},{1,9},{2,10},{3,11},{4,12},{5,13},{6,14},{7,15},{8,0},{9,1},... | collective-permute-start | bytes 1597448 | tf_op jit(solution)/shard_map/ppermute | solution.py:344
  115.2 24.3 %collective-permute-start.14 = (f16[2,1040,128]{2,1,0:T(8,128)(2,1)}, f16[2,1040,128]{2,1,0:T(8,128)(2,1)}, u32[]{:S(2)}, u32[]{:S(2)}) collective-permute-start(f16[2,1040,128]{2,1,0:T(8,128)(2,1)} %convert_element_type.49), channel_id=1, source_target_pairs={{0,12},{1,13},{2,14},{3,15},{4,0},{5,1},{6,2},{7,3},{8,4},{9,5},{1... | collective-permute-start | bytes 1597448 | tf_op jit(solution)/shard_map/ppermute | solution.py:344
  132.5 2.9 %copy-start.3 = (bf16[64,32,512]{2,1,0:T(8,128)(2,1)S(1)}, bf16[64,32,512]{2,1,0:T(8,128)(2,1)}, u32[]{:S(2)}) copy-start(bf16[64,32,512]{2,1,0:T(8,128)(2,1)} %diff_ref.5) | copy-start | bytes 6291460
  132.5 4.1 %copy-start.5 = (f32[64,32,512]{2,1,0:T(8,128)S(1)}, f32[64,32,512]{2,1,0:T(8,128)}, u32[]{:S(2)}) copy-start(f32[64,32,512]{2,1,0:T(8,128)} %copy-done.4) | copy-start | bytes 12582916
  136.6 6.7 %copy-start.16 = (f32[2,1040,128]{2,1,0:T(8,128)S(1)}, f32[2,1040,128]{2,1,0:T(8,128)}, u32[]{:S(2)}) copy-start(f32[2,1040,128]{2,1,0:T(8,128)} %copy-done.15) | copy-start | bytes 3194884
  136.6 6.7 %copy-start.18 = (f32[2,1040,128]{2,1,0:T(8,128)S(1)}, f32[2,1040,128]{2,1,0:T(8,128)}, u32[]{:S(2)}) copy-start(f32[2,1040,128]{2,1,0:T(8,128)} %copy-done.17) | copy-start | bytes 3194884
  139.5 3.7 %copy-start.7 = (f32[2,1040,128]{2,1,0:T(8,128)S(1)}, f32[2,1040,128]{2,1,0:T(8,128)}, u32[]{:S(2)}) copy-start(f32[2,1040,128]{2,1,0:T(8,128)} %convert_element_type.51.refs_2_) | copy-start | bytes 3194884
  139.5 3.7 %copy-start.8 = (f32[2,1040,128]{2,1,0:T(8,128)S(1)}, f32[2,1040,128]{2,1,0:T(8,128)}, u32[]{:S(2)}) copy-start(f32[2,1040,128]{2,1,0:T(8,128)} %convert_element_type.52.refs_3_) | copy-start | bytes 3194884
  139.6 3.7 %copy-start.11 = (bf16[64,32,512]{2,1,0:T(8,128)(2,1)S(1)}, bf16[64,32,512]{2,1,0:T(8,128)(2,1)}, u32[]{:S(2)}) copy-start(bf16[64,32,512]{2,1,0:T(8,128)(2,1)} %drift_ref.3) | copy-start | bytes 6291460
  (4 other events, 4.1 us)

commit v5 on v4

--- a/solution.py
+++ b/solution.py
@@ -320,7 +320,7 @@
 
 
 def add_y(part, diff, y_back):
-    jb = 8
+    jb = 16
     n = NJ // jb
     field = pl.BlockSpec((jb, NK, NI), lambda j: (j, 0, 0))
     return pl.pallas_call(
@@ -335,7 +335,7 @@
         ],
         out_specs=field,
         out_shape=jax.ShapeDtypeStruct((NJ, NK, NI), F32),
-        compiler_params=params(20),
+        compiler_params=params(30),
         name="addy",
     )(part, diff, y_back, y_back, y_back)
 

time: 149 us -> 149 us (level)
  no operation moved by 1% of the time
where the time goes in v5:
time: 149 us; the launch traced here: 148 us
  waiting for transfers between devices  40.7 us (27%)
  Pallas kernels  35.1 us (24%)
  starting transfers between devices  33.7 us (23%)
  other arithmetic  19.9 us (13%)
  local copies, waits for them, and re-layouts  17.2 us (12%)
    unnamed x64, local copies, waits for them, and re-layouts  16.2 us
    ppermute x9, waiting for transfers between devices, ring(): lax.ppermute(x, 'col', [(c, (c + 4 * shift) % 16) for c in range(16)])  14.5 us
    ppermute x9, starting transfers between devices, ring(): lax.ppermute(x, 'col', [(c, (c + 4 * shift) % 16) for c in range(16)])  11.7 us
    all_to_all x1, waiting for transfers between devices, on_device(): y_back = lax.all_to_all(y_out, 'row', 0, 0, tiled=False)  11.2 us
    ppermute x9, starting transfers between devices, flip(): return lax.ppermute(x, 'col', [(c, c ^ bits) for c in range(16)])  10.1 us
    pallas_call x1, Pallas kernels, y_terms(): pl.pallas_call(y_kernel, grid=(8,), in_specs=[pl.BlockSpec(memory_space=p...  9.01 us
    all_to_all x1, waiting for transfers between devices, on_device(): scalar_y = lax.all_to_all(pack(scalar, mine[0]), 'row', 0, 0, tiled=False)  7.95 us
    ppermute x9, waiting for transfers between devices, flip(): return lax.ppermute(x, 'col', [(c, c ^ bits) for c in range(16)])  7.05 us
  transfers between devices with their start and end apart: 20, of which 6 were waited for; matrix products, arithmetic and copies ran while one was open for 12% of the time, Pallas kernels for 19%

profile of v5, /device:TPU:1, one launch (start us, length us, event | category | flops | bytes accessed | tf_op | source)
XLA Modules:
  0.0 147.6 jit_solution(7955350156321024194)
XLA Ops:
  0.7 1.6 %copy-done = bf16[64,32,512]{2,1,0:T(8,128)(2,1)S(1)} copy-done((bf16[64,32,512]{2,1,0:T(8,128)(2,1)S(1)}, bf16[64,32,512]{2,1,0:T(8,128)(2,1)}, u32[]{:S(2)}) %copy-start) | copy-done | bytes 2097176
  2.3 2.4 %cut.1 = (bf16[64,32,128]{2,1,0:T(8,128)(2,1)S(1)}, bf16[64,32,128]{2,1,0:T(8,128)(2,1)}, bf16[64,32,128]{2,1,0:T(8,128)(2,1)}, bf16[64,32,128]{2,1,0:T(8,128)(2,1)}) custom-call(s32[2]{0:T(128)S(1)} %pad_add_fusion.at, bf16[64,32,512]{2,1,0:T(8,128)(2,1)S(1)} %copy-done), custom_call_target="tpu_custom_call" | custom-call | tf_op jit(solution)/shard_map/cut/pallas_call | solution.py:40
  4.7 2.5 %collective-permute-start = (bf16[64,32,128]{2,1,0:T(8,128)(2,1)}, bf16[64,32,128]{2,1,0:T(8,128)(2,1)}, u32[]{:S(2)}, u32[]{:S(2)}) collective-permute-start(bf16[64,32,128]{2,1,0:T(8,128)(2,1)} %get-tuple-element.46), channel_id=1, source_target_pairs={{0,4},{1,5},{2,6},{3,7},{4,8},{5,9},{6,10},{7,11},{8,12},{9,13},{1... | collective-permute-start | bytes 1572872 | tf_op jit(solution)/shard_map/ppermute | solution.py:344
  7.2 3.3 %collective-permute-start.1 = (bf16[64,32,128]{2,1,0:T(8,128)(2,1)}, bf16[64,32,128]{2,1,0:T(8,128)(2,1)}, u32[]{:S(2)}, u32[]{:S(2)}) collective-permute-start(bf16[64,32,128]{2,1,0:T(8,128)(2,1)} %get-tuple-element.47), channel_id=1, source_target_pairs={{0,8},{1,9},{2,10},{3,11},{4,12},{5,13},{6,14},{7,15},{8,0},{9,1},... | collective-permute-start | bytes 1572872 | tf_op jit(solution)/shard_map/ppermute | solution.py:344
  11.2 1.2 collective-permute-start.3
  13.2 1.3 copy-done.6
  14.5 6.6 %all-to-all-start = ((bf16[8,64,16,128]{3,2,1,0:T(8,128)(2,1)}), bf16[8,64,16,128]{3,2,1,0:T(8,128)(2,1)}, u32[]{:S(2)}, u32[]{:S(2)}) async-start(bf16[8,64,16,128]{3,2,1,0:T(8,128)(2,1)} %copy-done.6), calls=%async_computation | async-start | bytes 4194304 | tf_op jit(solution)/shard_map/all_to_all | solution.py:374
  21.2 1.6 %copy-done.2 = bf16[64,32,512]{2,1,0:T(8,128)(2,1)S(1)} copy-done((bf16[64,32,512]{2,1,0:T(8,128)(2,1)S(1)}, bf16[64,32,512]{2,1,0:T(8,128)(2,1)}, u32[]{:S(2)}) %copy-start.2) | copy-done | bytes 2097176
  22.7 2.2 %copy-done.9 = f32[64,32,512]{2,1,0:T(8,128)S(1)} copy-done((f32[64,32,512]{2,1,0:T(8,128)S(1)}, f32[64,32,512]{2,1,0:T(8,128)}, u32[]{:S(2)}) %copy-start.9) | copy-done | bytes 4194328
  24.9 1.6 %copy-done.10 = bf16[64,32,512]{2,1,0:T(8,128)(2,1)S(1)} copy-done((bf16[64,32,512]{2,1,0:T(8,128)(2,1)S(1)}, bf16[64,32,512]{2,1,0:T(8,128)(2,1)}, u32[]{:S(2)}) %copy-start.10) | copy-done | bytes 2097176
  26.5 1.0 copy-done.22
  27.6 4.4 %xterms.1.part_ref = f32[64,32,512]{2,1,0:T(8,128)S(1)} custom-call(bf16[64,32,512]{2,1,0:T(8,128)(2,1)S(1)} %copy-done.1, f32[64,32,512]{2,1,0:T(8,128)S(1)} %copy-done.9, bf16[64,32,512]{2,1,0:T(8,128)(2,1)S(1)} %copy-done.10, bf16[64,32,512]{2,1,0:T(8,128)(2,1)S(1)} %copy-done.2, bf16[512,512]{1,0:T(8,128)(2,1)S(1)} %copy-done.21, ...), custom_call_target="tpu_custom_call" | custom-call | flops 1000 | bytes 8192 | tf_op jit(solution)/shard_map/xterms/pallas_call | solution.py:241
  32.1 1.0 operator.1
  33.1 1.0 copy-done.4
  34.1 3.7 %merge.1 = (bf16[3,32,32,128]{3,2,1,0:T(8,128)(2,1)}, bf16[3,32,32,128]{3,2,1,0:T(8,128)(2,1)}) custom-call(bf16[64,32,128]{2,1,0:T(8,128)(2,1)} %collective-permute-done.r1, bf16[64,32,128]{2,1,0:T(8,128)(2,1)} %collective-permute-done.1.r2, bf16[64,32,128]{2,1,0:T(8,128)(2,1)} %collective-permute-done.2.r3), custom_call_target="tpu_custom_call" | custom-call | flops 20000000000 | bytes 3145728 | tf_op jit(solution)/shard_map/merge/pallas_call | solution.py:70
  37.8 2.3 %collective-permute-start.4 = (bf16[3,32,32,128]{3,2,1,0:T(8,128)(2,1)}, bf16[3,32,32,128]{3,2,1,0:T(8,128)(2,1)}, u32[]{:S(2)}, u32[]{:S(2)}) collective-permute-start(bf16[3,32,32,128]{3,2,1,0:T(8,128)(2,1)} %get-tuple-element.68.refs_5_), channel_id=1, source_target_pairs={{0,1},{1,0},{2,3},{3,2},{4,5},{5,4},{6,7},{7,6},{8,9},{9,8},{10,11... | collective-permute-start | bytes 2359304 | tf_op jit(solution)/shard_map/ppermute | solution.py:348
  40.2 7.9 %all-to-all-done.s_ref = bf16[8,64,16,128]{3,2,1,0:T(8,128)(2,1)} async-done(((bf16[8,64,16,128]{3,2,1,0:T(8,128)(2,1)}), bf16[8,64,16,128]{3,2,1,0:T(8,128)(2,1)}, u32[]{:S(2)}, u32[]{:S(2)}) %all-to-all-start) | async-done | bytes 2097184 | tf_op jit(solution)/shard_map/all_to_all | solution.py:374
  48.2 1.6 %copy-done.14 = bf16[32,64,512]{2,1,0:T(8,128)(2,1)S(1)} copy-done((bf16[32,64,512]{2,1,0:T(8,128)(2,1)S(1)}, bf16[32,64,512]{2,1,0:T(8,128)(2,1)}, u32[]{:S(2)}) %copy-start.14) | copy-done | bytes 2097176
  49.8 1.2 copy-done.20
  51.0 9.0 %yterms.1 = f32[8,2064,128]{2,1,0:T(8,128)S(1)} custom-call(s32[1]{0:T(128)} %bitcast.4.odd_ref, bf16[8,64,16,128]{3,2,1,0:T(8,128)(2,1)} %all-to-all-done.s_ref, bf16[32,64,512]{2,1,0:T(8,128)(2,1)S(1)} %copy-done.14, bf16[1024,512]{1,0:T(8,128)(2,1)S(1)} %copy-done.20, f32[512,1]{1,0:T(8,128)S(1)} %copy.17.metric_ref), custom_call_target="tpu_custom_call" | custom-call | flops 1000 | bytes 8192 | tf_op jit(solution)/shard_map/yterms/pallas_call | solution.py:166
  60.0 2.6 %convert_element_type.42 = f16[8,2064,128]{2,1,0:T(8,128)(2,1)} convert(f32[8,2064,128]{2,1,0:T(8,128)S(1)} %yterms.1) | non-fusion elementwise | flops 2113536 | bytes 12681216 | tf_op jit(solution)/shard_map/convert_element_type | solution.py:386
  62.6 3.9 %collective-permute-start.8 = (bf16[3,32,32,128]{3,2,1,0:T(8,128)(2,1)}, bf16[3,32,32,128]{3,2,1,0:T(8,128)(2,1)S(1)}, u32[]{:S(2)}, u32[]{:S(2)}) collective-permute-start(bf16[3,32,32,128]{3,2,1,0:T(8,128)(2,1)} %collective-permute-done.5.refs_7_), channel_id=1, source_target_pairs={{0,1},{1,0},{2,3},{3,2},{4,5},{5,4},{6,7},{7,6},{8,9},{9,8},{10,11... | collective-permute-start | bytes 2359304 | tf_op jit(solution)/shard_map/ppermute | solution.py:348
  67.2 2.6 %collective-permute-done.6.refs_2_ = bf16[64,32,128]{2,1,0:T(8,128)(2,1)S(1)} collective-permute-done((bf16[64,32,128]{2,1,0:T(8,128)(2,1)S(1)}, bf16[64,32,128]{2,1,0:T(8,128)(2,1)S(1)}, u32[]{:S(2)}, u32[]{:S(2)}) %collective-permute-start.6) | collective-permute-done | bytes 524320 | tf_op jit(solution)/shard_map/ppermute | solution.py:348
  70.1 3.5 %zterms.2 = (f32[2,1040,128]{2,1,0:T(8,128)S(1)}, f32[2,1040,128]{2,1,0:T(8,128)S(1)}, f32[2,1040,128]{2,1,0:T(8,128)S(1)}, f32[2,1040,128]{2,1,0:T(8,128)S(1)}) custom-call(bf16[256,512]{1,0:T(8,128)(2,1)S(1)} %get-tuple-element.66.refs_0_, bf16[64,32,128]{2,1,0:T(8,128)(2,1)S(1)} %get-tuple-element.49.after_ref.refs_1_, ...), custom_call_target="tpu_custom_call" | custom-call | flops 1000 | bytes 8192 | tf_op jit(solution)/shard_map/zterms/pallas_call | solution.py:210
  73.6 1.0 convert_element_type.43
  74.6 0.9 convert_element_type.44
  76.4 5.3 %all-to-all-start.1 = ((f16[8,2064,128]{2,1,0:T(8,128)(2,1)}), f16[8,2064,128]{2,1,0:T(8,128)(2,1)}, u32[]{:S(2)}, u32[]{:S(2)}) async-start(f16[8,2064,128]{2,1,0:T(8,128)(2,1)} %convert_element_type.42), calls=%async_computation.1 | async-start | bytes 8454144 | tf_op jit(solution)/shard_map/all_to_all | solution.py:402
  82.3 4.1 %collective-permute-done.10.refs_7_ = bf16[3,32,32,128]{3,2,1,0:T(8,128)(2,1)} collective-permute-done((bf16[3,32,32,128]{3,2,1,0:T(8,128)(2,1)}, bf16[3,32,32,128]{3,2,1,0:T(8,128)(2,1)}, u32[]{:S(2)}, u32[]{:S(2)}) %collective-permute-start.10) | collective-permute-done | bytes 786464 | tf_op jit(solution)/shard_map/ppermute | solution.py:348
  86.4 1.3 collective-permute-start.11
  88.9 1.9 %collective-permute-start.17 = (f16[2,1040,128]{2,1,0:T(8,128)(2,1)}, f16[2,1040,128]{2,1,0:T(8,128)(2,1)}, u32[]{:S(2)}, u32[]{:S(2)}) collective-permute-start(f16[2,1040,128]{2,1,0:T(8,128)(2,1)} %convert_element_type.45), channel_id=1, source_target_pairs={{0,12},{1,13},{2,14},{3,15},{4,0},{5,1},{6,2},{7,3},{8,4},{9,5},{1... | collective-permute-start | bytes 1597448 | tf_op jit(solution)/shard_map/ppermute | solution.py:344
  90.9 1.0 copy-done.28
  91.9 3.2 %zterms.3 = (f32[2,1040,128]{2,1,0:T(8,128)S(1)}, f32[2,1040,128]{2,1,0:T(8,128)S(1)}, f32[2,1040,128]{2,1,0:T(8,128)S(1)}, f32[2,1040,128]{2,1,0:T(8,128)S(1)}) custom-call(bf16[256,512]{1,0:T(8,128)(2,1)S(1)} %get-tuple-element.66.refs_0_, bf16[64,32,128]{2,1,0:T(8,128)(2,1)S(1)} %get-tuple-element.49.after_ref.refs_1_, ...), custom_call_target="tpu_custom_call" | custom-call | flops 20000000000 | bytes 8192 | tf_op jit(solution)/shard_map/zterms/pallas_call | solution.py:210
  95.1 1.0 convert_element_type.47
  96.2 0.9 convert_element_type.48
  97.1 1.9 %collective-permute-start.13 = (f16[2,1040,128]{2,1,0:T(8,128)(2,1)}, f16[2,1040,128]{2,1,0:T(8,128)(2,1)}, u32[]{:S(2)}, u32[]{:S(2)}) collective-permute-start(f16[2,1040,128]{2,1,0:T(8,128)(2,1)} %convert_element_type.48), channel_id=1, source_target_pairs={{0,8},{1,9},{2,10},{3,11},{4,12},{5,13},{6,14},{7,15},{8,0},{9,1},... | collective-permute-start | bytes 1597448 | tf_op jit(solution)/shard_map/ppermute | solution.py:344
  99.0 0.9 convert_element_type.49
  99.9 14.5 %collective-permute-done.15 = f16[2,1040,128]{2,1,0:T(8,128)(2,1)S(1)} collective-permute-done((f16[2,1040,128]{2,1,0:T(8,128)(2,1)}, f16[2,1040,128]{2,1,0:T(8,128)(2,1)S(1)}, u32[]{:S(2)}, u32[]{:S(2)}) %collective-permute-start.15) | collective-permute-done | bytes 532512 | tf_op jit(solution)/shard_map/ppermute | solution.py:344
  116.0 1.1 convert_element_type.50.refs_1_
  117.1 2.1 %convert_element_type.51.refs_2_ = f32[2,1040,128]{2,1,0:T(8,128)} convert(f16[2,1040,128]{2,1,0:T(8,128)(2,1)} %collective-permute-done.16) | non-fusion elementwise | flops 266240 | bytes 1597440 | tf_op jit(solution)/shard_map/convert_element_type | solution.py:405
  119.2 2.1 %convert_element_type.52.refs_3_ = f32[2,1040,128]{2,1,0:T(8,128)} convert(f16[2,1040,128]{2,1,0:T(8,128)(2,1)} %collective-permute-done.17) | non-fusion elementwise | flops 266240 | bytes 1597440 | tf_op jit(solution)/shard_map/convert_element_type | solution.py:405
  121.3 11.2 %all-to-all-done.1 = f16[8,2064,128]{2,1,0:T(8,128)(2,1)} async-done(((f16[8,2064,128]{2,1,0:T(8,128)(2,1)}), f16[8,2064,128]{2,1,0:T(8,128)(2,1)}, u32[]{:S(2)}, u32[]{:S(2)}) %all-to-all-start.1) | async-done | bytes 4227104 | tf_op jit(solution)/shard_map/all_to_all | solution.py:402
  132.5 2.9 %convert_element_type.46.p_ref.c_ref.e_ref = f32[8,2064,128]{2,1,0:T(8,128)S(1)} convert(f16[8,2064,128]{2,1,0:T(8,128)(2,1)} %all-to-all-done.1) | non-fusion elementwise | flops 2113536 | bytes 12681216 | tf_op jit(solution)/shard_map/convert_element_type | solution.py:404
  135.4 1.2 copy-done.5
  136.6 2.6 %addy.1.part_ref = f32[64,32,512]{2,1,0:T(8,128)S(1)} custom-call(f32[64,32,512]{2,1,0:T(8,128)S(1)} %copy-done.5, bf16[64,32,512]{2,1,0:T(8,128)(2,1)S(1)} %copy-done.3, f32[8,2064,128]{2,1,0:T(8,128)S(1)} %convert_element_type.46.p_ref.c_ref.e_ref, f32[8,2064,128]{2,1,0:T(8,128)S(1)} %convert_element_type.46.p_ref.c_ref.e_ref, ...), custom_call_target="tpu_custom_call" | custom-call | tf_op jit(solution)/shard_map/addy/pallas_call | solution.py:326
  139.3 1.3 convert_element_type.53.refs_5_
  140.5 1.2 convert_element_type.54.refs_6_
  141.8 1.1 convert_element_type.55.refs_7_
  143.0 4.6 %last.1 = (f32[64,32,512]{2,1,0:T(8,128)}, bf16[64,32,512]{2,1,0:T(8,128)(2,1)}) custom-call(s32[2]{0:T(128)S(1)} %pad_add_fusion.at, bf16[64,32,512]{2,1,0:T(8,128)(2,1)S(1)} %copy-done.1, f32[64,32,512]{2,1,0:T(8,128)S(1)} %addy.1.part_ref, bf16[64,32,512]{2,1,0:T(8,128)(2,1)S(1)} %copy-done.11, bf16[64,32,512]{2,1,0:T(8,128)(2,1)S(1)} %copy-done.3, ...), custom_call_target="tpu_custom_call" | custom-call | tf_op jit(solution)/shard_map/last/pallas_call | solution.py:283
  (84 shorter events, 7.3 us)
Async XLA Ops:
  0.7 1.6 %copy-start = (bf16[64,32,512]{2,1,0:T(8,128)(2,1)S(1)}, bf16[64,32,512]{2,1,0:T(8,128)(2,1)}, u32[]{:S(2)}) copy-start(bf16[64,32,512]{2,1,0:T(8,128)(2,1)} %s_ref.7) | copy-start | bytes 6291460
  4.7 29.3 %collective-permute-start = (bf16[64,32,128]{2,1,0:T(8,128)(2,1)}, bf16[64,32,128]{2,1,0:T(8,128)(2,1)}, u32[]{:S(2)}, u32[]{:S(2)}) collective-permute-start(bf16[64,32,128]{2,1,0:T(8,128)(2,1)} %get-tuple-element.46), channel_id=1, source_target_pairs={{0,4},{1,5},{2,6},{3,7},{4,8},{5,9},{6,10},{7,11},{8,12},{9,13},{1... | collective-permute-start | bytes 1572872 | tf_op jit(solution)/shard_map/ppermute | solution.py:344
  7.2 26.9 %collective-permute-start.1 = (bf16[64,32,128]{2,1,0:T(8,128)(2,1)}, bf16[64,32,128]{2,1,0:T(8,128)(2,1)}, u32[]{:S(2)}, u32[]{:S(2)}) collective-permute-start(bf16[64,32,128]{2,1,0:T(8,128)(2,1)} %get-tuple-element.47), channel_id=1, source_target_pairs={{0,8},{1,9},{2,10},{3,11},{4,12},{5,13},{6,14},{7,15},{8,0},{9,1},... | collective-permute-start | bytes 1572872 | tf_op jit(solution)/shard_map/ppermute | solution.py:344
  10.5 23.6 %collective-permute-start.2 = (bf16[64,32,128]{2,1,0:T(8,128)(2,1)}, bf16[64,32,128]{2,1,0:T(8,128)(2,1)}, u32[]{:S(2)}, u32[]{:S(2)}) collective-permute-start(bf16[64,32,128]{2,1,0:T(8,128)(2,1)} %get-tuple-element.48), channel_id=1, source_target_pairs={{0,12},{1,13},{2,14},{3,15},{4,0},{5,1},{6,2},{7,3},{8,4},{9,5},{1... | collective-permute-start | bytes 1572872 | tf_op jit(solution)/shard_map/ppermute | solution.py:344
  11.2 22.9 %collective-permute-start.3 = (bf16[64,32,128]{2,1,0:T(8,128)(2,1)S(1)}, bf16[64,32,128]{2,1,0:T(8,128)(2,1)}, u32[]{:S(2)}, u32[]{:S(2)}) collective-permute-start(bf16[64,32,128]{2,1,0:T(8,128)(2,1)S(1)} %get-tuple-element.49.after_ref.refs_1_), channel_id=1, source_target_pairs={{0,2},{1,3},{2,0},{3,1},{4,6},{5,7},{6,4},{7,5},{8,10},{9,11},{10,... | collective-permute-start | bytes 1572872 | tf_op jit(solution)/shard_map/ppermute | solution.py:348
  13.2 1.3 copy-start.6
  14.5 6.6 %copy-start.1 = (bf16[64,32,512]{2,1,0:T(8,128)(2,1)S(1)}, bf16[64,32,512]{2,1,0:T(8,128)(2,1)}, u32[]{:S(2)}) copy-start(bf16[64,32,512]{2,1,0:T(8,128)(2,1)} %s_ref.7) | copy-start | bytes 6291460
  14.5 6.6 %copy-start.21 = (bf16[512,512]{1,0:T(8,128)(2,1)S(1)}, bf16[512,512]{1,0:T(8,128)(2,1)}, u32[]{:S(2)}) copy-start(bf16[512,512]{1,0:T(8,128)(2,1)} %first_ref.3) | copy-start | bytes 1572868
  14.5 6.6 %copy-start.29 = (f32[512]{0:T(512)S(1)}, f32[512]{0:T(512)}, u32[]{:S(2)}) copy-start(f32[512]{0:T(512)} %param.21) | copy-start | bytes 6148
  14.5 33.7 %all-to-all-start = ((bf16[8,64,16,128]{3,2,1,0:T(8,128)(2,1)}), bf16[8,64,16,128]{3,2,1,0:T(8,128)(2,1)}, u32[]{:S(2)}, u32[]{:S(2)}) async-start(bf16[8,64,16,128]{3,2,1,0:T(8,128)(2,1)} %copy-done.6), calls=%async_computation | async-start | bytes 4194304 | tf_op jit(solution)/shard_map/all_to_all | solution.py:374
  21.1 1.6 %copy-start.2 = (bf16[64,32,512]{2,1,0:T(8,128)(2,1)S(1)}, bf16[64,32,512]{2,1,0:T(8,128)(2,1)}, u32[]{:S(2)}) copy-start(bf16[64,32,512]{2,1,0:T(8,128)(2,1)} %diff_ref.5) | copy-start | bytes 6291460
  22.7 2.2 %copy-start.9 = (f32[64,32,512]{2,1,0:T(8,128)S(1)}, f32[64,32,512]{2,1,0:T(8,128)}, u32[]{:S(2)}) copy-start(f32[64,32,512]{2,1,0:T(8,128)} %reg_ref.1) | copy-start | bytes 12582916
  24.9 1.6 %copy-start.10 = (bf16[64,32,512]{2,1,0:T(8,128)(2,1)S(1)}, bf16[64,32,512]{2,1,0:T(8,128)(2,1)}, u32[]{:S(2)}) copy-start(bf16[64,32,512]{2,1,0:T(8,128)(2,1)} %drift_ref.2) | copy-start | bytes 6291460
  27.6 4.5 %copy-start.12 = (bf16[512,32,64]{0,2,1:T(8,128)(2,1)S(1)}, bf16[512,32,64]{0,2,1:T(8,128)(2,1)}, u32[]{:S(2)}) copy-start(bf16[512,32,64]{0,2,1:T(8,128)(2,1)} %param.18) | copy-start | bytes 6291460
  27.6 4.5 %copy-start.23 = (bf16[512,512]{1,0:T(8,128)(2,1)S(1)}, bf16[512,512]{1,0:T(8,128)(2,1)}, u32[]{:S(2)}) copy-start(bf16[512,512]{1,0:T(8,128)(2,1)} %first_ref.2) | copy-start | bytes 1572868
  27.6 4.5 %copy-start.24 = (bf16[512,512]{1,0:T(8,128)(2,1)S(1)}, bf16[512,512]{1,0:T(8,128)(2,1)}, u32[]{:S(2)}) copy-start(bf16[512,512]{1,0:T(8,128)(2,1)} %second_ref.2) | copy-start | bytes 1572868
  27.6 4.5 %copy-start.25 = (bf16[512,512]{1,0:T(8,128)(2,1)S(1)}, bf16[512,512]{1,0:T(8,128)(2,1)}, u32[]{:S(2)}) copy-start(bf16[512,512]{1,0:T(8,128)(2,1)} %first_y.1) | copy-start | bytes 1572868
  27.6 4.5 %copy-start.26 = (bf16[512,512]{1,0:T(8,128)(2,1)S(1)}, bf16[512,512]{1,0:T(8,128)(2,1)}, u32[]{:S(2)}) copy-start(bf16[512,512]{1,0:T(8,128)(2,1)} %second_y.1) | copy-start | bytes 1572868
  32.0 2.0 %copy-start.4 = (f32[64,32,512]{2,1,0:T(8,128)}, f32[64,32,512]{2,1,0:T(8,128)S(1)}, u32[]{:S(2)}) copy-start(f32[64,32,512]{2,1,0:T(8,128)S(1)} %xterms.1.part_ref) | copy-start | bytes 12582916
  34.1 3.7 %copy-start.13 = (bf16[32,64,512]{2,1,0:T(8,128)(2,1)}, bf16[32,64,512]{2,1,0:T(8,128)(2,1)S(1)}, u32[]{:S(2)}) copy-start(bf16[32,64,512]{2,1,0:T(8,128)(2,1)S(1)} %get-tuple-element.63.drift_ref) | copy-start | bytes 6291460
  34.1 3.7 %copy-start.19 = (bf16[1024,512]{1,0:T(8,128)(2,1)}, bf16[1024,512]{1,0:T(8,128)(2,1)S(1)}, u32[]{:S(2)}) copy-start(bf16[1024,512]{1,0:T(8,128)(2,1)S(1)} %get-tuple-element.64.ops_ref) | copy-start | bytes 3145732
  34.1 6.0 %copy-start.31 = (f32[512]{0:T(512)S(1)}, f32[512]{0:T(512)}, u32[]{:S(2)}) copy-start(f32[512]{0:T(512)} %param.22) | copy-start | bytes 6148
  37.8 24.8 %collective-permute-start.5 = (bf16[3,32,32,128]{3,2,1,0:T(8,128)(2,1)}, bf16[3,32,32,128]{3,2,1,0:T(8,128)(2,1)}, u32[]{:S(2)}, u32[]{:S(2)}) collective-permute-start(bf16[3,32,32,128]{3,2,1,0:T(8,128)(2,1)} %get-tuple-element.68.refs_5_), channel_id=1, source_target_pairs={{0,2},{1,3},{2,0},{3,1},{4,6},{5,7},{6,4},{7,5},{8,10},{9,11},{10,... | collective-permute-start | bytes 2359304 | tf_op jit(solution)/shard_map/ppermute | solution.py:348
  37.8 24.8 %collective-permute-start.4 = (bf16[3,32,32,128]{3,2,1,0:T(8,128)(2,1)}, bf16[3,32,32,128]{3,2,1,0:T(8,128)(2,1)}, u32[]{:S(2)}, u32[]{:S(2)}) collective-permute-start(bf16[3,32,32,128]{3,2,1,0:T(8,128)(2,1)} %get-tuple-element.68.refs_5_), channel_id=1, source_target_pairs={{0,1},{1,0},{2,3},{3,2},{4,5},{5,4},{6,7},{7,6},{8,9},{9,8},{10,11... | collective-permute-start | bytes 2359304 | tf_op jit(solution)/shard_map/ppermute | solution.py:348
  48.2 1.6 %copy-start.14 = (bf16[32,64,512]{2,1,0:T(8,128)(2,1)S(1)}, bf16[32,64,512]{2,1,0:T(8,128)(2,1)}, u32[]{:S(2)}) copy-start(bf16[32,64,512]{2,1,0:T(8,128)(2,1)} %copy-done.13) | copy-start | bytes 6291460
  62.6 7.6 %collective-permute-start.8 = (bf16[3,32,32,128]{3,2,1,0:T(8,128)(2,1)}, bf16[3,32,32,128]{3,2,1,0:T(8,128)(2,1)S(1)}, u32[]{:S(2)}, u32[]{:S(2)}) collective-permute-start(bf16[3,32,32,128]{3,2,1,0:T(8,128)(2,1)} %collective-permute-done.5.refs_7_), channel_id=1, source_target_pairs={{0,1},{1,0},{2,3},{3,2},{4,5},{5,4},{6,7},{7,6},{8,9},{9,8},{10,11... | collective-permute-start | bytes 2359304 | tf_op jit(solution)/shard_map/ppermute | solution.py:348
  66.5 3.3 %collective-permute-start.6 = (bf16[64,32,128]{2,1,0:T(8,128)(2,1)S(1)}, bf16[64,32,128]{2,1,0:T(8,128)(2,1)S(1)}, u32[]{:S(2)}, u32[]{:S(2)}) collective-permute-start(bf16[64,32,128]{2,1,0:T(8,128)(2,1)S(1)} %get-tuple-element.49.after_ref.refs_1_), channel_id=1, source_target_pairs={{0,1},{1,0},{2,3},{3,2},{4,5},{5,4},{6,7},{7,6},{8,9},{9,8},{10,11... | collective-permute-start | bytes 1572872 | tf_op jit(solution)/shard_map/ppermute | solution.py:348
  66.6 3.5 %collective-permute-start.7 = (bf16[64,32,128]{2,1,0:T(8,128)(2,1)}, bf16[64,32,128]{2,1,0:T(8,128)(2,1)S(1)}, u32[]{:S(2)}, u32[]{:S(2)}) collective-permute-start(bf16[64,32,128]{2,1,0:T(8,128)(2,1)} %collective-permute-done.3.refs_3_), channel_id=1, source_target_pairs={{0,1},{1,0},{2,3},{3,2},{4,5},{5,4},{6,7},{7,6},{8,9},{9,8},{10,11... | collective-permute-start | bytes 1572872 | tf_op jit(solution)/shard_map/ppermute | solution.py:348
  67.0 19.4 %collective-permute-start.10 = (bf16[3,32,32,128]{3,2,1,0:T(8,128)(2,1)}, bf16[3,32,32,128]{3,2,1,0:T(8,128)(2,1)}, u32[]{:S(2)}, u32[]{:S(2)}) collective-permute-start(bf16[3,32,32,128]{3,2,1,0:T(8,128)(2,1)} %get-tuple-element.76.refs_5_), channel_id=1, source_target_pairs={{0,2},{1,3},{2,0},{3,1},{4,6},{5,7},{6,4},{7,5},{8,10},{9,11},{10,... | collective-permute-start | bytes 2359304 | tf_op jit(solution)/shard_map/ppermute | solution.py:348
  70.1 3.5 %copy-start.27 = (bf16[64,32,128]{2,1,0:T(8,128)(2,1)}, bf16[64,32,128]{2,1,0:T(8,128)(2,1)S(1)}, u32[]{:S(2)}) copy-start(bf16[64,32,128]{2,1,0:T(8,128)(2,1)S(1)} %collective-permute-done.7.refs_4_) | copy-start | bytes 1572868
  73.6 2.7 %copy-start.15 = (f32[2,1040,128]{2,1,0:T(8,128)}, f32[2,1040,128]{2,1,0:T(8,128)S(1)}, u32[]{:S(2)}) copy-start(f32[2,1040,128]{2,1,0:T(8,128)S(1)} %get-tuple-element.82.refs_0_) | copy-start | bytes 3194884
  76.4 56.1 %all-to-all-start.1 = ((f16[8,2064,128]{2,1,0:T(8,128)(2,1)}), f16[8,2064,128]{2,1,0:T(8,128)(2,1)}, u32[]{:S(2)}, u32[]{:S(2)}) async-start(f16[8,2064,128]{2,1,0:T(8,128)(2,1)} %convert_element_type.42), calls=%async_computation.1 | async-start | bytes 8454144 | tf_op jit(solution)/shard_map/all_to_all | solution.py:402
  81.7 9.2 %collective-permute-start.9 = (bf16[3,32,32,128]{3,2,1,0:T(8,128)(2,1)}, bf16[3,32,32,128]{3,2,1,0:T(8,128)(2,1)S(1)}, u32[]{:S(2)}, u32[]{:S(2)}) collective-permute-start(bf16[3,32,32,128]{3,2,1,0:T(8,128)(2,1)} %get-tuple-element.76.refs_5_), channel_id=1, source_target_pairs={{0,1},{1,0},{2,3},{3,2},{4,5},{5,4},{6,7},{7,6},{8,9},{9,8},{10,11... | collective-permute-start | bytes 2359304 | tf_op jit(solution)/shard_map/ppermute | solution.py:348
  86.4 4.5 %collective-permute-start.11 = (bf16[3,32,32,128]{3,2,1,0:T(8,128)(2,1)}, bf16[3,32,32,128]{3,2,1,0:T(8,128)(2,1)S(1)}, u32[]{:S(2)}, u32[]{:S(2)}) collective-permute-start(bf16[3,32,32,128]{3,2,1,0:T(8,128)(2,1)} %collective-permute-done.10.refs_7_), channel_id=1, source_target_pairs={{0,1},{1,0},{2,3},{3,2},{4,5},{5,4},{6,7},{7,6},{8,9},{9,8},{10,11... | collective-permute-start | bytes 2359304 | tf_op jit(solution)/shard_map/ppermute | solution.py:348
  87.8 26.7 %collective-permute-start.15 = (f16[2,1040,128]{2,1,0:T(8,128)(2,1)}, f16[2,1040,128]{2,1,0:T(8,128)(2,1)S(1)}, u32[]{:S(2)}, u32[]{:S(2)}) collective-permute-start(f16[2,1040,128]{2,1,0:T(8,128)(2,1)} %convert_element_type.43), channel_id=1, source_target_pairs={{0,4},{1,5},{2,6},{3,7},{4,8},{5,9},{6,10},{7,11},{8,12},{9,13},{1... | collective-permute-start | bytes 1597448 | tf_op jit(solution)/shard_map/ppermute | solution.py:344
  88.5 28.6 %collective-permute-start.16 = (f16[2,1040,128]{2,1,0:T(8,128)(2,1)}, f16[2,1040,128]{2,1,0:T(8,128)(2,1)}, u32[]{:S(2)}, u32[]{:S(2)}) collective-permute-start(f16[2,1040,128]{2,1,0:T(8,128)(2,1)} %convert_element_type.44), channel_id=1, source_target_pairs={{0,8},{1,9},{2,10},{3,11},{4,12},{5,13},{6,14},{7,15},{8,0},{9,1},... | collective-permute-start | bytes 1597448 | tf_op jit(solution)/shard_map/ppermute | solution.py:344
  88.9 30.3 %collective-permute-start.17 = (f16[2,1040,128]{2,1,0:T(8,128)(2,1)}, f16[2,1040,128]{2,1,0:T(8,128)(2,1)}, u32[]{:S(2)}, u32[]{:S(2)}) collective-permute-start(f16[2,1040,128]{2,1,0:T(8,128)(2,1)} %convert_element_type.45), channel_id=1, source_target_pairs={{0,12},{1,13},{2,14},{3,15},{4,0},{5,1},{6,2},{7,3},{8,4},{9,5},{1... | collective-permute-start | bytes 1597448 | tf_op jit(solution)/shard_map/ppermute | solution.py:344
  95.1 4.8 %copy-start.17 = (f32[2,1040,128]{2,1,0:T(8,128)}, f32[2,1040,128]{2,1,0:T(8,128)S(1)}, u32[]{:S(2)}) copy-start(f32[2,1040,128]{2,1,0:T(8,128)S(1)} %get-tuple-element.86.refs_4_) | copy-start | bytes 3194884
  96.1 43.1 %collective-permute-start.12 = (f16[2,1040,128]{2,1,0:T(8,128)(2,1)}, f16[2,1040,128]{2,1,0:T(8,128)(2,1)}, u32[]{:S(2)}, u32[]{:S(2)}) collective-permute-start(f16[2,1040,128]{2,1,0:T(8,128)(2,1)} %convert_element_type.47), channel_id=1, source_target_pairs={{0,4},{1,5},{2,6},{3,7},{4,8},{5,9},{6,10},{7,11},{8,12},{9,13},{1... | collective-permute-start | bytes 1597448 | tf_op jit(solution)/shard_map/ppermute | solution.py:344
  97.1 42.1 %collective-permute-start.13 = (f16[2,1040,128]{2,1,0:T(8,128)(2,1)}, f16[2,1040,128]{2,1,0:T(8,128)(2,1)}, u32[]{:S(2)}, u32[]{:S(2)}) collective-permute-start(f16[2,1040,128]{2,1,0:T(8,128)(2,1)} %convert_element_type.48), channel_id=1, source_target_pairs={{0,8},{1,9},{2,10},{3,11},{4,12},{5,13},{6,14},{7,15},{8,0},{9,1},... | collective-permute-start | bytes 1597448 | tf_op jit(solution)/shard_map/ppermute | solution.py:344
  115.2 24.0 %collective-permute-start.14 = (f16[2,1040,128]{2,1,0:T(8,128)(2,1)}, f16[2,1040,128]{2,1,0:T(8,128)(2,1)}, u32[]{:S(2)}, u32[]{:S(2)}) collective-permute-start(f16[2,1040,128]{2,1,0:T(8,128)(2,1)} %convert_element_type.49), channel_id=1, source_target_pairs={{0,12},{1,13},{2,14},{3,15},{4,0},{5,1},{6,2},{7,3},{8,4},{9,5},{1... | collective-permute-start | bytes 1597448 | tf_op jit(solution)/shard_map/ppermute | solution.py:344
  132.5 2.9 %copy-start.3 = (bf16[64,32,512]{2,1,0:T(8,128)(2,1)S(1)}, bf16[64,32,512]{2,1,0:T(8,128)(2,1)}, u32[]{:S(2)}) copy-start(bf16[64,32,512]{2,1,0:T(8,128)(2,1)} %diff_ref.5) | copy-start | bytes 6291460
  132.5 4.1 %copy-start.5 = (f32[64,32,512]{2,1,0:T(8,128)S(1)}, f32[64,32,512]{2,1,0:T(8,128)}, u32[]{:S(2)}) copy-start(f32[64,32,512]{2,1,0:T(8,128)} %copy-done.4) | copy-start | bytes 12582916
  136.6 6.4 %copy-start.16 = (f32[2,1040,128]{2,1,0:T(8,128)S(1)}, f32[2,1040,128]{2,1,0:T(8,128)}, u32[]{:S(2)}) copy-start(f32[2,1040,128]{2,1,0:T(8,128)} %copy-done.15) | copy-start | bytes 3194884
  136.6 6.4 %copy-start.18 = (f32[2,1040,128]{2,1,0:T(8,128)S(1)}, f32[2,1040,128]{2,1,0:T(8,128)}, u32[]{:S(2)}) copy-start(f32[2,1040,128]{2,1,0:T(8,128)} %copy-done.17) | copy-start | bytes 3194884
  139.2 3.7 %copy-start.7 = (f32[2,1040,128]{2,1,0:T(8,128)S(1)}, f32[2,1040,128]{2,1,0:T(8,128)}, u32[]{:S(2)}) copy-start(f32[2,1040,128]{2,1,0:T(8,128)} %convert_element_type.51.refs_2_) | copy-start | bytes 3194884
  139.2 3.7 %copy-start.8 = (f32[2,1040,128]{2,1,0:T(8,128)S(1)}, f32[2,1040,128]{2,1,0:T(8,128)}, u32[]{:S(2)}) copy-start(f32[2,1040,128]{2,1,0:T(8,128)} %convert_element_type.52.refs_3_) | copy-start | bytes 3194884
  139.3 3.7 %copy-start.11 = (bf16[64,32,512]{2,1,0:T(8,128)(2,1)S(1)}, bf16[64,32,512]{2,1,0:T(8,128)(2,1)}, u32[]{:S(2)}) copy-start(bf16[64,32,512]{2,1,0:T(8,128)(2,1)} %drift_ref.3) | copy-start | bytes 6291460
  (4 other events, 4.1 us)
